TPU v7x, 32 devices: a whole 2x2x4 slice. The times are simulated.
32 devices in a mesh: dp: 16 (over z, y, x), head: 2 (over core).
Axes of the slice: x: 2, y: 2, z: 4, core: 2. Of those that a mesh axis runs over, the one named last changes fastest.
Arguments:
- tokens: bfloat16 [16384, 768], P(('dp', 'head')), may hold values from -6 to 6
- seq_len: int32 [32], P('dp'), may hold values from 128 to 512, as said below
- w_query: float32 [2, 768, 768], P(None, 'dp', 'head'), may hold values from -0.21875 to 0.21875
- w_key: float32 [2, 768, 768], P(None, 'dp', 'head'), may hold values from -0.21875 to 0.21875
- w_value: float32 [2, 768, 768], P(None, 'dp', 'head'), may hold values from -0.21875 to 0.21875
- w_out: float32 [2, 768, 768], P(None, ('dp', 'head')), may hold values from -0.875 to 0.875
- w_up: float32 [2, 768, 3072], P(None, ('dp', 'head')), may hold values from -0.21875 to 0.21875
- w_down: float32 [2, 3072, 768], P(None, ('dp', 'head')), may hold values from -0.109375 to 0.109375
- a_query: float32 [2, 768, 8], replicated, may hold values from -0.21875 to 0.21875
- b_query: float32 [2, 8, 768], P(None, None, 'head'), may hold values from -0.9 to 0.9
- a_value: float32 [2, 768, 8], replicated, may hold values from -0.21875 to 0.21875
- b_value: float32 [2, 8, 768], P(None, None, 'head'), may hold values from -0.9 to 0.9
- ln_gain: float32 [2, 2, 768], replicated, may hold values from 0.1 to 1.9
- ln_bias: float32 [2, 2, 768], replicated, may hold values from -1.5 to 1.5
- cotangent: bfloat16 [16384, 768], P(('dp', 'head')), may hold values from -6 to 6
Outputs:
- output: bfloat16 [16384, 768], P(('dp', 'head'))
- input_grad: float32 [16384, 768], P(('dp', 'head'))
- grad_a_query: float32 [2, 768, 8], replicated
- grad_b_query: float32 [2, 8, 768], P(None, None, 'head')
- grad_a_value: float32 [2, 768, 8], replicated
- grad_b_value: float32 [2, 8, 768], P(None, None, 'head')
Inputs may be any that keep to these rules, and one draw needn't show every extreme that they name: Each block of 512 tokens holds whole sequences of length seq_len[block], which is a quarter of 512, half of it or all of it; the numbers of blocks of the three lengths differ by at most one.
All inputs are finite; a program needn't handle non-finite values.
Results may differ from a plain program's by a relative error of at most 0.028.
Values may be sent and summed in bfloat16 or wider, within the bound.
No kernel may reach another device: no remote copies, remote signals or barrier semaphores. Data moves between devices by JAX's collectives and lax.ppermute only.
A program may use at most 192 MiB of HBM per device.

v0:
```python
import jax
import jax.numpy as jnp
from jax import lax
from jax.sharding import PartitionSpec as P

HEAD_DIM = 64


epsilon = 1e-05
highest = lax.Precision.HIGHEST


def exact_dot(left, right):
    return jnp.dot(left, right, precision=highest, preferred_element_type=jnp.float32)


def dot_right_t(left, right):
    return lax.dot_general(
        left, right, (((1,), (1,)), ((), ())), preferred_element_type=jnp.float32
    )


def exact_right_t(left, right):
    return lax.dot_general(
        left, right, (((1,), (1,)), ((), ())), precision=highest, preferred_element_type=jnp.float32
    )


def exact_left_t(left, right):
    return lax.dot_general(
        left, right, (((0,), (0,)), ((), ())), precision=highest, preferred_element_type=jnp.float32
    )


def layer_norm(values, gain_row, offset_row):
    center = values - jnp.mean(values, -1, keepdims=True)
    spread = jnp.mean(center * center, -1, keepdims=True)
    return center * lax.rsqrt(spread + epsilon) * gain_row + offset_row


def gelu_exact(values):
    return jax.nn.gelu(values, approximate=False)


def gather_head(w_query, w_key, w_value, layer_at):
    pieces = (
        w_query[layer_at].astype(jnp.bfloat16),
        w_key[layer_at].astype(jnp.bfloat16),
        w_value[layer_at].astype(jnp.bfloat16),
    )
    gathered = (
        lax.all_gather(pieces[0], "dp", axis=0, tiled=True),
        lax.all_gather(pieces[1], "dp", axis=0, tiled=True),
        lax.all_gather(pieces[2], "dp", axis=0, tiled=True),
    )
    return gathered


def gather_dense(w_out, w_up, w_down, layer_at):
    pieces = (
        w_out[layer_at].astype(jnp.bfloat16),
        w_up[layer_at].astype(jnp.bfloat16),
        w_down[layer_at].astype(jnp.bfloat16),
    )
    return (
        lax.all_gather(pieces[0], ("dp", "head"), axis=0, tiled=True),
        lax.all_gather(pieces[1], ("dp", "head"), axis=0, tiled=True),
        lax.all_gather(pieces[2], ("dp", "head"), axis=0, tiled=True),
    )


def block_scores(queries, key_rows, length):
    row_count = queries.shape[0]
    scaling = queries.shape[-1] ** (-0.5)
    scores = (
        jnp.einsum("qhd,khd->hqk", queries, key_rows, preferred_element_type=jnp.float32) * scaling
    )
    segment = lax.iota(jnp.int32, row_count) // length
    allowed = segment[:, None] == segment[None, :]
    return (jnp.where(allowed[None], scores, -1e30), scaling)


def attend_forward(pieces):
    queries, key_rows, value_rows, length = pieces
    scores, scaling = block_scores(queries, key_rows, length)
    largest = jnp.max(scores, -1, keepdims=True)
    raised = jnp.exp(scores - largest)
    totals = jnp.sum(raised, -1, keepdims=True)
    weights_now = (raised / totals).astype(jnp.bfloat16)
    mixed_rows = jnp.einsum(
        "hqk,khd->qhd", weights_now, value_rows, preferred_element_type=jnp.float32
    )
    return (mixed_rows.astype(jnp.bfloat16), (largest + jnp.log(totals))[..., 0])


def attend_backward(pieces):
    queries, key_rows, value_rows, upstream, log_total, length = pieces
    scores, scaling = block_scores(queries, key_rows, length)
    weights_now = jnp.exp(scores - log_total[..., None])
    grad_weights = jnp.einsum(
        "qhd,khd->hqk", upstream, value_rows, preferred_element_type=jnp.float32
    )
    row_dot = jnp.sum(weights_now * grad_weights, -1, keepdims=True)
    grad_scores = (weights_now * (grad_weights - row_dot)).astype(jnp.bfloat16)
    grad_queries = (
        jnp.einsum("hqk,khd->qhd", grad_scores, key_rows, preferred_element_type=jnp.float32)
        * scaling
    )
    grad_keys = (
        jnp.einsum("hqk,qhd->khd", grad_scores, queries, preferred_element_type=jnp.float32)
        * scaling
    )
    grad_values = jnp.einsum(
        "hqk,qhd->khd",
        weights_now.astype(jnp.bfloat16),
        upstream,
        preferred_element_type=jnp.float32,
    )
    return (
        grad_queries.astype(jnp.bfloat16),
        grad_keys.astype(jnp.bfloat16),
        grad_values.astype(jnp.bfloat16),
    )


def split_blocks(matrix, blocks):
    return matrix.reshape(blocks, matrix.shape[0] // blocks, matrix.shape[1] // HEAD_DIM, HEAD_DIM)


def layer_forward(stream, head_mats, dense_mats, adapters, norm_pair, lengths):
    query_w, key_w, value_w = head_mats
    out_w, up_w, down_w = dense_mats
    a_query, b_query, a_value, b_value = adapters
    gain_rows, offset_rows = norm_pair
    full_rows = lax.all_gather(stream.astype(jnp.bfloat16), "head", axis=0, tiled=True)
    exact_rows = full_rows.astype(jnp.float32)
    mid_query = exact_dot(exact_rows, a_query).astype(jnp.bfloat16).astype(jnp.float32)
    mid_value = exact_dot(exact_rows, a_value).astype(jnp.bfloat16).astype(jnp.float32)
    queries = (
        jnp.dot(full_rows, query_w, preferred_element_type=jnp.float32)
        + 2.0 * exact_dot(mid_query, b_query)
    ).astype(jnp.bfloat16)
    key_rows = jnp.dot(full_rows, key_w, preferred_element_type=jnp.float32).astype(jnp.bfloat16)
    value_rows = (
        jnp.dot(full_rows, value_w, preferred_element_type=jnp.float32)
        + 2.0 * exact_dot(mid_value, b_value)
    ).astype(jnp.bfloat16)
    blocks = lengths.shape[0]
    attended, log_total = lax.map(
        attend_forward,
        (
            split_blocks(queries, blocks),
            split_blocks(key_rows, blocks),
            split_blocks(value_rows, blocks),
            lengths,
        ),
    )
    attended = attended.reshape(queries.shape)
    merged = lax.all_to_all(attended, "head", split_axis=0, concat_axis=1, tiled=True)
    hidden = stream.astype(jnp.float32) + jnp.dot(merged, out_w, preferred_element_type=jnp.float32)
    normed = layer_norm(hidden, gain_rows[0], offset_rows[0])
    pre_act = jnp.dot(normed.astype(jnp.bfloat16), up_w, preferred_element_type=jnp.float32)
    activated = gelu_exact(pre_act).astype(jnp.bfloat16)
    second = normed + jnp.dot(activated, down_w, preferred_element_type=jnp.float32)
    result = layer_norm(second, gain_rows[1], offset_rows[1])
    saved_state = (
        full_rows,
        mid_query,
        mid_value,
        queries,
        key_rows,
        value_rows,
        log_total,
        hidden,
        normed,
        second,
    )
    saved_state = saved_state + ()
    return (result, saved_state)


def layer_backward(grad_out, saved_state, head_mats, dense_mats, adapters, norm_pair, lengths):
    (
        full_rows,
        mid_query,
        mid_value,
        queries,
        key_rows,
        value_rows,
        log_total,
        hidden,
        normed,
        second,
    ) = saved_state[:10]
    query_w, key_w, value_w = head_mats
    out_w, up_w, down_w = dense_mats
    a_query, b_query, a_value, b_value = adapters
    gain_rows, offset_rows = norm_pair
    unused, pull_second = jax.vjp(
        lambda values: layer_norm(values, gain_rows[1], offset_rows[1]), second
    )
    (grad_second,) = pull_second(grad_out)
    grad_act = dot_right_t(grad_second.astype(jnp.bfloat16), down_w)
    pre_act = jnp.dot(normed.astype(jnp.bfloat16), up_w, preferred_element_type=jnp.float32)
    unused, pull_act = jax.vjp(gelu_exact, pre_act)
    (grad_pre,) = pull_act(grad_act)
    grad_normed = grad_second + dot_right_t(grad_pre.astype(jnp.bfloat16), up_w)
    unused, pull_first = jax.vjp(
        lambda values: layer_norm(values, gain_rows[0], offset_rows[0]), hidden
    )
    (grad_hidden,) = pull_first(grad_normed)
    grad_merged = dot_right_t(grad_hidden.astype(jnp.bfloat16), out_w).astype(jnp.bfloat16)
    grad_attended = lax.all_to_all(grad_merged, "head", split_axis=1, concat_axis=0, tiled=True)
    blocks = lengths.shape[0]
    grad_q, grad_k, grad_v = lax.map(
        attend_backward,
        (
            split_blocks(queries, blocks),
            split_blocks(key_rows, blocks),
            split_blocks(value_rows, blocks),
            split_blocks(grad_attended, blocks),
            log_total,
            lengths,
        ),
    )
    grad_q = grad_q.reshape(queries.shape)
    grad_k = grad_k.reshape(queries.shape)
    grad_v = grad_v.reshape(queries.shape)
    grad_mid_query = 2.0 * exact_right_t(grad_q.astype(jnp.float32), b_query)
    grad_mid_value = 2.0 * exact_right_t(grad_v.astype(jnp.float32), b_value)
    partial_sum = (
        dot_right_t(grad_q, query_w) + dot_right_t(grad_k, key_w) + dot_right_t(grad_v, value_w)
    )
    partial_sum = (
        partial_sum
        + exact_right_t(grad_mid_query, a_query)
        + exact_right_t(grad_mid_value, a_value)
    )
    grad_rows = lax.psum_scatter(
        partial_sum.astype(jnp.bfloat16), "head", scatter_dimension=0, tiled=True
    ).astype(jnp.float32)
    exact_rows = full_rows.astype(jnp.float32)
    adapter_terms = (
        exact_left_t(exact_rows, grad_mid_query),
        2.0 * exact_left_t(mid_query, grad_q.astype(jnp.float32)),
        exact_left_t(exact_rows, grad_mid_value),
        2.0 * exact_left_t(mid_value, grad_v.astype(jnp.float32)),
    )
    return (grad_hidden + grad_rows, adapter_terms)


def widen(term):
    width = term.shape[-1]
    placed = jnp.zeros(term.shape[:-1] + (width * lax.axis_size("head"),), jnp.float32)
    return lax.dynamic_update_slice_in_dim(
        placed, term, lax.axis_index("head") * width, term.ndim - 1
    )


def narrow(total):
    width = total.shape[-1] // lax.axis_size("head")
    return lax.dynamic_slice_in_dim(total, lax.axis_index("head") * width, width, total.ndim - 1)


def body(
    tokens,
    seq_len,
    w_query,
    w_key,
    w_value,
    w_out,
    w_up,
    w_down,
    a_query,
    b_query,
    a_value,
    b_value,
    ln_gain,
    ln_bias,
    cotangent,
):
    layer_count = w_query.shape[0]
    b_query_all, b_value_all = (b_query, b_value)
    stream = tokens
    head_list = []
    dense_list = []
    saved_list = []
    for layer_at in range(layer_count):
        head_mats = gather_head(w_query, w_key, w_value, layer_at)
        dense_mats = gather_dense(w_out, w_up, w_down, layer_at)
        adapters = (
            a_query[layer_at],
            b_query_all[layer_at],
            a_value[layer_at],
            b_value_all[layer_at],
        )
        stream, saved_state = layer_forward(
            stream, head_mats, dense_mats, adapters, (ln_gain[layer_at], ln_bias[layer_at]), seq_len
        )
        head_list.append(head_mats)
        dense_list.append(dense_mats)
        saved_list.append(saved_state)
    output = stream.astype(jnp.bfloat16)
    grad_stream = cotangent.astype(jnp.float32)
    collected = [None] * layer_count
    for layer_at in reversed(range(layer_count)):
        adapters = (
            a_query[layer_at],
            b_query_all[layer_at],
            a_value[layer_at],
            b_value_all[layer_at],
        )
        grad_stream, adapter_terms = layer_backward(
            grad_stream,
            saved_list[layer_at],
            head_list[layer_at],
            dense_list[layer_at],
            adapters,
            (ln_gain[layer_at], ln_bias[layer_at]),
            seq_len,
        )
        wide_terms = (
            adapter_terms[0],
            widen(adapter_terms[1]),
            adapter_terms[2],
            widen(adapter_terms[3]),
        )
        summed = lax.psum(
            (wide_terms[0], wide_terms[1], wide_terms[2], wide_terms[3]), ("dp", "head")
        )
        collected[layer_at] = (summed[0], narrow(summed[1]), summed[2], narrow(summed[3]))
    stacked = [jnp.stack([record[member] for record in collected]) for member in range(4)]
    return (output, grad_stream, stacked[0], stacked[1], stacked[2], stacked[3])


def solution(mesh):
    placed = (
        P(("dp", "head"), None),
        P("dp"),
        P(None, "dp", "head"),
        P(None, "dp", "head"),
        P(None, "dp", "head"),
        P(None, ("dp", "head"), None),
        P(None, ("dp", "head"), None),
        P(None, ("dp", "head"), None),
        P(),
        P(None, None, "head"),
        P(),
        P(None, None, "head"),
        P(),
        P(),
        P(("dp", "head"), None),
    )
    return jax.shard_map(
        body,
        mesh=mesh,
        in_specs=placed,
        out_specs=(
            P(("dp", "head"), None),
            P(("dp", "head"), None),
            P(),
            P(None, None, "head"),
            P(),
            P(None, None, "head"),
        ),
        check_vma=False,
    )
```

profile of v0, /device:TPU:0, one launch (start us, length us, event | category | flops | bytes accessed | tf_op | source)
XLA Modules:
  0.0 761.6 jit_solution(3034509669714473869)
XLA Ops:
  14.4 46.7 %all-gather = bf16[1,768,384]{2,1,0:T(8,128)(2,1)S(1)} all-gather(bf16[1,48,384]{2,1,0:T(8,128)(2,1)S(1)} %get-tuple-element.700), channel_id=2, replica_groups=mesh['dp'=16,'head'=2] {'dp'}, dimensions={1}, use_global_device_ids=true | all-gather | bytes 626688 | tf_op jit(solution)/shard_map/all_gather | solution.py:54
  61.1 42.6 %all-gather.1 = bf16[1,768,384]{2,1,0:T(8,128)(2,1)} all-gather(bf16[1,48,384]{2,1,0:T(8,128)(2,1)S(1)} %get-tuple-element.698), channel_id=3, replica_groups=mesh['dp'=16,'head'=2] {'dp'}, dimensions={1}, use_global_device_ids=true | all-gather | bytes 626688 | tf_op jit(solution)/shard_map/all_gather | solution.py:52
  103.8 45.1 %all-gather.2 = bf16[1,768,384]{2,1,0:T(8,128)(2,1)} all-gather(bf16[1,48,384]{2,1,0:T(8,128)(2,1)S(1)} %get-tuple-element.696), channel_id=4, replica_groups=mesh['dp'=16,'head'=2] {'dp'}, dimensions={1}, use_global_device_ids=true | all-gather | bytes 626688 | tf_op jit(solution)/shard_map/all_gather | solution.py:53
  150.1 2.6 fusion.207
  167.1 2.9 convolution_convert_fusion.3
  173.1 15.2 %while.60 = (s32[]{:T(128)}, bf16[2,512,6,64]{1,3,2,0:T(8,128)(2,1)}, f32[2,6,512]{2,1,0:T(8,128)S(1)}, bf16[2,512,6,64]{1,3,2,0:T(8,128)(2,1)S(1)}, s32[2]{0:T(...) while((s32[]{:T(128)}, ...), condition=%wide.region_3.4_spmd, body=%wide.region_0.3_spmd.sunk | while | flops 421987328 | bytes 21620852 | solution.py:149
  178.0 2.7 fusion.354
  185.6 2.7 fusion.354
  188.3 6.6 all_to_all.70
  194.9 2.6 fusion.265
  197.9 19.1 %fusion.122 = (f32[512,3072]{1,0:T(8,128)}, f32[512,3072]{1,0:T(8,128)}) fusion(bf16[1,768,3072]{2,1,0:T(8,128)(2,1)} %all-gather.27.cloned.1.call-done, f32[512,768]{1,0:T(8,128)S(1)} %get-tuple-element.704, f32[768]{0:T(1024)S(1)} %get-tuple-element.594, f32[768]{0:T(1024)S(1)} %get-tuple-element.590, f32[512]{0:T(512)S(1)} %fusion.243, ...), kind=kOutput, calls=%fused_computation.146 | convolution fusion | flops 2515402752 | bytes 18884608 | tf_op jit(solution)/shard_map/dot_general | solution.py:162
  217.9 7.6 fusion.266
  229.1 42.6 %all-gather.7 = bf16[1,768,384]{2,1,0:T(8,128)(2,1)S(1)} all-gather(bf16[1,48,384]{2,1,0:T(8,128)(2,1)S(1)} %get-tuple-element.697), channel_id=9, replica_groups=mesh['dp'=16,'head'=2] {'dp'}, dimensions={1}, use_global_device_ids=true | all-gather | bytes 626688 | tf_op jit(solution)/shard_map/all_gather | solution.py:52
  271.8 42.7 %all-gather.6 = bf16[1,768,384]{2,1,0:T(8,128)(2,1)} all-gather(bf16[1,48,384]{2,1,0:T(8,128)(2,1)S(1)} %get-tuple-element.699), channel_id=8, replica_groups=mesh['dp'=16,'head'=2] {'dp'}, dimensions={1}, use_global_device_ids=true | all-gather | bytes 626688 | tf_op jit(solution)/shard_map/all_gather | solution.py:54
  314.4 45.0 %all-gather.8 = bf16[1,768,384]{2,1,0:T(8,128)(2,1)} all-gather(bf16[1,48,384]{2,1,0:T(8,128)(2,1)S(1)} %get-tuple-element.695), channel_id=10, replica_groups=mesh['dp'=16,'head'=2] {'dp'}, dimensions={1}, use_global_device_ids=true | all-gather | bytes 626688 | tf_op jit(solution)/shard_map/all_gather | solution.py:53
  359.5 2.7 convolution_convert_fusion.4
  366.5 2.7 convolution_convert_fusion.5
  369.2 2.5 fusion.196
  378.5 3.4 convolution_convert_fusion.2
  386.9 15.3 %while.61 = (s32[]{:T(128)}, bf16[2,512,6,64]{1,3,2,0:T(8,128)(2,1)}, f32[2,6,512]{2,1,0:T(8,128)S(1)}, bf16[2,512,6,64]{1,3,2,0:T(8,128)(2,1)}, s32[2]{0:T(128)...) while((s32[]{:T(128)}, ...), condition=%wide.region_11.12_spmd, body=%wide.region_8.11_spmd.sunk | while | flops 421987328 | bytes 24766608 | solution.py:149
  391.8 2.7 fusion.358
  399.5 2.7 fusion.358
  402.2 4.4 all-to-all-start.1
  408.7 4.0 fusion.267
  414.5 20.0 %fusion.123 = (f32[512,3072]{1,0:T(8,128)}, f32[512,3072]{1,0:T(8,128)}) fusion(bf16[1,768,3072]{2,1,0:T(8,128)(2,1)} %all-gather.33.cloned.1.call-done, f32[512,768]{1,0:T(8,128)} %get-tuple-element.710, f32[768]{0:T(1024)S(1)} %copy-done.68, f32[768]{0:T(1024)S(1)} %copy-done.66, f32[512]{0:T(512)S(1)} %fusion.245, f32[512]{0:T(512)S(1)} %broadcast_multiply_fusion.1), kind=kOutput, calls=%fused_computation.147 | convolution fusion | flops 2515402752 | bytes 18884608 | tf_op jit(solution)/shard_map/dot_general | solution.py:162
  434.5 9.3 %fusion.268 = (f32[512]{0:T(512)S(1)}, f32[512,768]{1,0:T(8,128)S(1)}) fusion(bf16[1,3072,768]{2,1,0:T(8,128)(2,1)} %all-gather.35.cloned.1.call-done, f32[512,3072]{1,0:T(8,128)} %get-tuple-element.711, f32[512,3072]{1,0:T(8,128)} %get-tuple-element.712, f32[768]{0:T(1024)S(1)} %copy-done.68, f32[768]{0:T(1024)S(1)} %copy-done.66, f32[512]{0:T(512)S(1)} %fusion.245, ...), kind=kOutput, calls=%fused_computation.389 | convolution fusion | flops 2422996480 | bytes 20459520 | tf_op jit(solution)/shard_map/dot_general | solution.py:164
  447.3 4.8 fusion.134
  452.1 10.8 %multiply_reduce_fusion.4 = (f32[512]{0:T(512)S(1)}, f32[512,768]{1,0:T(8,128)}) fusion(f32[512,768]{1,0:T(8,128)} %get-tuple-element.710, f32[512]{0:T(512)S(1)} %broadcast_multiply_fusion.1, f32[768]{0:T(1024)S(1)} %copy-done.66, bf16[1,768,3072]{2,1,0:T(8,128)(2,1)} %all-gather.33.cloned.1.call-done, f32[512,3072]{1,0:T(8,128)} %fusion.134, ...), kind=kOutput, calls=%fused_computation.207 | convolution fusion | flops 2440297984 | bytes 28320768 | tf_op jit(solution)/shard_map/dot_general | solution.py:18
  463.0 3.6 fusion.257
  468.9 4.6 all_to_all.71
  477.6 27.2 %while.62 = (s32[]{:T(128)}, bf16[2,512,6,64]{1,3,2,0:T(8,128)(2,1)}, bf16[2,512,6,64]{1,3,2,0:T(8,128)(2,1)}, bf16[2,512,6,64]{1,3,2,0:T(8,128)(2,1)}, bf16[2,5...) while((s32[]{:T(128)}, ...), condition=%wide.region_22.23_spmd, body=%wide.region_20.22_spmd.sunk | while | flops 1031472128 | bytes 61707488 | solution.py:215
  488.4 2.6 fusion.370
  516.0 2.7 fusion.209
  518.7 4.1 add_convert_fusion.3
  531.1 2.6 fusion.256
  533.8 7.1 fusion.142
  540.9 9.1 %multiply_reduce_fusion.2 = (f32[512]{0:T(512)S(1)}, f32[512,768]{1,0:T(8,128)S(1)}) fusion(f32[512,768]{1,0:T(8,128)S(1)} %copy-done.10, f32[512]{0:T(512)S(1)} %copy-done.49, f32[768]{0:T(1024)S(1)} %copy-done.65, bf16[1,768,3072]{2,1,0:T(8,128)(2,1)} %all-gather.27.cloned.1.call-done, f32[512,3072]{1,0:T(8,128)} %fusion.142, ...), kind=kOutput, calls=%fused_computation.203 | convolution fusion | flops 2440297984 | bytes 28320768 | tf_op jit(solution)/shard_map/dot_general | solution.py:18
  552.7 4.6 all_to_all.72
  561.4 27.0 %while.63 = (s32[]{:T(128)}, bf16[2,512,6,64]{1,3,2,0:T(8,128)(2,1)}, bf16[2,512,6,64]{1,3,2,0:T(8,128)(2,1)}, bf16[2,512,6,64]{1,3,2,0:T(8,128)(2,1)}, bf16[2,5...) while((s32[]{:T(128)}, ...), condition=%wide.region_30.31_spmd, body=%wide.region_28.30_spmd.sunk | while | flops 1031472128 | bytes 61707488 | solution.py:215
  572.2 2.5 fusion.382
  585.6 2.5 fusion.382
  595.6 2.6 fusion.205
  599.9 2.7 fusion.198
  602.6 4.3 fusion.214
  609.7 6.4 add_convert_fusion.2
  616.1 120.6 %all-reduce.3.cloned.1.call-done = (f32[1,768,8]{1,2,0:T(8,128)}, f32[1,768,8]{1,2,0:T(8,128)}, f32[8,768]{1,0:T(8,128)}, f32[8,768]{1,0:T(8,128)}, f32[1,768,8]...) async-done(((f32[1,768,8]{1,2,0:T(8,128)}, f32[1,768,8]{1,2,0:T(8,128)}, f32[8,768]{1,0:T(8,128)}, f32[8,768]{1,0:T(8,128)}, ...) | async-done | bytes 196624 | tf_op jit(solution)/shard_map/psum | solution.py:328
  740.8 10.8 %reduce-scatter.5.cloned.1.call-done = bf16[512,768]{1,0:T(8,128)(2,1)} async-done(((bf16[1024,768]{1,0:T(8,128)(2,1)}), bf16[512,768]{1,0:T(8,128)(2,1)}) %reduce-scatter.5.cloned.1.call-update) | async-done | bytes 786448 | tf_op jit(solution)/shard_map/reduce_scatter | solution.py:239
  751.6 3.0 convert_add_fusion
  (405 shorter events, 161.3 us)
Async XLA Ops:
  7.2 53.9 %copy-start.46 = (f32[2,48,384]{2,1,0:T(8,128)S(1)}, f32[2,48,384]{2,1,0:T(8,128)}, u32[]{:S(2)}) copy-start(f32[2,48,384]{2,1,0:T(8,128)} %param.25) | copy-start | bytes 442372
  7.2 96.6 %copy-start.47 = (f32[2,48,384]{2,1,0:T(8,128)S(1)}, f32[2,48,384]{2,1,0:T(8,128)}, u32[]{:S(2)}) copy-start(f32[2,48,384]{2,1,0:T(8,128)} %param.26) | copy-start | bytes 442372
  7.2 141.7 %copy-start.76 = (f32[2,2,768]{2,1,0:T(2,128)S(1)}, f32[2,2,768]{2,1,0:T(2,128)}, u32[]{:S(2)}) copy-start(f32[2,2,768]{2,1,0:T(2,128)} %param.35) | copy-start | bytes 36868
  7.2 142.3 %copy-start.77 = (f32[2,2,768]{2,1,0:T(2,128)S(1)}, f32[2,2,768]{2,1,0:T(2,128)}, u32[]{:S(2)}) copy-start(f32[2,2,768]{2,1,0:T(2,128)} %param.36) | copy-start | bytes 36868
  7.2 142.9 %all-gather.21.cloned.1.call-start = ((), (), s32[]{:S(2)}) async-start(), calls=%async_computation.6 | async-start | bytes 2359296 | tf_op jit(solution)/shard_map/all_gather | solution.py:135
  7.9 187.0 %all-gather.25.cloned.1.call-start = ((), (), s32[]{:S(2)}) async-start(), calls=%async_computation.10 | async-start | bytes 1216512 | tf_op jit(solution)/shard_map/all_gather | solution.py:66
  9.6 188.3 %all-gather.27.cloned.1.call-start = ((), (), s32[]{:S(2)}) async-start(), calls=%async_computation.11 | async-start | bytes 4866048 | tf_op jit(solution)/shard_map/all_gather | solution.py:67
  11.5 206.4 %all-gather.29.cloned.1.call-start = ((), (), s32[]{:S(2)}) async-start(), calls=%async_computation.12 | async-start | bytes 4866048 | tf_op jit(solution)/shard_map/all_gather | solution.py:68
  13.4 346.1 %all-gather.23.cloned.1.call-start = ((), (), s32[]{:S(2)}) async-start(), calls=%async_computation.7 | async-start | bytes 2359296 | tf_op jit(solution)/shard_map/all_gather | solution.py:135
  14.4 138.3 %copy-start.36 = (f32[2,768,8]{1,2,0:T(8,128)S(1)}, f32[2,768,8]{1,2,0:T(8,128)}, u32[]{:S(2)}) copy-start(f32[2,768,8]{1,2,0:T(8,128)} %param.33) | copy-start | bytes 147460
  61.1 93.0 %copy-start.26 = (bf16[1,768,384]{2,1,0:T(8,128)(2,1)}, bf16[1,768,384]{2,1,0:T(8,128)(2,1)S(1)}, u32[]{:S(2)}) copy-start(bf16[1,768,384]{2,1,0:T(8,128)(2,1)S(1)} %all-gather) | copy-start | bytes 1769476
  103.8 50.3 %copy-start.52 = (f32[2,8,384]{2,1,0:T(8,128)S(1)}, f32[2,8,384]{2,1,0:T(8,128)}, u32[]{:S(2)}) copy-start(f32[2,8,384]{2,1,0:T(8,128)} %param.34) | copy-start | bytes 73732
  149.5 68.4 %copy-start.64 = (f32[768]{0:T(1024)}, f32[768]{0:T(1024)S(1)}, u32[]{:S(2)}) copy-start(f32[768]{0:T(1024)S(1)} %get-tuple-element.590) | copy-start | bytes 9220
  149.5 259.2 %copy-start.60 = (f32[768]{0:T(1024)}, f32[768]{0:T(1024)S(1)}, u32[]{:S(2)}) copy-start(f32[768]{0:T(1024)S(1)} %get-tuple-element.589) | copy-start | bytes 9220
  161.3 8.8 %copy-start.40 = (bf16[1024,8]{0,1:T(8,128)(2,1)}, bf16[1024,8]{0,1:T(8,128)(2,1)S(1)}, u32[]{:S(2)}) copy-start(bf16[1024,8]{0,1:T(8,128)(2,1)S(1)} %convolution_convert_fusion.6) | copy-start | bytes 49156
  188.3 28.7 %copy-start = (bf16[2,512,6,64]{1,3,2,0:T(8,128)(2,1)}, bf16[2,512,6,64]{1,3,2,0:T(8,128)(2,1)S(1)}, u32[]{:S(2)}) copy-start(bf16[2,512,6,64]{1,3,2,0:T(8,128)(2,1)S(1)} %get-tuple-element.1089) | copy-start | bytes 2359300
  188.3 28.7 %copy-start.2 = (bf16[2,512,6,64]{1,3,2,0:T(8,128)(2,1)}, bf16[2,512,6,64]{1,3,2,0:T(8,128)(2,1)S(1)}, u32[]{:S(2)}) copy-start(bf16[2,512,6,64]{1,3,2,0:T(8,128)(2,1)S(1)} %get-tuple-element.1090) | copy-start | bytes 2359300
  197.5 20.3 %copy-start.9 = (f32[512,768]{1,0:T(8,128)}, f32[512,768]{1,0:T(8,128)S(1)}, u32[]{:S(2)}) copy-start(f32[512,768]{1,0:T(8,128)S(1)} %get-tuple-element.704) | copy-start | bytes 4718596
  197.6 20.3 %copy-start.48 = (f32[512]{0:T(512)}, f32[512]{0:T(512)S(1)}, u32[]{:S(2)}) copy-start(f32[512]{0:T(512)S(1)} %broadcast_multiply_fusion.3) | copy-start | bytes 6148
  197.9 19.2 %copy-start.71 = (f32[512]{0:T(512)}, f32[512]{0:T(512)S(1)}, u32[]{:S(2)}) copy-start(f32[512]{0:T(512)S(1)} %multiply_reduce_fusion.9) | copy-start | bytes 6148
  197.9 20.0 %copy-start.58 = (f32[512]{0:T(512)}, f32[512]{0:T(512)S(1)}, u32[]{:S(2)}) copy-start(f32[512]{0:T(512)S(1)} %fusion.243) | copy-start | bytes 6148
  225.5 183.2 %copy-start.4 = (f32[512,768]{1,0:T(8,128)}, f32[512,768]{1,0:T(8,128)S(1)}, u32[]{:S(2)}) copy-start(f32[512,768]{1,0:T(8,128)S(1)} %get-tuple-element.708) | copy-start | bytes 4718596
  225.5 183.2 %copy-start.62 = (f32[512]{0:T(512)}, f32[512]{0:T(512)S(1)}, u32[]{:S(2)}) copy-start(f32[512]{0:T(512)S(1)} %broadcast_multiply_fusion.2) | copy-start | bytes 6148
  225.8 138.8 %copy-start.73 = (f32[512]{0:T(512)}, f32[512]{0:T(512)S(1)}, u32[]{:S(2)}) copy-start(f32[512]{0:T(512)S(1)} %multiply_reduce_fusion.8) | copy-start | bytes 6148
  225.8 182.9 %copy-start.69 = (f32[512]{0:T(512)}, f32[512]{0:T(512)S(1)}, u32[]{:S(2)}) copy-start(f32[512]{0:T(512)S(1)} %fusion.244) | copy-start | bytes 6148
  227.0 179.8 %all-gather.31.cloned.1.call-start = ((), (), s32[]{:S(2)}) async-start(), calls=%async_computation.13 | async-start | bytes 1216512 | tf_op jit(solution)/shard_map/all_gather | solution.py:66
  227.6 186.8 %all-gather.33.cloned.1.call-start = ((), (), s32[]{:S(2)}) async-start(), calls=%async_computation.14 | async-start | bytes 4866048 | tf_op jit(solution)/shard_map/all_gather | solution.py:67
  228.4 206.1 %all-gather.35.cloned.1.call-start = ((), (), s32[]{:S(2)}) async-start(), calls=%async_computation.15 | async-start | bytes 4866048 | tf_op jit(solution)/shard_map/all_gather | solution.py:68
  271.8 92.9 %copy-start.30 = (bf16[1,768,384]{2,1,0:T(8,128)(2,1)}, bf16[1,768,384]{2,1,0:T(8,128)(2,1)S(1)}, u32[]{:S(2)}) copy-start(bf16[1,768,384]{2,1,0:T(8,128)(2,1)S(1)} %all-gather.7) | copy-start | bytes 1769476
  402.2 12.3 %copy-start.66 = (f32[768]{0:T(1024)S(1)}, f32[768]{0:T(1024)}, u32[]{:S(2)}) copy-start(f32[768]{0:T(1024)} %get-tuple-element.591) | copy-start | bytes 9220
  402.2 12.3 %copy-start.68 = (f32[768]{0:T(1024)S(1)}, f32[768]{0:T(1024)}, u32[]{:S(2)}) copy-start(f32[768]{0:T(1024)} %get-tuple-element.595) | copy-start | bytes 9220
  402.2 6.5 all-to-all-start.1
  406.6 122.1 %reduce-scatter.3.cloned.1.call-start = ((), (), s32[]{:S(2)}) async-start(), calls=%async_computation.8 | async-start | bytes 2359296 | tf_op jit(solution)/shard_map/reduce_scatter | solution.py:239
  434.5 12.8 %slice-start.6 = ((s8[4718592]{0:T(1024)(128)(4,1)}), s8[4194304]{0:T(1024)(128)(4,1)S(1)}, s32[]{:S(2)}) async-start(s8[4718592]{0:T(1024)(128)(4,1)} %bitcast.488), calls=%async_computation.23 | async-start | bytes 8388608
  434.5 9.4 %copy-start.22 = (bf16[512,768]{1,0:T(8,128)(2,1)S(1)}, bf16[512,768]{1,0:T(8,128)(2,1)}, u32[]{:S(2)}) copy-start(bf16[512,768]{1,0:T(8,128)(2,1)} %param.37) | copy-start | bytes 2359300
  434.5 9.4 %copy-start.67 = (f32[768]{0:T(1024)S(1)}, f32[768]{0:T(1024)}, u32[]{:S(2)}) copy-start(f32[768]{0:T(1024)} %get-tuple-element.588) | copy-start | bytes 9220
  434.5 9.9 %copy-start.75 = (f32[768]{0:T(1024)S(1)}, f32[768]{0:T(1024)}, u32[]{:S(2)}) copy-start(f32[768]{0:T(1024)} %get-tuple-element.592) | copy-start | bytes 9220
  434.5 12.7 %slice-start.7 = ((s8[4718592]{0:T(1024)(128)(4,1)}), s8[524288]{0:T(1024)(128)(4,1)S(1)}, s32[]{:S(2)}) async-start(s8[4718592]{0:T(1024)(128)(4,1)} %bitcast.488), calls=%async_computation.24 | async-start | bytes 1048576
  477.6 29.3 %copy-start.51 = (f32[2,8,384]{2,1,0:T(8,128)S(1)}, f32[2,8,384]{2,1,0:T(8,128)}, u32[]{:S(2)}) copy-start(f32[2,8,384]{2,1,0:T(8,128)} %param.32) | copy-start | bytes 73732
  522.8 213.9 %all-reduce.3.cloned.1.call-start = ((), (), s32[]{:S(2)}) async-start(), calls=%async_computation.16 | async-start | bytes 393216 | tf_op jit(solution)/shard_map/psum | solution.py:328
  531.1 9.8 %slice-start = ((s8[6291456]{0:T(1024)(128)(4,1)}), s8[4194304]{0:T(1024)(128)(4,1)S(1)}, s32[]{:S(2)}) async-start(s8[6291456]{0:T(1024)(128)(4,1)} %bitcast.482), calls=%async_computation.17 | async-start | bytes 8388608
  540.9 9.2 %copy-start.72 = (f32[512]{0:T(512)S(1)}, f32[512]{0:T(512)}, u32[]{:S(2)}) copy-start(f32[512]{0:T(512)} %copy-done.71) | copy-start | bytes 6148
  540.9 9.2 %copy-start.59 = (f32[512]{0:T(512)S(1)}, f32[512]{0:T(512)}, u32[]{:S(2)}) copy-start(f32[512]{0:T(512)} %copy-done.58) | copy-start | bytes 6148
  551.8 9.6 %copy-start.1 = (bf16[2,512,6,64]{1,3,2,0:T(8,128)(2,1)S(1)}, bf16[2,512,6,64]{1,3,2,0:T(8,128)(2,1)}, u32[]{:S(2)}) copy-start(bf16[2,512,6,64]{1,3,2,0:T(8,128)(2,1)} %copy-done) | copy-start | bytes 2359300
  551.8 9.6 %copy-start.3 = (bf16[2,512,6,64]{1,3,2,0:T(8,128)(2,1)S(1)}, bf16[2,512,6,64]{1,3,2,0:T(8,128)(2,1)}, u32[]{:S(2)}) copy-start(bf16[2,512,6,64]{1,3,2,0:T(8,128)(2,1)} %copy-done.2) | copy-start | bytes 2359300
  551.8 9.6 %copy-start.33 = (f32[2,6,512]{2,1,0:T(8,128)S(1)}, f32[2,6,512]{2,1,0:T(8,128)}, u32[]{:S(2)}) copy-start(f32[2,6,512]{2,1,0:T(8,128)} %copy-done.32) | copy-start | bytes 73732
  598.5 8.4 %copy-start.57 = (f32[8,768]{1,0:T(8,128)}, f32[8,768]{1,0:T(8,128)S(1)}, u32[]{:S(2)}) copy-start(f32[8,768]{1,0:T(8,128)S(1)} %fusion.170) | copy-start | bytes 73732
  609.6 142.0 %reduce-scatter.5.cloned.1.call-start = ((), (), s32[]{:S(2)}) async-start(), calls=%async_computation.9 | async-start | bytes 2359296 | tf_op jit(solution)/shard_map/reduce_scatter | solution.py:239
  (60 other events, 260.6 us)
Sparse Core Ops, SparseCore 0:
  9.6 12.4 all-gather.20
  25.6 55.6 all-gather.24
  84.2 67.4 all-gather.26
  155.0 62.7 all-gather.28
  227.2 8.6 all-gather.22
  239.1 56.9 all-gather.30
  299.0 64.2 all-gather.32
  366.2 63.0 all-gather.34
  522.9 5.5 reduce-scatter.2
  609.7 126.9 all-reduce.2
  741.4 10.1 reduce-scatter.4
where the time goes:
time: 773 us; the launch traced here: 762 us
  blocking collectives  280 us (36%)
  matrix products  218 us (28%)
  waiting for transfers between devices  137 us (18%)
  local copies, waits for them, and re-layouts  53.2 us (7%)
  other arithmetic  46 us (6%)
  between operations  15.6 us (2%)
    psum x1, waiting for transfers between devices, body(): lax.psum((wide_terms[0], wide_terms[1], wide_terms[2], wide_terms[3]), ('...  121 us
    all_gather x2, blocking collectives, gather_head(): lax.all_gather(pieces[1], 'dp', axis=0, tiled=True)  90.1 us
    all_gather x2, blocking collectives, gather_head(): lax.all_gather(pieces[2], 'dp', axis=0, tiled=True)  89.4 us
    all_gather x2, blocking collectives, gather_head(): lax.all_gather(pieces[0], 'dp', axis=0, tiled=True)  85.3 us
    dot_general x12, matrix products, dot_right_t(): lax.dot_general(left, right, (((1,), (1,)), ((), ())), preferred_element_...  46.5 us
    dot_general x2, matrix products, layer_forward(): jnp.dot(normed.astype(jnp.bfloat16), up_w, preferred_element_type=jnp.flo...  39.2 us
    dot_general x8, matrix products, exact_right_t(): lax.dot_general(left, right, (((1,), (1,)), ((), ())), precision=highest,...  19.2 us
    dot_general x2, matrix products, layer_forward(): jnp.dot(activated, down_w, preferred_element_type=jnp.float32)  16.9 us
  transfers between devices with their start and end apart: 12, of which 4 were waited for; matrix products, arithmetic and copies ran while one was open for 20% of the time, Pallas kernels for 0%

commit v1 on v0

v1 whole, which is shorter than its diff:
```python
import functools

import jax
import jax.numpy as jnp
from jax import lax
from jax.experimental import pallas as pl
from jax.experimental.pallas import tpu as pltpu
from jax.sharding import PartitionSpec as P

HEAD_DIM = 64
EPS = 1e-05
BF = jnp.bfloat16
F32 = jnp.float32
TAIL_T = 0.3
TAIL_POLY = (
    0.11962930085896954,
    0.12075392575453824,
    0.09991367489054633,
    0.1285610470550418,
    -0.0536825996264651,
    0.20635243353234553,
    -0.1572025001665815,
    0.03567464489776359,
)
PHI_SCALE = 0.3989422804014327
VMEM_LIMIT = 60 * 1024 * 1024


def mm(left, right):
    return lax.dot_general(left, right, (((1,), (0,)), ((), ())), preferred_element_type=F32)


def mm_rt(left, right):
    return lax.dot_general(left, right, (((1,), (1,)), ((), ())), preferred_element_type=F32)


def mm_lt(left, right):
    return lax.dot_general(left, right, (((0,), (0,)), ((), ())), preferred_element_type=F32)


def chip_grid(count):
    side = round((count / 2) ** (1 / 3))
    if 2 * side**3 == count:
        return (2 * side, side, side)
    return (count, 1, 1)


def shift(values, grid, axis, by):
    nz, ny, nx = grid
    pairs = []
    for z in range(nz):
        for y in range(ny):
            for x in range(nx):
                to = [z, y, x]
                to[axis] = (to[axis] + by) % grid[axis]
                pairs.append(((z * ny + y) * nx + x, (to[0] * ny + to[1]) * nx + to[2]))
    return lax.ppermute(values, "dp", pairs)


def swap_cores(values):
    size = lax.axis_size("head")
    return lax.ppermute(values, "head", [(i, (i + 1) % size) for i in range(size)])


def after(values, *earlier):
    return lax.optimization_barrier((values, *earlier))[0]


def spread_z(packed, grid):
    return [packed] + [shift(packed, grid, 0, k) for k in range(1, grid[0])]


def spread_yx(part, grid, first, second):
    lines = jnp.stack([part] + [shift(part, grid, first, k) for k in range(1, grid[first])])
    return [lines] + [shift(lines, grid, second, k) for k in range(1, grid[second])]


def copy_list(grid, a_refs, b_refs, a_jobs, b_jobs, sem):
    nz, ny, nx = grid
    dp = lax.axis_index("dp")
    core = lax.axis_index("head")
    z, y, x = dp // (ny * nx), (dp // nx) % ny, dp % nx
    for refs, jobs, first_is_y in ((a_refs, a_jobs, True), (b_refs, b_jobs, False)):
        if not jobs:
            continue
        for last, pair in enumerate(refs):
            for other in range(2):
                ref = pair[other]
                c = core if other == 0 else 1 - core
                for first in range(ref.shape[0]):
                    for kz in range(nz):
                        zz = lax.rem(z + nz - kz, nz)
                        if first_is_y:
                            yy, xx = lax.rem(y + ny - first, ny), lax.rem(x + nx - last, nx)
                        else:
                            yy, xx = lax.rem(y + ny - last, ny), lax.rem(x + nx - first, nx)
                        owner = (zz * ny + yy) * nx + xx
                        for job in jobs:
                            job(ref.at[first, kz], owner, c, sem)


def job_cols(dst, rows, lane0, width, col0):
    def run(src, owner, c, sem):
        row = pl.multiple_of(owner * rows, 16)
        col = pl.multiple_of(col0 + c * width, 128)
        pltpu.make_async_copy(
            src.at[:, pl.ds(lane0, width)], dst.at[pl.ds(row, rows), pl.ds(col, width)], sem
        ).start()

    return run


def job_rows(dst, rows, parts, part, lane0):
    def run(src, owner, c, sem):
        row = pl.multiple_of(((owner * 2 + c) * parts + part) * rows, 16)
        width = dst.shape[1]
        pltpu.make_async_copy(
            src.at[:, pl.ds(lane0 + part * width, width)], dst.at[pl.ds(row, rows), :], sem
        ).start()

    return run


def wait_all(dst, sem):
    pltpu.make_async_copy(dst, dst, sem).wait()


class Weights:
    def __init__(self, grid, arrays):
        self.grid = grid
        self.arrays = arrays

    def flat(self, names):
        leaves = []
        for name in names:
            leaves += jax.tree.leaves(self.arrays[name])
        return leaves

    def unflat(self, names, refs):
        out, at = {}, 0
        for name in names:
            leaves, tree = jax.tree.flatten(self.arrays[name])
            out[name] = jax.tree.unflatten(tree, refs[at : at + len(leaves)])
            at += len(leaves)
        return out, refs[at:]


def start_qkv(grid, refs, dst, sem):
    if "qkv" in refs:
        pltpu.make_async_copy(refs["qkv"], dst, sem).start()
        return
    rows, half = refs["qk"][0][0].shape[2], dst.shape[1] // 6
    copy_list(
        grid,
        refs["qk"],
        refs["v"],
        (job_cols(dst, rows, 0, half, 0), job_cols(dst, rows, half, half, 2 * half)),
        (job_cols(dst, rows, 0, half, 4 * half),),
        sem,
    )


def start_out(grid, refs, dst, sem):
    if "out" in refs:
        pltpu.make_async_copy(refs["out"], dst, sem).start()
        return
    ref = refs["rest"][0][0]
    rows, half = ref.shape[2], dst.shape[1] // 2
    copy_list(
        grid, (), refs["rest"], (), (job_cols(dst, rows, ref.shape[3] - half, half, 0),), sem
    )


def start_up(grid, refs, dst, sem):
    if "out" in refs:
        pltpu.make_async_copy(refs["up"], dst, sem).start()
        return
    rows, half = refs["up"][0][0].shape[2], dst.shape[1] // 2
    copy_list(grid, refs["up"], (), (job_cols(dst, rows, 0, half, 0),), (), sem)


def start_down(grid, refs, dst, sem):
    if "out" in refs:
        pltpu.make_async_copy(refs["down"], dst, sem).start()
        return
    ref = refs["rest"][0][0]
    rows = ref.shape[2]
    parts = ref.shape[3] // dst.shape[1]
    jobs = tuple(job_rows(dst, rows, parts, i, 0) for i in range(parts))
    copy_list(grid, (), refs["rest"], (), jobs, sem)


QKV_NAMES = {True: ("qk", "v"), False: ("qkv",)}
DENSE_NAMES = {True: ("up", "rest"), False: ("out", "up", "down")}


def kernel_call(body, outs, scratch, flops, ins_vmem, ins_any, scalar):
    specs = [pl.BlockSpec(memory_space=pltpu.SMEM)] * len(scalar)
    specs += [pl.BlockSpec(memory_space=pltpu.VMEM)] * len(ins_vmem)
    specs += [pl.BlockSpec(memory_space=pl.ANY)] * len(ins_any)
    moved = sum(v.size * v.dtype.itemsize for v in (*ins_vmem, *ins_any, *outs))
    return pl.pallas_call(
        body,
        out_shape=tuple(outs),
        in_specs=specs,
        out_specs=tuple([pl.BlockSpec(memory_space=pltpu.VMEM)] * len(outs)),
        scratch_shapes=scratch,
        compiler_params=pltpu.CompilerParams(vmem_limit_bytes=VMEM_LIMIT),
        cost_estimate=pl.CostEstimate(flops=flops, bytes_accessed=moved, transcendentals=0),
    )(*scalar, *ins_vmem, *ins_any)


def sds(shape, dtype):
    return jax.ShapeDtypeStruct(shape, dtype)


def mask_bias(length, rows):
    near = lax.broadcasted_iota(jnp.int32, (rows, rows), 0) // length
    far = lax.broadcasted_iota(jnp.int32, (rows, rows), 1) // length
    return jnp.where(near == far, 0.0, -1e30).astype(F32)


def block_length(len_ref):
    return len_ref[lax.axis_index("head")]


def attend_forward(x, down, up, weights, pieces, lengths):
    rows, width = x.shape
    names = QKV_NAMES[pieces]
    wide = 3 * width
    pairs = width // 128

    def body(len_ref, x_ref, down_ref, up_ref, *rest):
        refs, rest = weights.unflat(names, rest)
        q_ref, k_ref, v_ref, o_ref, lse_ref, mid_ref, w_ref, bias_ref, sem = rest
        start_qkv(weights.grid, refs, w_ref, sem)
        r = x_ref[...].astype(BF)
        mid = mm(r, down_ref[...]).astype(BF)
        mid_ref[...] = mid
        bias_ref[...] = mask_bias(block_length(len_ref), rows)
        wait_all(w_ref, sem)
        tile = 256
        for at, out in enumerate((q_ref, k_ref, v_ref)):
            for j in range(0, width, tile):
                c = at * width + j
                total = mm(r, w_ref[:, c : c + tile])
                if at != 1:
                    total += mm(mid, up_ref[:, c : c + tile])
                out[:, j : j + tile] = total.astype(BF)

        lane = lax.broadcasted_iota(jnp.int32, (rows, 128), 1)
        low = lane < HEAD_DIM
        zero = jnp.zeros((rows, 128), BF)
        one_low = jnp.where(low, 1.0, 0.0).astype(BF)
        one_high = jnp.where(low, 0.0, 1.0).astype(BF)

        def pair(p, carry):
            lanes = pl.ds(pl.multiple_of(p * 128, 128), 128)
            q2 = q_ref[:, lanes] * 0.125
            k2 = k_ref[:, lanes]
            v2 = v_ref[:, lanes]
            bias = bias_ref[...]
            s0 = mm_rt(q2, jnp.where(low, k2, zero)) + bias
            s1 = mm_rt(q2, jnp.where(low, zero, k2)) + bias
            m0 = jnp.max(s0, -1, keepdims=True)
            m1 = jnp.max(s1, -1, keepdims=True)
            e0 = jnp.exp(s0 - m0).astype(BF)
            e1 = jnp.exp(s1 - m1).astype(BF)
            v0 = jnp.concatenate([jnp.where(low, v2, zero), one_low], 1)
            v1 = jnp.concatenate([jnp.where(low, zero, v2), one_high], 1)
            both = mm(e0, v0) + mm(e1, v1)
            total = both[:, 128:]
            o_ref[:, lanes] = (both[:, :128] / total).astype(BF)
            lse = jnp.where(low, m0, m1) + jnp.log(total)
            flip = lse.T
            lse_ref[2 * p] = flip[0:8]
            lse_ref[2 * p + 1] = flip[64:72]
            return carry

        lax.fori_loop(0, pairs, pair, 0)

    act = sds((rows, width), BF)
    outs = (act, act, act, act, sds((2 * pairs, 8, rows), F32), sds((rows, 128), BF))
    flops = 2 * rows * width * wide + 4 * rows * rows * width * 4
    return kernel_call(
        body,
        outs,
        [
            pltpu.VMEM((width, wide), BF),
            pltpu.VMEM((rows, rows), F32),
            pltpu.SemaphoreType.DMA,
        ],
        flops,
        (x, down, up),
        weights.flat(names),
        (lengths,),
    )


def normalize(values):
    center = values - jnp.mean(values, -1, keepdims=True)
    scale = lax.rsqrt(jnp.mean(center * center, -1, keepdims=True) + EPS)
    return center * scale, scale


def gelu_pair(u):
    size = jnp.abs(u)
    t = 1.0 / (1.0 + TAIL_T * size)
    bell = jnp.exp(-0.5 * (u * u))
    poly = jnp.full_like(u, TAIL_POLY[-1])
    for coef in TAIL_POLY[-2::-1]:
        poly = poly * t + coef
    tail = poly * (t * bell)
    value = jnp.maximum(u, 0.0) - size * tail
    slope = jnp.where(u < 0.0, tail, 1.0 - tail) + u * (bell * PHI_SCALE)
    return value, slope


def dense_forward(x, attended, rows8, weights, pieces, out_type):
    rows, width = x.shape
    ff = weights.ff
    names = DENSE_NAMES[pieces]
    tile = 256

    def body(x_ref, o_ref, rows_ref, *rest):
        refs, rest = weights.unflat(names, rest)
        out_ref, n1_ref, n2_ref, rs_ref, slope_ref, wo_ref, wu_ref, wd_ref, y_ref, z_ref, sem = rest
        start_out(weights.grid, refs, wo_ref, sem.at[0])
        start_up(weights.grid, refs, wu_ref, sem.at[1])
        start_down(weights.grid, refs, wd_ref, sem.at[2])
        wait_all(wo_ref, sem.at[0])
        hid = x_ref[...].astype(F32) + mm(o_ref[...], wo_ref[...])
        n1, rs1 = normalize(hid)
        n1_ref[...] = n1.astype(BF)
        y = n1 * rows_ref[0:1] + rows_ref[1:2]
        z_ref[...] = y
        y_ref[...] = y.astype(BF)
        wait_all(wu_ref, sem.at[1])
        wait_all(wd_ref, sem.at[2])

        def step(j, carry):
            cols = pl.ds(pl.multiple_of(j * tile, tile), tile)
            u = mm(y_ref[...], wu_ref[:, cols])
            value, slope = gelu_pair(u)
            slope_ref[:, cols] = slope.astype(BF)
            z_ref[...] += mm(value.astype(BF), wd_ref[cols, :])
            return carry

        lax.fori_loop(0, ff // tile, step, 0)
        n2, rs2 = normalize(z_ref[...])
        n2_ref[...] = n2.astype(BF)
        lane = lax.broadcasted_iota(jnp.int32, (rows, 128), 1)
        rs_ref[...] = jnp.where(lane < 64, rs1, rs2)
        out_ref[...] = (n2 * rows_ref[2:3] + rows_ref[3:4]).astype(out_type)

    outs = (
        sds((rows, width), out_type),
        sds((rows, width), BF),
        sds((rows, width), BF),
        sds((rows, 128), F32),
        sds((rows, ff), BF),
    )
    flops = 2 * rows * width * (width + 2 * ff)
    return kernel_call(
        body,
        outs,
        [
            pltpu.VMEM((width, width), BF),
            pltpu.VMEM((width, ff), BF),
            pltpu.VMEM((ff, width), BF),
            pltpu.VMEM((rows, width), BF),
            pltpu.VMEM((rows, width), F32),
            pltpu.SemaphoreType.DMA((3,)),
        ],
        flops,
        (x, attended, rows8),
        weights.flat(names),
        (),
    )


def norm_backward(gn, n, scale):
    return (gn - jnp.mean(gn, -1, keepdims=True) - n * jnp.mean(gn * n, -1, keepdims=True)) * scale


def dense_backward(g, saved, rows8, weights, pieces):
    n1, n2, rs, slope = saved
    rows, width = g.shape
    ff = weights.ff
    names = DENSE_NAMES[pieces]
    tile = 256

    def body(g_ref, n1_ref, n2_ref, rs_ref, slope_ref, rows_ref, *rest):
        refs, rest = weights.unflat(names, rest)
        ghid_ref, go_ref, wo_ref, wu_ref, wd_ref, gz_ref, gy_ref, sem = rest
        start_down(weights.grid, refs, wd_ref, sem.at[2])
        start_up(weights.grid, refs, wu_ref, sem.at[1])
        start_out(weights.grid, refs, wo_ref, sem.at[0])
        gn = g_ref[...].astype(F32) * rows_ref[2:3]
        gz = norm_backward(gn, n2_ref[...].astype(F32), rs_ref[:, 64:65])
        gz_ref[...] = gz.astype(BF)
        gy_ref[...] = gz
        wait_all(wd_ref, sem.at[2])
        wait_all(wu_ref, sem.at[1])

        def step(j, carry):
            cols = pl.ds(pl.multiple_of(j * tile, tile), tile)
            ga = mm_rt(gz_ref[...], wd_ref[cols, :])
            gu = (ga * slope_ref[:, cols].astype(F32)).astype(BF)
            gy_ref[...] += mm_rt(gu, wu_ref[:, cols])
            return carry

        lax.fori_loop(0, ff // tile, step, 0)
        gn1 = gy_ref[...] * rows_ref[0:1]
        ghid = norm_backward(gn1, n1_ref[...].astype(F32), rs_ref[:, 0:1])
        ghid_ref[...] = ghid
        wait_all(wo_ref, sem.at[0])
        go_ref[...] = mm_rt(ghid.astype(BF), wo_ref[...]).astype(BF)

    outs = (sds((rows, width), F32), sds((rows, width), BF))
    flops = 2 * rows * width * (width + 2 * ff)
    return kernel_call(
        body,
        outs,
        [
            pltpu.VMEM((width, width), BF),
            pltpu.VMEM((width, ff), BF),
            pltpu.VMEM((ff, width), BF),
            pltpu.VMEM((rows, width), BF),
            pltpu.VMEM((rows, width), F32),
            pltpu.SemaphoreType.DMA((3,)),
        ],
        flops,
        (g, n1, n2, rs, slope, rows8),
        weights.flat(names),
        (),
    )


def attend_backward(saved, go, lengths):
    q, k, v, o, lse = saved
    rows, width = q.shape
    pairs = width // 128

    def body(len_ref, q_ref, k_ref, v_ref, o_ref, go_ref, lse_ref, gq_ref, gk_ref, gv_ref, bias_ref):
        bias_ref[...] = mask_bias(block_length(len_ref), rows)
        low = lax.broadcasted_iota(jnp.int32, (rows, 128), 1) < HEAD_DIM
        zero = jnp.zeros((rows, 128), BF)
        side = lax.broadcasted_iota(jnp.int32, (16, 128), 0) < 8
        pick = (side == (lax.broadcasted_iota(jnp.int32, (16, 128), 1) < HEAD_DIM)).astype(F32)

        def pair(p, carry):
            lanes = pl.ds(pl.multiple_of(p * 128, 128), 128)
            q2 = q_ref[:, lanes] * 0.125
            k2 = k_ref[:, lanes]
            v2 = v_ref[:, lanes]
            go2 = go_ref[:, lanes]
            prod = go2.astype(F32) * o_ref[:, lanes].astype(F32)
            dots = lax.dot_general(
                pick,
                prod,
                (((1,), (1,)), ((), ())),
                precision=lax.Precision.HIGHEST,
                preferred_element_type=F32,
            )
            gq = jnp.zeros((rows, 128), F32)
            gk = jnp.zeros((rows, 128), F32)
            gv = jnp.zeros((rows, 128), F32)
            for h in range(2):
                keep = (lambda t: jnp.where(low, t, zero)) if h == 0 else (lambda t: jnp.where(low, zero, t))
                qh, kh, goh = keep(q2), keep(k2), keep(go2)
                s = mm_rt(k2, qh) + bias_ref[...]
                prob = jnp.exp(s - lse_ref[2 * p + h][0:1])
                gp = mm_rt(v2, goh)
                gs = (prob * (gp - dots[8 * h : 8 * h + 1])).astype(BF)
                gq += mm_lt(gs, kh)
                gk += mm(gs, qh)
                gv += mm(prob.astype(BF), goh)
            gq_ref[:, lanes] = (gq * 0.125).astype(BF)
            gk_ref[:, lanes] = gk.astype(BF)
            gv_ref[:, lanes] = gv.astype(BF)
            return carry

        lax.fori_loop(0, pairs, pair, 0)

    act = sds((rows, width), BF)
    return kernel_call(
        body,
        (act, act, act),
        [pltpu.VMEM((rows, rows), F32)],
        20 * rows * rows * width,
        (q, k, v, o, go, lse),
        (),
        (lengths,),
    )


def adapter_grads(x, mid, gq, gv, up):
    rows, width = x.shape

    def body(x_ref, mid_ref, gq_ref, gv_ref, up_ref, gm_ref, sums_ref):
        gq, gv, mid = gq_ref[...], gv_ref[...], mid_ref[...]
        gm = mm_rt(gq, up_ref[:, :width]) + mm_rt(gv, up_ref[:, 2 * width :])
        gm = gm.astype(BF)
        gm_ref[...] = gm
        sums_ref[0:16] = mm_lt(gm, x_ref[...].astype(BF))[0:16]
        sums_ref[16:24] = 2.0 * mm_lt(mid, gq)[0:8]
        sums_ref[24:32] = 2.0 * mm_lt(mid, gv)[8:16]

    return kernel_call(
        body,
        (sds((rows, 128), BF), sds((32, width), F32)),
        [],
        2 * rows * width * 128 * 5,
        (x, mid, gq, gv, up),
        (),
        (),
    )


def input_grad(ghid, gq, gk, gv, gm, down, weights, pieces):
    rows, width = ghid.shape
    names = QKV_NAMES[pieces]

    def body(ghid_ref, gq_ref, gk_ref, gv_ref, gm_ref, down_ref, *rest):
        refs, rest = weights.unflat(names, rest)
        out_ref, w_ref, sem = rest
        start_qkv(weights.grid, refs, w_ref, sem)
        total = ghid_ref[...] + mm_rt(gm_ref[...], down_ref[...])
        wait_all(w_ref, sem)
        total += mm_rt(gq_ref[...], w_ref[:, :width])
        total += mm_rt(gk_ref[...], w_ref[:, width : 2 * width])
        total += mm_rt(gv_ref[...], w_ref[:, 2 * width :])
        out_ref[...] = total

    return kernel_call(
        body,
        (sds((rows, width), F32),),
        [pltpu.VMEM((width, 3 * width), BF), pltpu.SemaphoreType.DMA],
        6 * rows * width * width,
        (ghid, gq, gk, gv, gm, down),
        weights.flat(names),
        (),
    )[0]


def gather_pieces(grid, packs, halves):
    gathered = []
    gate = None
    for packed, (cut_a, cut_b) in zip(packs, halves):
        if gate is not None:
            packed = after(packed, *gate)
        line = spread_z(packed, grid)
        gate = line[1:]
        a_part = jnp.stack([cut_a(piece) for piece in line])
        b_part = jnp.stack([cut_b(piece) for piece in line])
        a_all = spread_yx(a_part, grid, 1, 2)
        b_all = spread_yx(b_part, grid, 2, 1)
        gathered.append(
            (
                [(own, swap_cores(own)) for own in a_all],
                [(own, swap_cores(own)) for own in b_all],
            )
        )
    return gathered


def all_weights(grid, w_query, w_key, w_value, w_out, w_up, w_down):
    layers = w_query.shape[0]
    ff = w_up.shape[2]
    half = w_query.shape[2]
    width = 2 * half
    pieces = w_query.shape[1] % 16 == 0 and lax.axis_size("head") == 2
    everything = []
    if not pieces:
        for at in range(layers):
            qkv = jnp.concatenate([w[at].astype(BF) for w in (w_query, w_key, w_value)], 1)
            qkv = lax.all_gather(qkv, "dp", axis=0, tiled=True)
            qkv = lax.all_gather(qkv, "head", axis=0, tiled=False)
            qkv = qkv.reshape(-1, width, 3, half).transpose(1, 2, 0, 3).reshape(width, 3 * width)
            rest = [
                lax.all_gather(w[at].astype(BF), ("dp", "head"), axis=0, tiled=True)
                for w in (w_out, w_up, w_down)
            ]
            layer = Weights(grid, {"qkv": qkv, "out": rest[0], "up": rest[1], "down": rest[2]})
            layer.ff = ff
            everything.append(layer)
        return pieces, everything
    core = lax.axis_index("head")
    both = jnp.concatenate([w_out, w_up], 2).astype(BF)
    mine = [lax.dynamic_slice_in_dim(both, core * half, half, 2)]
    mine += [lax.dynamic_slice_in_dim(both, width + core * (ff // 2), ff // 2, 2)]
    send = [lax.dynamic_slice_in_dim(both, (1 - core) * half, half, 2)]
    send += [lax.dynamic_slice_in_dim(both, width + (1 - core) * (ff // 2), ff // 2, 2)]
    mine = jnp.concatenate(mine, 2)
    come = swap_cores(jnp.concatenate(send, 2))
    both = jnp.concatenate([jnp.where(core == 0, mine, come), jnp.where(core == 0, come, mine)], 1)
    packs, halves = [], []
    rows = w_query.shape[1]
    for at in range(layers):
        packs.append(
            jnp.concatenate([w[at].astype(BF) for w in (w_query, w_key, w_value)], 1)
        )
        halves.append((lambda t: t[:, :width], lambda t: t[:, width:]))
        wd = w_down[at].astype(BF)
        wd = [wd[i : i + rows] for i in range(0, wd.shape[0], rows)]
        packs.append(jnp.concatenate([both[at, :, half:], *wd, both[at, :, :half]], 1))
        halves.append((lambda t: t[:, : ff // 2], lambda t: t[:, ff // 2 :]))
    gathered = gather_pieces(grid, packs, halves)
    for at in range(layers):
        attn, dense = gathered[2 * at], gathered[2 * at + 1]
        layer = Weights(grid, {"qk": attn[0], "v": attn[1], "up": dense[0], "rest": dense[1]})
        layer.ff = ff
        everything.append(layer)
    return pieces, everything


def sum_over_devices(sums, grid):
    half = sums.shape[1] // 2
    core = lax.axis_index("head")
    mine = lax.dynamic_slice_in_dim(sums, core * half, half, 1)
    other = lax.dynamic_slice_in_dim(sums, (1 - core) * half, half, 1)
    total = mine + swap_cores(other)
    for axis in (2, 1, 0):
        parts = [total] + [shift(total, grid, axis, k) for k in range(1, grid[axis])]
        total = functools.reduce(jnp.add, parts)
    return total


def body(
    tokens,
    seq_len,
    w_query,
    w_key,
    w_value,
    w_out,
    w_up,
    w_down,
    a_query,
    b_query,
    a_value,
    b_value,
    ln_gain,
    ln_bias,
    cotangent,
):
    layers, width = w_query.shape[0], tokens.shape[1]
    rank = a_query.shape[2]
    half = b_query.shape[2]
    grid = chip_grid(lax.axis_size("dp"))
    core = lax.axis_index("head")
    pieces, weights = all_weights(grid, w_query, w_key, w_value, w_out, w_up, w_down)

    own = jnp.stack([b_query, b_value], 1).astype(BF)
    other = swap_cores(own)
    up_all = jnp.concatenate(
        [jnp.where(core == 0, own, other), jnp.where(core == 0, other, own)], -1
    )
    downs, ups, rows8 = [], [], []
    for at in range(layers):
        pair = jnp.concatenate([a_query[at], a_value[at]], 1).astype(BF)
        downs.append(jnp.pad(pair, ((0, 0), (0, 128 - 2 * rank))))
        q_up = jnp.pad(2.0 * up_all[at, 0], ((0, 128 - rank), (0, 0)))
        v_up = jnp.pad(2.0 * up_all[at, 1], ((rank, 128 - 2 * rank), (0, 0)))
        ups.append(jnp.concatenate([q_up, jnp.zeros_like(q_up), v_up], 1))
        rows8.append(
            jnp.pad(
                jnp.stack([ln_gain[at, 0], ln_bias[at, 0], ln_gain[at, 1], ln_bias[at, 1]]),
                ((0, 4), (0, 0)),
            )
        )

    stream = tokens
    saved = []
    for at in range(layers):
        q, k, v, o, lse, mid = attend_forward(stream, downs[at], ups[at], weights[at], pieces, seq_len)
        last = at == layers - 1
        result, n1, n2, rs, slope = dense_forward(
            stream, o, rows8[at], weights[at], pieces, BF if last else F32
        )
        saved.append((stream, mid, (q, k, v, o, lse), (n1, n2, rs, slope)))
        stream = result
    output = stream
    grad = cotangent
    sums = [None] * layers
    for at in reversed(range(layers)):
        x, mid, attn, dense = saved[at]
        ghid, go = dense_backward(grad, dense, rows8[at], weights[at], pieces)
        gq, gk, gv = attend_backward(attn, go, seq_len)
        gm, sums[at] = adapter_grads(x, mid, gq, gv, ups[at])
        grad = input_grad(ghid, gq, gk, gv, gm, downs[at], weights[at], pieces)
    total = sum_over_devices(jnp.concatenate(sums, 0), grid).reshape(layers, 4, rank, half)
    lower = total[:, :2].reshape(layers * 2 * rank, half)
    far = swap_cores(lower)
    lower = jnp.concatenate([jnp.where(core == 0, lower, far), jnp.where(core == 0, far, lower)], 1)
    lower = lower.reshape(layers, 2, rank, width).transpose(0, 1, 3, 2)
    return (output, grad, lower[:, 0], total[:, 2], lower[:, 1], total[:, 3])


def solution(mesh):
    both = ("dp", "head")
    placed = (
        P(both, None),
        P("dp"),
        P(None, "dp", "head"),
        P(None, "dp", "head"),
        P(None, "dp", "head"),
        P(None, both, None),
        P(None, both, None),
        P(None, both, None),
        P(),
        P(None, None, "head"),
        P(),
        P(None, None, "head"),
        P(),
        P(),
        P(both, None),
    )
    return jax.shard_map(
        body,
        mesh=mesh,
        in_specs=placed,
        out_specs=(
            P(both, None),
            P(both, None),
            P(),
            P(None, None, "head"),
            P(),
            P(None, None, "head"),
        ),
        check_vma=False,
    )
```

time: 773 us -> 425 us (0.55)
  blocking collectives: 280 us -> 0 us
  matrix products: 218 us -> 0 us
  Pallas kernels: 0 us -> 194 us
  local copies, waits for them, and re-layouts: 53.2 us -> 8.73 us
  other arithmetic: 46 us -> 7.36 us
  starting transfers between devices: 5.24 us -> 39 us
  waiting for transfers between devices: 137 us -> 170 us
  between operations: 15.6 us -> 1.96 us
    all_gather x6 -> x0, blocking collectives: 265 us -> none  [the longest x2 90.1 us: gather_head(): lax.all_gather(pieces[1], 'dp', axis=0, tiled=True)]
    dot_general x76 -> x0, matrix products: 218 us -> none  [the longest x12 46.5 us: dot_right_t(): lax.dot_general(left, right, (((1,), (1,)), ((), ())), preferred_element_...]
    pallas_call x0 -> x12, Pallas kernels: none -> 194 us  [kernel_call(): pl.pallas_call(body, out_shape=tuple(outs), in_specs=specs, out_specs=tup...]
    ppermute x0 -> x53, waiting for transfers between devices: none -> 170 us  [the longest x33 167 us: shift(): return lax.ppermute(values, 'dp', pairs)]
    psum x1 -> x0, waiting for transfers between devices: 121 us -> none  [body(): lax.psum((wide_terms[0], wide_terms[1], wide_terms[2], wide_terms[3]), ('...]
    ppermute x0 -> x53, starting transfers between devices: none -> 39 us  [the longest x33 36 us: shift(): return lax.ppermute(values, 'dp', pairs)]
    reduce_sum x13 -> x0, other arithmetic: 18.6 us -> none  [the longest x4 8.28 us: layer_norm(): center = values - jnp.mean(values, -1, keepdims=True)]
    all_to_all x3 -> x0, blocking collectives: 15.7 us -> none  [the longest x2 9.16 us: layer_backward(): lax.all_to_all(grad_merged, 'head', split_axis=1, concat_axis=0, tiled=True)]
  transfers between devices with their start and end apart: 12 -> 53, of which waited for: 4 -> 22; matrix products, arithmetic and copies ran while one was open for 20% -> 2% of each run, Pallas kernels for 0% -> 17%
where the time goes in v1:
time: 425 us; the launch traced here: 421 us
  Pallas kernels  194 us (46%)
  waiting for transfers between devices  170 us (40%)
  starting transfers between devices  39 us (9%)
  local copies, waits for them, and re-layouts  8.73 us (2%)
  other arithmetic  7.36 us (2%)
    pallas_call x12, Pallas kernels, kernel_call(): pl.pallas_call(body, out_shape=tuple(outs), in_specs=specs, out_specs=tup...  194 us
    ppermute x33, waiting for transfers between devices, shift(): return lax.ppermute(values, 'dp', pairs)  167 us
    ppermute x33, starting transfers between devices, shift(): return lax.ppermute(values, 'dp', pairs)  36 us
  transfers between devices with their start and end apart: 53, of which 22 were waited for; matrix products, arithmetic and copies ran while one was open for 2% of the time, Pallas kernels for 17%

profile of v1, /device:TPU:0, one launch (start us, length us, event | category | flops | bytes accessed | tf_op | source)
XLA Modules:
  0.0 421.2 jit_solution(2536852770681080382)
XLA Ops:
  3.6 5.1 %collective-permute-start.3 = (bf16[48,1152]{1,0:T(8,128)(2,1)S(1)}, bf16[48,1152]{1,0:T(8,128)(2,1)S(1)}, u32[]{:S(2)}, u32[]{:S(2)}) collective-permute-start(bf16[48,1152]{1,0:T(8,128)(2,1)S(1)} %pad_maximum_fusion.20), channel_id=1, source_target_pairs={{0,24},{2,26},{4,28},{6,30},{8,0},{10,2},{12,4},{14,6},{16,8},{18,... | collective-permute-start | bytes 331784 | tf_op jit(solution)/shard_map/ppermute | solution.py:57
  10.9 1.2 collective-permute-done.3
  12.1 6.2 %collective-permute-done.2 = bf16[48,1152]{1,0:T(8,128)(2,1)S(1)} collective-permute-done((bf16[48,1152]{1,0:T(8,128)(2,1)S(1)}, bf16[48,1152]{1,0:T(8,128)(2,1)S(1)}, u32[]{:S(2)}, u32[]{:S(2)}) %collective-permute-start.2) | collective-permute-done | bytes 110624 | tf_op jit(solution)/shard_map/ppermute | solution.py:57
  18.4 1.6 collective-permute-start.8
  20.0 1.6 collective-permute-start.4
  21.8 1.9 collective-permute-start.15
  24.4 1.9 collective-permute-start.13
  26.5 1.6 collective-permute-done.4
  28.1 1.5 collective-permute-start.10
  29.6 2.4 collective-permute-done.15
  32.0 20.2 %collective-permute-done.14 = bf16[48,3456]{1,0:T(8,128)(2,1)S(1)} collective-permute-done((bf16[48,3456]{1,0:T(8,128)(2,1)S(1)}, bf16[48,3456]{1,0:T(8,128)(2,1)S(1)}, u32[]{:S(2)}, u32[]{:S(2)}) %collective-permute-start.14) | collective-permute-done | bytes 331808 | tf_op jit(solution)/shard_map/ppermute | solution.py:57
  52.3 1.1 collective-permute-start.25
  53.4 2.0 collective-permute-start.24
  55.8 2.0 collective-permute-done.26
  57.7 6.0 %collective-permute-done.25 = bf16[48,1152]{1,0:T(8,128)(2,1)S(1)} collective-permute-done((bf16[48,1152]{1,0:T(8,128)(2,1)S(1)}, bf16[48,1152]{1,0:T(8,128)(2,1)S(1)}, u32[]{:S(2)}, u32[]{:S(2)}) %collective-permute-start.25) | collective-permute-done | bytes 110624 | tf_op jit(solution)/shard_map/ppermute | solution.py:57
  65.2 4.1 collective-permute-done.31
  69.3 3.5 collective-permute-done.27
  72.9 1.5 collective-permute-start.6
  74.4 1.8 collective-permute-start.36
  76.3 14.0 %collective-permute-done.36 = bf16[48,3456]{1,0:T(8,128)(2,1)S(1)} collective-permute-done((bf16[48,3456]{1,0:T(8,128)(2,1)S(1)}, bf16[48,3456]{1,0:T(8,128)(2,1)S(1)}, u32[]{:S(2)}, u32[]{:S(2)}) %collective-permute-start.36) | collective-permute-done | bytes 331808 | tf_op jit(solution)/shard_map/ppermute | solution.py:57
  91.4 10.1 %collective-permute-done.35 = bf16[48,3456]{1,0:T(8,128)(2,1)S(1)} collective-permute-done((bf16[48,3456]{1,0:T(8,128)(2,1)S(1)}, bf16[48,3456]{1,0:T(8,128)(2,1)S(1)}, u32[]{:S(2)}, u32[]{:S(2)}) %collective-permute-start.35) | collective-permute-done | bytes 331808 | tf_op jit(solution)/shard_map/ppermute | solution.py:57
  103.1 1.1 collective-permute-start.33
  105.1 18.7 %collective-permute-done.33.rest_6_ = bf16[2,4,48,384]{3,2,1,0:T(8,128)(2,1)S(1)} collective-permute-done((bf16[2,4,48,384]{3,2,1,0:T(8,128)(2,1)S(1)}, bf16[2,4,48,384]{3,2,1,0:T(8,128)(2,1)S(1)}, u32[]{:S(2)}, u32[]{:S(2)}) %collective-permute-start.33) | collective-permute-done | bytes 294944 | tf_op jit(solution)/shard_map/ppermute | solution.py:57
  127.2 1.6 collective-permute-start.18
  128.9 14.3 %collective-permute-done.42 = bf16[4,48,1920]{2,1,0:T(8,128)(2,1)S(1)} collective-permute-done((bf16[4,48,1920]{2,1,0:T(8,128)(2,1)S(1)}, bf16[4,48,1920]{2,1,0:T(8,128)(2,1)S(1)}, u32[]{:S(2)}, u32[]{:S(2)}) %collective-permute-start.42) | collective-permute-done | bytes 737312 | tf_op jit(solution)/shard_map/ppermute | solution.py:57
  143.2 1.3 pad_maximum_fusion.1.rest_4_
  144.4 27.7 %collective-permute-done.38 = bf16[4,48,1536]{2,1,0:T(8,128)(2,1)S(1)} collective-permute-done((bf16[4,48,1536]{2,1,0:T(8,128)(2,1)S(1)}, bf16[4,48,1536]{2,1,0:T(8,128)(2,1)S(1)}, u32[]{:S(2)}, u32[]{:S(2)}) %collective-permute-start.38) | collective-permute-done | bytes 589856 | tf_op jit(solution)/shard_map/ppermute | solution.py:57
  172.8 1.4 collective-permute-start.40
  179.1 21.1 %collective-permute-done.40.rest_2_ = bf16[2,4,48,1536]{3,2,1,0:T(8,128)(2,1)} collective-permute-done((bf16[2,4,48,1536]{3,2,1,0:T(8,128)(2,1)S(1)}, bf16[2,4,48,1536]{3,2,1,0:T(8,128)(2,1)}, u32[]{:S(2)}, u32[]{:S(2)}) %collective-permute-start.40) | collective-permute-done | bytes 1179680 | tf_op jit(solution)/shard_map/ppermute | solution.py:57
  200.2 6.1 %collective-permute-done.44.rest_6_ = bf16[2,4,48,1920]{3,2,1,0:T(8,128)(2,1)} collective-permute-done((bf16[2,4,48,1920]{3,2,1,0:T(8,128)(2,1)}, bf16[2,4,48,1920]{3,2,1,0:T(8,128)(2,1)}, u32[]{:S(2)}, u32[]{:S(2)}) %collective-permute-start.44) | collective-permute-done | bytes 1474592 | tf_op jit(solution)/shard_map/ppermute | solution.py:57
  206.3 1.1 fusion.7
  208.5 18.7 %shard_map.190 = (bf16[512,768]{1,0:T(8,128)(2,1)}, bf16[512,768]{1,0:T(8,128)(2,1)}, bf16[512,768]{1,0:T(8,128)(2,1)}, bf16[512,768]{1,0:T(8,128)(2,1)}, f32[12...) custom-call(s32[2]{0:T(128)} %len_ref.7, bf16[512,768]{1,0:T(8,128)(2,1)} %x_ref.5, bf16[768,128]{1,0:T(8,128)(2,1)} %pad.28.down_ref, ...), custom_call_target="tpu_custom_call" | custom-call | flops 5033164800 | bytes 8585216 | tf_op jit(solution)/shard_map/pallas_call | solution.py:202
  227.1 25.8 %shard_map.191 = (f32[512,768]{1,0:T(8,128)}, bf16[512,768]{1,0:T(8,128)(2,1)}, bf16[512,768]{1,0:T(8,128)(2,1)}, f32[512,128]{1,0:T(8,128)}, bf16[512,3072]{1,0:T(8,128)(2,1)}) custom-call(bf16[512,768]{1,0:T(8,128)(2,1)} %x_ref.5, bf16[512,768]{1,0:T(8,128)(2,1)} %get-tuple-element.45.o_ref, f32[8,768]{1,0:T(8,128)} %select_maximum_fusion.3.rows_ref, ...), custom_call_target="tpu_custom_call" | custom-call | flops 5435817984 | bytes 18767872 | tf_op jit(solution)/shard_map/pallas_call | solution.py:202
  253.7 18.9 %shard_map.192 = (bf16[512,768]{1,0:T(8,128)(2,1)}, bf16[512,768]{1,0:T(8,128)(2,1)}, bf16[512,768]{1,0:T(8,128)(2,1)}, bf16[512,768]{1,0:T(8,128)(2,1)}, f32[12...) custom-call(s32[2]{0:T(128)} %len_ref.7, f32[512,768]{1,0:T(8,128)} %get-tuple-element.47.x_ref, ...), custom_call_target="tpu_custom_call" | custom-call | flops 5033164800 | bytes 9371648 | tf_op jit(solution)/shard_map/pallas_call | solution.py:202
  273.6 25.8 %shard_map.193 = (bf16[512,768]{1,0:T(8,128)(2,1)}, bf16[512,768]{1,0:T(8,128)(2,1)}, bf16[512,768]{1,0:T(8,128)(2,1)}, f32[512,128]{1,0:T(8,128)}, bf16[512,3072]{1,0:T(8,128)(2,1)}) custom-call(f32[512,768]{1,0:T(8,128)} %get-tuple-element.47.x_ref, bf16[512,768]{1,0:T(8,128)(2,1)} %get-tuple-element.49.o_ref, f32[8,768]{1,0:T(8,128)} %select_maximum_fusion.rows_ref, ...), custom_call_target="tpu_custom_call" | custom-call | flops 5435817984 | bytes 18767872 | tf_op jit(solution)/shard_map/pallas_call | solution.py:202
  299.4 20.9 %shard_map.194 = (f32[512,768]{1,0:T(8,128)}, bf16[512,768]{1,0:T(8,128)(2,1)}) custom-call(bf16[512,768]{1,0:T(8,128)(2,1)} %g_ref.1, bf16[512,768]{1,0:T(8,128)(2,1)} %get-tuple-element.52.n1_ref, bf16[512,768]{1,0:T(8,128)(2,1)} %get-tuple-element.53.n2_ref, f32[512,128]{1,0:T(8,128)} %get-tuple-element.54.rs_ref, ...), custom_call_target="tpu_custom_call" | custom-call | flops 5435817984 | bytes 18767872 | tf_op jit(solution)/shard_map/pallas_call | solution.py:202
  320.3 20.0 %shard_map.195 = (bf16[512,768]{1,0:T(8,128)(2,1)}, bf16[512,768]{1,0:T(8,128)(2,1)}, bf16[512,768]{1,0:T(8,128)(2,1)}) custom-call(s32[2]{0:T(128)} %len_ref.7, bf16[512,768]{1,0:T(8,128)(2,1)} %get-tuple-element.57.q_ref, bf16[512,768]{1,0:T(8,128)(2,1)} %get-tuple-element.58.k_ref, bf16[512,768]{1,0:T(8,128)(2,1)} %get-tuple-element.59.v_ref, ...), custom_call_target="tpu_custom_call" | custom-call | flops 4026531840 | bytes 6488064 | tf_op jit(solution)/shard_map/pallas_call | solution.py:202
  340.3 4.3 %shard_map.196 = (bf16[512,128]{1,0:T(8,128)(2,1)}, f32[32,768]{1,0:T(8,128)}) custom-call(f32[512,768]{1,0:T(8,128)} %get-tuple-element.47.x_ref, bf16[512,128]{1,0:T(8,128)(2,1)} %get-tuple-element.65.mid_ref, bf16[512,768]{1,0:T(8,128)(2,1)} %get-tuple-element.62.gq_ref, bf16[512,768]{1,0:T(8,128)(2,1)} %get-tuple-element.64.gv_ref, ...), custom_call_target="tpu_custom_call" | custom-call | flops 503316480 | bytes 4096000 | tf_op jit(solution)/shard_map/pallas_call | solution.py:202
  344.6 7.4 %shard_map.197.g_ref = f32[512,768]{1,0:T(8,128)} custom-call(f32[512,768]{1,0:T(8,128)} %get-tuple-element.56.ghid_ref, bf16[512,768]{1,0:T(8,128)(2,1)} %get-tuple-element.62.gq_ref, bf16[512,768]{1,0:T(8,128)(2,1)} %get-tuple-element.63.gk_ref, bf16[512,768]{1,0:T(8,128)(2,1)} %get-tuple-element.64.gv_ref, bf16[512,128]{1,0:T(8,128)(2,1)} %get-tuple-element.66.gm_ref, ...), custom_call_target="tpu_custom_call" | custom-call | flops 1811939328 | bytes 9371648 | tf_op jit(solution)/shard_map/pallas_call | solution.py:202
  352.0 21.1 %shard_map.198 = (f32[512,768]{1,0:T(8,128)}, bf16[512,768]{1,0:T(8,128)(2,1)}) custom-call(f32[512,768]{1,0:T(8,128)} %shard_map.197.g_ref, bf16[512,768]{1,0:T(8,128)(2,1)} %get-tuple-element.67.n1_ref, bf16[512,768]{1,0:T(8,128)(2,1)} %get-tuple-element.68.n2_ref, f32[512,128]{1,0:T(8,128)} %get-tuple-element.69.rs_ref, ...), custom_call_target="tpu_custom_call" | custom-call | flops 5435817984 | bytes 19554304 | tf_op jit(solution)/shard_map/pallas_call | solution.py:202
  373.2 19.9 %shard_map.199 = (bf16[512,768]{1,0:T(8,128)(2,1)}, bf16[512,768]{1,0:T(8,128)(2,1)}, bf16[512,768]{1,0:T(8,128)(2,1)}) custom-call(s32[2]{0:T(128)} %len_ref.7, bf16[512,768]{1,0:T(8,128)(2,1)} %get-tuple-element.72.q_ref, bf16[512,768]{1,0:T(8,128)(2,1)} %get-tuple-element.73.k_ref, bf16[512,768]{1,0:T(8,128)(2,1)} %get-tuple-element.74.v_ref, ...), custom_call_target="tpu_custom_call" | custom-call | flops 4026531840 | bytes 6488064 | tf_op jit(solution)/shard_map/pallas_call | solution.py:202
  393.0 4.1 shard_map.200
  398.2 1.2 collective-permute-done.46
  399.5 1.3 collective-permute-start.47
  400.7 3.6 collective-permute-done.47
  405.0 4.1 collective-permute-done.48
  409.1 1.8 collective-permute-start.51
  411.5 7.4 %shard_map.201 = f32[512,768]{1,0:T(8,128)} custom-call(f32[512,768]{1,0:T(8,128)} %get-tuple-element.71.ghid_ref, bf16[512,768]{1,0:T(8,128)(2,1)} %get-tuple-element.77.gq_ref, bf16[512,768]{1,0:T(8,128)(2,1)} %get-tuple-element.78.gk_ref, bf16[512,768]{1,0:T(8,128)(2,1)} %get-tuple-element.79.gv_ref, bf16[512,128]{1,0:T(8,128)(2,1)} %get-tuple-element.81.gm_ref, ...), custom_call_target="tpu_custom_call" | custom-call | flops 1811939328 | bytes 9371648 | tf_op jit(solution)/shard_map/pallas_call | solution.py:202
  (234 shorter events, 27.4 us)
Async XLA Ops:
  3.6 8.6 %collective-permute-start.3 = (bf16[48,1152]{1,0:T(8,128)(2,1)S(1)}, bf16[48,1152]{1,0:T(8,128)(2,1)S(1)}, u32[]{:S(2)}, u32[]{:S(2)}) collective-permute-start(bf16[48,1152]{1,0:T(8,128)(2,1)S(1)} %pad_maximum_fusion.20), channel_id=1, source_target_pairs={{0,24},{2,26},{4,28},{6,30},{8,0},{10,2},{12,4},{14,6},{16,8},{18,... | collective-permute-start | bytes 331784 | tf_op jit(solution)/shard_map/ppermute | solution.py:57
  8.7 9.7 %collective-permute-start.2 = (bf16[48,1152]{1,0:T(8,128)(2,1)S(1)}, bf16[48,1152]{1,0:T(8,128)(2,1)S(1)}, u32[]{:S(2)}, u32[]{:S(2)}) collective-permute-start(bf16[48,1152]{1,0:T(8,128)(2,1)S(1)} %pad_maximum_fusion.20), channel_id=1, source_target_pairs={{0,16},{2,18},{4,20},{6,22},{8,24},{10,26},{12,28},{14,30},{16,0},... | collective-permute-start | bytes 331784 | tf_op jit(solution)/shard_map/ppermute | solution.py:57
  8.7 9.7 %collective-permute-start.1 = (bf16[48,1152]{1,0:T(8,128)(2,1)S(1)}, bf16[48,1152]{1,0:T(8,128)(2,1)S(1)}, u32[]{:S(2)}, u32[]{:S(2)}) collective-permute-start(bf16[48,1152]{1,0:T(8,128)(2,1)S(1)} %pad_maximum_fusion.20), channel_id=1, source_target_pairs={{0,8},{2,10},{4,12},{6,14},{8,16},{10,18},{12,20},{14,22},{16,24},... | collective-permute-start | bytes 331784 | tf_op jit(solution)/shard_map/ppermute | solution.py:57
  10.0 11.6 %collective-permute-start.12 = (bf16[2,24,1920]{2,1,0:T(8,128)(2,1)S(1)}, bf16[2,24,1920]{2,1,0:T(8,128)(2,1)S(1)}, u32[]{:S(2)}, u32[]{:S(2)}) collective-permute-start(bf16[2,24,1920]{2,1,0:T(8,128)(2,1)S(1)} %pad_maximum_fusion.17), channel_id=1, source_target_pairs={{0,1},{1,0},{2,3},{3,2},{4,5},{5,4},{6,7},{7,6},{8,9},{9,8},{10,11... | collective-permute-start | bytes 552968 | tf_op jit(solution)/shard_map/ppermute | solution.py:62
  18.4 7.9 %collective-permute-start.8 = (bf16[4,48,384]{2,1,0:T(8,128)(2,1)S(1)}, bf16[4,48,384]{2,1,0:T(8,128)(2,1)S(1)}, u32[]{:S(2)}, u32[]{:S(2)}) collective-permute-start(bf16[4,48,384]{2,1,0:T(8,128)(2,1)S(1)} %get-tuple-element.115), channel_id=1, source_target_pairs={{0,2},{2,0},{4,6},{6,4},{8,10},{10,8},{12,14},{14,12},{16,18},{18,... | collective-permute-start | bytes 442376 | tf_op jit(solution)/shard_map/ppermute | solution.py:57
  20.0 8.0 %collective-permute-start.4 = (bf16[4,48,768]{2,1,0:T(8,128)(2,1)S(1)}, bf16[4,48,768]{2,1,0:T(8,128)(2,1)S(1)}, u32[]{:S(2)}, u32[]{:S(2)}) collective-permute-start(bf16[4,48,768]{2,1,0:T(8,128)(2,1)S(1)} %get-tuple-element.109), channel_id=1, source_target_pairs={{0,4},{2,6},{4,0},{6,2},{8,12},{10,14},{12,8},{14,10},{16,20},{18,... | collective-permute-start | bytes 884744 | tf_op jit(solution)/shard_map/ppermute | solution.py:57
  21.8 10.2 %collective-permute-start.15 = (bf16[48,3456]{1,0:T(8,128)(2,1)S(1)}, bf16[48,3456]{1,0:T(8,128)(2,1)S(1)}, u32[]{:S(2)}, u32[]{:S(2)}) collective-permute-start(bf16[48,3456]{1,0:T(8,128)(2,1)S(1)} %pad_maximum_fusion.10), channel_id=1, source_target_pairs={{0,24},{2,26},{4,28},{6,30},{8,0},{10,2},{12,4},{14,6},{16,8},{18,... | collective-permute-start | bytes 995336 | tf_op jit(solution)/shard_map/ppermute | solution.py:57
  23.7 28.5 %collective-permute-start.14 = (bf16[48,3456]{1,0:T(8,128)(2,1)S(1)}, bf16[48,3456]{1,0:T(8,128)(2,1)S(1)}, u32[]{:S(2)}, u32[]{:S(2)}) collective-permute-start(bf16[48,3456]{1,0:T(8,128)(2,1)S(1)} %pad_maximum_fusion.10), channel_id=1, source_target_pairs={{0,16},{2,18},{4,20},{6,22},{8,24},{10,26},{12,28},{14,30},{16,0},... | collective-permute-start | bytes 995336 | tf_op jit(solution)/shard_map/ppermute | solution.py:57
  24.4 27.9 %collective-permute-start.13 = (bf16[48,3456]{1,0:T(8,128)(2,1)S(1)}, bf16[48,3456]{1,0:T(8,128)(2,1)S(1)}, u32[]{:S(2)}, u32[]{:S(2)}) collective-permute-start(bf16[48,3456]{1,0:T(8,128)(2,1)S(1)} %pad_maximum_fusion.10), channel_id=1, source_target_pairs={{0,8},{2,10},{4,12},{6,14},{8,16},{10,18},{12,20},{14,22},{16,24},... | collective-permute-start | bytes 995336 | tf_op jit(solution)/shard_map/ppermute | solution.py:57
  26.3 75.2 %collective-permute-start = (bf16[2,2,8,384]{3,2,1,0:T(8,128)(2,1)S(1)}, bf16[2,2,8,384]{3,2,1,0:T(8,128)(2,1)S(1)}, u32[]{:S(2)}, u32[]{:S(2)}) collective-permute-start(bf16[2,2,8,384]{3,2,1,0:T(8,128)(2,1)S(1)} %pad_maximum_fusion.25), channel_id=1, source_target_pairs={{0,1},{1,0},{2,3},{3,2},{4,5},{5,4},{6,7},{7,6},{8,9},{9,8},{10,11... | collective-permute-start | bytes 73736 | tf_op jit(solution)/shard_map/ppermute | solution.py:62
  28.1 62.8 %collective-permute-start.10 = (bf16[2,4,48,384]{3,2,1,0:T(8,128)(2,1)S(1)}, bf16[2,4,48,384]{3,2,1,0:T(8,128)(2,1)S(1)}, u32[]{:S(2)}, u32[]{:S(2)}) collective-permute-start(bf16[2,4,48,384]{3,2,1,0:T(8,128)(2,1)S(1)} %pad_maximum_fusion.13.rest_4_), channel_id=1, source_target_pairs={{0,4},{2,6},{4,0},{6,2},{8,12},{10,14},{12,8},{14,10},{16,20},{18,... | collective-permute-start | bytes 884744 | tf_op jit(solution)/shard_map/ppermute | solution.py:57
  52.2 5.5 %collective-permute-start.26 = (bf16[48,1152]{1,0:T(8,128)(2,1)S(1)}, bf16[48,1152]{1,0:T(8,128)(2,1)S(1)}, u32[]{:S(2)}, u32[]{:S(2)}) collective-permute-start(bf16[48,1152]{1,0:T(8,128)(2,1)S(1)} %pad_maximum_fusion.21), channel_id=1, source_target_pairs={{0,24},{2,26},{4,28},{6,30},{8,0},{10,2},{12,4},{14,6},{16,8},{18,... | collective-permute-start | bytes 331784 | tf_op jit(solution)/shard_map/ppermute | solution.py:57
  52.3 11.4 %collective-permute-start.25 = (bf16[48,1152]{1,0:T(8,128)(2,1)S(1)}, bf16[48,1152]{1,0:T(8,128)(2,1)S(1)}, u32[]{:S(2)}, u32[]{:S(2)}) collective-permute-start(bf16[48,1152]{1,0:T(8,128)(2,1)S(1)} %pad_maximum_fusion.21), channel_id=1, source_target_pairs={{0,16},{2,18},{4,20},{6,22},{8,24},{10,26},{12,28},{14,30},{16,0},... | collective-permute-start | bytes 331784 | tf_op jit(solution)/shard_map/ppermute | solution.py:57
  53.4 10.3 %collective-permute-start.24 = (bf16[48,1152]{1,0:T(8,128)(2,1)S(1)}, bf16[48,1152]{1,0:T(8,128)(2,1)S(1)}, u32[]{:S(2)}, u32[]{:S(2)}) collective-permute-start(bf16[48,1152]{1,0:T(8,128)(2,1)S(1)} %pad_maximum_fusion.21), channel_id=1, source_target_pairs={{0,8},{2,10},{4,12},{6,14},{8,16},{10,18},{12,20},{14,22},{16,24},... | collective-permute-start | bytes 331784 | tf_op jit(solution)/shard_map/ppermute | solution.py:57
  63.7 10.7 %collective-permute-start.37 = (bf16[48,3456]{1,0:T(8,128)(2,1)S(1)}, bf16[48,3456]{1,0:T(8,128)(2,1)S(1)}, u32[]{:S(2)}, u32[]{:S(2)}) collective-permute-start(bf16[48,3456]{1,0:T(8,128)(2,1)S(1)} %pad_maximum_fusion.11), channel_id=1, source_target_pairs={{0,24},{2,26},{4,28},{6,30},{8,0},{10,2},{12,4},{14,6},{16,8},{18,... | collective-permute-start | bytes 995336 | tf_op jit(solution)/shard_map/ppermute | solution.py:57
  63.9 5.4 %collective-permute-start.31 = (bf16[4,48,384]{2,1,0:T(8,128)(2,1)S(1)}, bf16[4,48,384]{2,1,0:T(8,128)(2,1)S(1)}, u32[]{:S(2)}, u32[]{:S(2)}) collective-permute-start(bf16[4,48,384]{2,1,0:T(8,128)(2,1)S(1)} %get-tuple-element.111), channel_id=1, source_target_pairs={{0,2},{2,0},{4,6},{6,4},{8,10},{10,8},{12,14},{14,12},{16,18},{18,... | collective-permute-start | bytes 442376 | tf_op jit(solution)/shard_map/ppermute | solution.py:57
  64.6 8.3 %collective-permute-start.27 = (bf16[4,48,768]{2,1,0:T(8,128)(2,1)S(1)}, bf16[4,48,768]{2,1,0:T(8,128)(2,1)S(1)}, u32[]{:S(2)}, u32[]{:S(2)}) collective-permute-start(bf16[4,48,768]{2,1,0:T(8,128)(2,1)S(1)} %get-tuple-element.107), channel_id=1, source_target_pairs={{0,4},{2,6},{4,0},{6,2},{8,12},{10,14},{12,8},{14,10},{16,20},{18,... | collective-permute-start | bytes 884744 | tf_op jit(solution)/shard_map/ppermute | solution.py:57
  69.3 32.8 %collective-permute-start.9 = (bf16[2,4,48,384]{3,2,1,0:T(8,128)(2,1)S(1)}, bf16[2,4,48,384]{3,2,1,0:T(8,128)(2,1)S(1)}, u32[]{:S(2)}, u32[]{:S(2)}) collective-permute-start(bf16[2,4,48,384]{3,2,1,0:T(8,128)(2,1)S(1)} %pad_maximum_fusion.13.rest_4_), channel_id=1, source_target_pairs={{0,1},{1,0},{2,3},{3,2},{4,5},{5,4},{6,7},{7,6},{8,9},{9,8},{10,11... | collective-permute-start | bytes 884744 | tf_op jit(solution)/shard_map/ppermute | solution.py:62
  72.9 31.3 %collective-permute-start.6 = (bf16[2,4,48,768]{3,2,1,0:T(8,128)(2,1)S(1)}, bf16[2,4,48,768]{3,2,1,0:T(8,128)(2,1)S(1)}, u32[]{:S(2)}, u32[]{:S(2)}) collective-permute-start(bf16[2,4,48,768]{3,2,1,0:T(8,128)(2,1)S(1)} %pad_maximum_fusion.6.rest_0_), channel_id=1, source_target_pairs={{0,2},{2,0},{4,6},{6,4},{8,10},{10,8},{12,14},{14,12},{16,18},{18,... | collective-permute-start | bytes 1769480 | tf_op jit(solution)/shard_map/ppermute | solution.py:57
  74.4 15.9 %collective-permute-start.36 = (bf16[48,3456]{1,0:T(8,128)(2,1)S(1)}, bf16[48,3456]{1,0:T(8,128)(2,1)S(1)}, u32[]{:S(2)}, u32[]{:S(2)}) collective-permute-start(bf16[48,3456]{1,0:T(8,128)(2,1)S(1)} %pad_maximum_fusion.11), channel_id=1, source_target_pairs={{0,16},{2,18},{4,20},{6,22},{8,24},{10,26},{12,28},{14,30},{16,0},... | collective-permute-start | bytes 995336 | tf_op jit(solution)/shard_map/ppermute | solution.py:57
  90.3 11.2 %collective-permute-start.35 = (bf16[48,3456]{1,0:T(8,128)(2,1)S(1)}, bf16[48,3456]{1,0:T(8,128)(2,1)S(1)}, u32[]{:S(2)}, u32[]{:S(2)}) collective-permute-start(bf16[48,3456]{1,0:T(8,128)(2,1)S(1)} %pad_maximum_fusion.11), channel_id=1, source_target_pairs={{0,8},{2,10},{4,12},{6,14},{8,16},{10,18},{12,20},{14,22},{16,24},... | collective-permute-start | bytes 995336 | tf_op jit(solution)/shard_map/ppermute | solution.py:57
  90.8 33.6 %collective-permute-start.20 = (bf16[4,48,1920]{2,1,0:T(8,128)(2,1)S(1)}, bf16[4,48,1920]{2,1,0:T(8,128)(2,1)S(1)}, u32[]{:S(2)}, u32[]{:S(2)}) collective-permute-start(bf16[4,48,1920]{2,1,0:T(8,128)(2,1)S(1)} %get-tuple-element.87), channel_id=1, source_target_pairs={{0,2},{2,0},{4,6},{6,4},{8,10},{10,8},{12,14},{14,12},{16,18},{18,... | collective-permute-start | bytes 2211848 | tf_op jit(solution)/shard_map/ppermute | solution.py:57
  102.1 22.7 %collective-permute-start.16 = (bf16[4,48,1536]{2,1,0:T(8,128)(2,1)S(1)}, bf16[4,48,1536]{2,1,0:T(8,128)(2,1)S(1)}, u32[]{:S(2)}, u32[]{:S(2)}) collective-permute-start(bf16[4,48,1536]{2,1,0:T(8,128)(2,1)S(1)} %get-tuple-element.91), channel_id=1, source_target_pairs={{0,4},{2,6},{4,0},{6,2},{8,12},{10,14},{12,8},{14,10},{16,20},{18,... | collective-permute-start | bytes 1769480 | tf_op jit(solution)/shard_map/ppermute | solution.py:57
  103.1 20.7 %collective-permute-start.33 = (bf16[2,4,48,384]{3,2,1,0:T(8,128)(2,1)S(1)}, bf16[2,4,48,384]{3,2,1,0:T(8,128)(2,1)S(1)}, u32[]{:S(2)}, u32[]{:S(2)}) collective-permute-start(bf16[2,4,48,384]{3,2,1,0:T(8,128)(2,1)S(1)} %pad_maximum_fusion.15.rest_4_), channel_id=1, source_target_pairs={{0,4},{2,6},{4,0},{6,2},{8,12},{10,14},{12,8},{14,10},{16,20},{18,... | collective-permute-start | bytes 884744 | tf_op jit(solution)/shard_map/ppermute | solution.py:57
  104.2 19.6 %collective-permute-start.32 = (bf16[2,4,48,384]{3,2,1,0:T(8,128)(2,1)S(1)}, bf16[2,4,48,384]{3,2,1,0:T(8,128)(2,1)S(1)}, u32[]{:S(2)}, u32[]{:S(2)}) collective-permute-start(bf16[2,4,48,384]{3,2,1,0:T(8,128)(2,1)S(1)} %pad_maximum_fusion.15.rest_4_), channel_id=1, source_target_pairs={{0,1},{1,0},{2,3},{3,2},{4,5},{5,4},{6,7},{7,6},{8,9},{9,8},{10,11... | collective-permute-start | bytes 884744 | tf_op jit(solution)/shard_map/ppermute | solution.py:62
  104.5 22.8 %collective-permute-start.29 = (bf16[2,4,48,768]{3,2,1,0:T(8,128)(2,1)S(1)}, bf16[2,4,48,768]{3,2,1,0:T(8,128)(2,1)}, u32[]{:S(2)}, u32[]{:S(2)}) collective-permute-start(bf16[2,4,48,768]{3,2,1,0:T(8,128)(2,1)S(1)} %pad_maximum_fusion.8.rest_0_), channel_id=1, source_target_pairs={{0,2},{2,0},{4,6},{6,4},{8,10},{10,8},{12,14},{14,12},{16,18},{18,... | collective-permute-start | bytes 1769480 | tf_op jit(solution)/shard_map/ppermute | solution.py:57
  123.8 5.0 %collective-permute-start.28 = (bf16[2,4,48,768]{3,2,1,0:T(8,128)(2,1)S(1)}, bf16[2,4,48,768]{3,2,1,0:T(8,128)(2,1)S(1)}, u32[]{:S(2)}, u32[]{:S(2)}) collective-permute-start(bf16[2,4,48,768]{3,2,1,0:T(8,128)(2,1)S(1)} %pad_maximum_fusion.8.rest_0_), channel_id=1, source_target_pairs={{0,1},{1,0},{2,3},{3,2},{4,5},{5,4},{6,7},{7,6},{8,9},{9,8},{10,11... | collective-permute-start | bytes 1769480 | tf_op jit(solution)/shard_map/ppermute | solution.py:62
  123.8 19.4 %collective-permute-start.42 = (bf16[4,48,1920]{2,1,0:T(8,128)(2,1)S(1)}, bf16[4,48,1920]{2,1,0:T(8,128)(2,1)S(1)}, u32[]{:S(2)}, u32[]{:S(2)}) collective-permute-start(bf16[4,48,1920]{2,1,0:T(8,128)(2,1)S(1)} %get-tuple-element.85), channel_id=1, source_target_pairs={{0,2},{2,0},{4,6},{6,4},{8,10},{10,8},{12,14},{14,12},{16,18},{18,... | collective-permute-start | bytes 2211848 | tf_op jit(solution)/shard_map/ppermute | solution.py:57
  124.8 49.6 %collective-permute-start.22 = (bf16[2,4,48,1920]{3,2,1,0:T(8,128)(2,1)S(1)}, bf16[2,4,48,1920]{3,2,1,0:T(8,128)(2,1)}, u32[]{:S(2)}, u32[]{:S(2)}) collective-permute-start(bf16[2,4,48,1920]{3,2,1,0:T(8,128)(2,1)S(1)} %pad_maximum_fusion.rest_4_), channel_id=1, source_target_pairs={{0,4},{2,6},{4,0},{6,2},{8,12},{10,14},{12,8},{14,10},{16,20},{18,... | collective-permute-start | bytes 4423688 | tf_op jit(solution)/shard_map/ppermute | solution.py:57
  126.2 45.9 %collective-permute-start.38 = (bf16[4,48,1536]{2,1,0:T(8,128)(2,1)S(1)}, bf16[4,48,1536]{2,1,0:T(8,128)(2,1)S(1)}, u32[]{:S(2)}, u32[]{:S(2)}) collective-permute-start(bf16[4,48,1536]{2,1,0:T(8,128)(2,1)S(1)} %get-tuple-element.89), channel_id=1, source_target_pairs={{0,4},{2,6},{4,0},{6,2},{8,12},{10,14},{12,8},{14,10},{16,20},{18,... | collective-permute-start | bytes 1769480 | tf_op jit(solution)/shard_map/ppermute | solution.py:57
  127.2 47.1 %collective-permute-start.18 = (bf16[2,4,48,1536]{3,2,1,0:T(8,128)(2,1)S(1)}, bf16[2,4,48,1536]{3,2,1,0:T(8,128)(2,1)}, u32[]{:S(2)}, u32[]{:S(2)}) collective-permute-start(bf16[2,4,48,1536]{3,2,1,0:T(8,128)(2,1)S(1)} %pad_maximum_fusion.2.rest_0_), channel_id=1, source_target_pairs={{0,2},{2,0},{4,6},{6,4},{8,10},{10,8},{12,14},{14,12},{16,18},{18,... | collective-permute-start | bytes 3538952 | tf_op jit(solution)/shard_map/ppermute | solution.py:57
  128.8 44.0 %collective-permute-start.7 = (bf16[2,4,48,768]{3,2,1,0:T(8,128)(2,1)S(1)}, bf16[2,4,48,768]{3,2,1,0:T(8,128)(2,1)S(1)}, u32[]{:S(2)}, u32[]{:S(2)}) collective-permute-start(bf16[2,4,48,768]{3,2,1,0:T(8,128)(2,1)S(1)} %collective-permute-done.6.rest_2_), channel_id=1, source_target_pairs={{0,1},{1,0},{2,3},{3,2},{4,5},{5,4},{6,7},{7,6},{8,9},{9,8},{10,11... | collective-permute-start | bytes 1769480 | tf_op jit(solution)/shard_map/ppermute | solution.py:62
  143.2 31.8 %collective-permute-start.17 = (bf16[2,4,48,1536]{3,2,1,0:T(8,128)(2,1)S(1)}, bf16[2,4,48,1536]{3,2,1,0:T(8,128)(2,1)S(1)}, u32[]{:S(2)}, u32[]{:S(2)}) collective-permute-start(bf16[2,4,48,1536]{3,2,1,0:T(8,128)(2,1)S(1)} %pad_maximum_fusion.2.rest_0_), channel_id=1, source_target_pairs={{0,1},{1,0},{2,3},{3,2},{4,5},{5,4},{6,7},{7,6},{8,9},{9,8},{10,11... | collective-permute-start | bytes 3538952 | tf_op jit(solution)/shard_map/ppermute | solution.py:62
  172.1 34.1 %collective-permute-start.44 = (bf16[2,4,48,1920]{3,2,1,0:T(8,128)(2,1)}, bf16[2,4,48,1920]{3,2,1,0:T(8,128)(2,1)}, u32[]{:S(2)}, u32[]{:S(2)}) collective-permute-start(bf16[2,4,48,1920]{3,2,1,0:T(8,128)(2,1)} %pad_maximum_fusion.1.rest_4_), channel_id=1, source_target_pairs={{0,4},{2,6},{4,0},{6,2},{8,12},{10,14},{12,8},{14,10},{16,20},{18,... | collective-permute-start | bytes 4423688 | tf_op jit(solution)/shard_map/ppermute | solution.py:57
  172.8 27.4 %collective-permute-start.40 = (bf16[2,4,48,1536]{3,2,1,0:T(8,128)(2,1)S(1)}, bf16[2,4,48,1536]{3,2,1,0:T(8,128)(2,1)}, u32[]{:S(2)}, u32[]{:S(2)}) collective-permute-start(bf16[2,4,48,1536]{3,2,1,0:T(8,128)(2,1)S(1)} %pad_maximum_fusion.3.rest_0_), channel_id=1, source_target_pairs={{0,2},{2,0},{4,6},{6,4},{8,10},{10,8},{12,14},{14,12},{16,18},{18,... | collective-permute-start | bytes 3538952 | tf_op jit(solution)/shard_map/ppermute | solution.py:57
  174.3 33.1 %collective-permute-start.21 = (bf16[2,4,48,1920]{3,2,1,0:T(8,128)(2,1)S(1)}, bf16[2,4,48,1920]{3,2,1,0:T(8,128)(2,1)}, u32[]{:S(2)}, u32[]{:S(2)}) collective-permute-start(bf16[2,4,48,1920]{3,2,1,0:T(8,128)(2,1)S(1)} %pad_maximum_fusion.rest_4_), channel_id=1, source_target_pairs={{0,1},{1,0},{2,3},{3,2},{4,5},{5,4},{6,7},{7,6},{8,9},{9,8},{10,11... | collective-permute-start | bytes 4423688 | tf_op jit(solution)/shard_map/ppermute | solution.py:62
  174.4 33.6 %collective-permute-start.23 = (bf16[2,4,48,1920]{3,2,1,0:T(8,128)(2,1)}, bf16[2,4,48,1920]{3,2,1,0:T(8,128)(2,1)}, u32[]{:S(2)}, u32[]{:S(2)}) collective-permute-start(bf16[2,4,48,1920]{3,2,1,0:T(8,128)(2,1)} %collective-permute-done.22.rest_6_), channel_id=1, source_target_pairs={{0,1},{1,0},{2,3},{3,2},{4,5},{5,4},{6,7},{7,6},{8,9},{9,8},{10,11... | collective-permute-start | bytes 4423688 | tf_op jit(solution)/shard_map/ppermute | solution.py:62
  175.0 33.0 %collective-permute-start.19 = (bf16[2,4,48,1536]{3,2,1,0:T(8,128)(2,1)}, bf16[2,4,48,1536]{3,2,1,0:T(8,128)(2,1)}, u32[]{:S(2)}, u32[]{:S(2)}) collective-permute-start(bf16[2,4,48,1536]{3,2,1,0:T(8,128)(2,1)} %collective-permute-done.18.rest_2_), channel_id=1, source_target_pairs={{0,1},{1,0},{2,3},{3,2},{4,5},{5,4},{6,7},{7,6},{8,9},{9,8},{10,11... | collective-permute-start | bytes 3538952 | tf_op jit(solution)/shard_map/ppermute | solution.py:62
  200.2 72.4 %collective-permute-start.43 = (bf16[2,4,48,1920]{3,2,1,0:T(8,128)(2,1)}, bf16[2,4,48,1920]{3,2,1,0:T(8,128)(2,1)}, u32[]{:S(2)}, u32[]{:S(2)}) collective-permute-start(bf16[2,4,48,1920]{3,2,1,0:T(8,128)(2,1)} %pad_maximum_fusion.1.rest_4_), channel_id=1, source_target_pairs={{0,1},{1,0},{2,3},{3,2},{4,5},{5,4},{6,7},{7,6},{8,9},{9,8},{10,11... | collective-permute-start | bytes 4423688 | tf_op jit(solution)/shard_map/ppermute | solution.py:62
  206.3 66.3 %collective-permute-start.45 = (bf16[2,4,48,1920]{3,2,1,0:T(8,128)(2,1)}, bf16[2,4,48,1920]{3,2,1,0:T(8,128)(2,1)}, u32[]{:S(2)}, u32[]{:S(2)}) collective-permute-start(bf16[2,4,48,1920]{3,2,1,0:T(8,128)(2,1)} %collective-permute-done.44.rest_6_), channel_id=1, source_target_pairs={{0,1},{1,0},{2,3},{3,2},{4,5},{5,4},{6,7},{7,6},{8,9},{9,8},{10,11... | collective-permute-start | bytes 4423688 | tf_op jit(solution)/shard_map/ppermute | solution.py:62
  207.4 45.5 %collective-permute-start.30 = (bf16[2,4,48,768]{3,2,1,0:T(8,128)(2,1)}, bf16[2,4,48,768]{3,2,1,0:T(8,128)(2,1)S(1)}, u32[]{:S(2)}, u32[]{:S(2)}) collective-permute-start(bf16[2,4,48,768]{3,2,1,0:T(8,128)(2,1)} %collective-permute-done.29.rest_2_), channel_id=1, source_target_pairs={{0,1},{1,0},{2,3},{3,2},{4,5},{5,4},{6,7},{7,6},{8,9},{9,8},{10,11... | collective-permute-start | bytes 1769480 | tf_op jit(solution)/shard_map/ppermute | solution.py:62
  207.9 64.6 %collective-permute-start.39 = (bf16[2,4,48,1536]{3,2,1,0:T(8,128)(2,1)S(1)}, bf16[2,4,48,1536]{3,2,1,0:T(8,128)(2,1)S(1)}, u32[]{:S(2)}, u32[]{:S(2)}) collective-permute-start(bf16[2,4,48,1536]{3,2,1,0:T(8,128)(2,1)S(1)} %pad_maximum_fusion.3.rest_0_), channel_id=1, source_target_pairs={{0,1},{1,0},{2,3},{3,2},{4,5},{5,4},{6,7},{7,6},{8,9},{9,8},{10,11... | collective-permute-start | bytes 3538952 | tf_op jit(solution)/shard_map/ppermute | solution.py:62
  208.0 64.6 %collective-permute-start.41 = (bf16[2,4,48,1536]{3,2,1,0:T(8,128)(2,1)}, bf16[2,4,48,1536]{3,2,1,0:T(8,128)(2,1)}, u32[]{:S(2)}, u32[]{:S(2)}) collective-permute-start(bf16[2,4,48,1536]{3,2,1,0:T(8,128)(2,1)} %collective-permute-done.40.rest_2_), channel_id=1, source_target_pairs={{0,1},{1,0},{2,3},{3,2},{4,5},{5,4},{6,7},{7,6},{8,9},{9,8},{10,11... | collective-permute-start | bytes 3538952 | tf_op jit(solution)/shard_map/ppermute | solution.py:62
  399.5 4.9 %collective-permute-start.47 = (f32[64,384]{1,0:T(8,128)S(1)}, f32[64,384]{1,0:T(8,128)S(1)}, u32[]{:S(2)}, u32[]{:S(2)}) collective-permute-start(f32[64,384]{1,0:T(8,128)S(1)} %dynamic-slice_add_fusion), channel_id=1, source_target_pairs={{0,2},{2,0},{4,6},{6,4},{8,10},{10,8},{12,14},{14,12},{16,18},{18,... | collective-permute-start | bytes 294920 | tf_op jit(solution)/shard_map/ppermute | solution.py:57
  404.4 4.7 %collective-permute-start.48 = (f32[64,384]{1,0:T(8,128)S(1)}, f32[64,384]{1,0:T(8,128)S(1)}, u32[]{:S(2)}, u32[]{:S(2)}) collective-permute-start(f32[64,384]{1,0:T(8,128)S(1)} %add.71), channel_id=1, source_target_pairs={{0,4},{2,6},{4,0},{6,2},{8,12},{10,14},{12,8},{14,10},{16,20},{18,... | collective-permute-start | bytes 294920 | tf_op jit(solution)/shard_map/ppermute | solution.py:57
  409.1 9.8 %collective-permute-start.51 = (f32[64,384]{1,0:T(8,128)S(1)}, f32[64,384]{1,0:T(8,128)S(1)}, u32[]{:S(2)}, u32[]{:S(2)}) collective-permute-start(f32[64,384]{1,0:T(8,128)S(1)} %add.72), channel_id=1, source_target_pairs={{0,24},{2,26},{4,28},{6,30},{8,0},{10,2},{12,4},{14,6},{16,8},{18,... | collective-permute-start | bytes 294920 | tf_op jit(solution)/shard_map/ppermute | solution.py:57
  410.9 8.1 %collective-permute-start.50 = (f32[64,384]{1,0:T(8,128)S(1)}, f32[64,384]{1,0:T(8,128)S(1)}, u32[]{:S(2)}, u32[]{:S(2)}) collective-permute-start(f32[64,384]{1,0:T(8,128)S(1)} %add.72), channel_id=1, source_target_pairs={{0,16},{2,18},{4,20},{6,22},{8,24},{10,26},{12,28},{14,30},{16,0},... | collective-permute-start | bytes 294920 | tf_op jit(solution)/shard_map/ppermute | solution.py:57
  410.9 8.1 %collective-permute-start.49 = (f32[64,384]{1,0:T(8,128)S(1)}, f32[64,384]{1,0:T(8,128)S(1)}, u32[]{:S(2)}, u32[]{:S(2)}) collective-permute-start(f32[64,384]{1,0:T(8,128)S(1)} %add.72), channel_id=1, source_target_pairs={{0,8},{2,10},{4,12},{6,14},{8,16},{10,18},{12,20},{14,22},{16,24},... | collective-permute-start | bytes 294920 | tf_op jit(solution)/shard_map/ppermute | solution.py:57
  (39 other events, 455.1 us)

commit v2 on v0

v2 whole, which is shorter than its diff:
```python
import functools

import jax
import jax.numpy as jnp
from jax import lax
from jax.experimental import pallas as pl
from jax.experimental.pallas import tpu as pltpu
from jax.sharding import PartitionSpec as P

HEAD_DIM = 64
EPS = 1e-05
BF = jnp.bfloat16
F32 = jnp.float32
ROOT_HALF = 0.7071067811865476
PHI_SCALE = 0.3989422804014327
VMEM_LIMIT = 60 * 1024 * 1024
TILE = 256


def mm(left, right):
    return lax.dot_general(left, right, (((1,), (0,)), ((), ())), preferred_element_type=F32)


def mm_rt(left, right):
    return lax.dot_general(left, right, (((1,), (1,)), ((), ())), preferred_element_type=F32)


def mm_lt(left, right):
    return lax.dot_general(left, right, (((0,), (0,)), ((), ())), preferred_element_type=F32)


def chip_grid(count):
    side = round((count / 2) ** (1 / 3))
    if 2 * side**3 == count:
        return (2 * side, side, side)
    return (count, 1, 1)


def shift(values, grid, axis, by):
    nz, ny, nx = grid
    pairs = []
    for z in range(nz):
        for y in range(ny):
            for x in range(nx):
                to = [z, y, x]
                to[axis] = (to[axis] + by) % grid[axis]
                pairs.append(((z * ny + y) * nx + x, (to[0] * ny + to[1]) * nx + to[2]))
    return lax.ppermute(values, "dp", pairs)


def swap_cores(values):
    size = lax.axis_size("head")
    return lax.ppermute(values, "head", [(i, (i + 1) % size) for i in range(size)])


def after(values, *earlier):
    return lax.optimization_barrier((values, *earlier))[0]


class Gathered:
    def __init__(self, grid, groups, places):
        self.grid = grid
        self.groups = groups
        self.places = places

    def wanted(self, keys):
        ids = []
        for key in keys:
            name = self.places[key][0]
            if name not in ids:
                ids.append(name)
        return ids

    def leaves(self, keys):
        return [leaf for name in self.wanted(keys) for leaf in jax.tree.leaves(self.groups[name])]

    def bind(self, keys, refs):
        bound, at = {}, 0
        for name in self.wanted(keys):
            leaves, tree = jax.tree.flatten(self.groups[name])
            bound[name] = jax.tree.unflatten(tree, refs[at : at + len(leaves)])
            at += len(leaves)
        return bound, refs[at:]

    def start(self, bound, key, dst, sem):
        name, items = self.places[key]
        if not isinstance(bound[name], list):
            ref = bound[name]
            for lane, width, row in items:
                pltpu.make_async_copy(
                    ref.at[:, pl.ds(lane, width)], dst.at[pl.ds(row, ref.shape[0]), :], sem
                ).start()
            return
        all_items = items
        nz, ny, nx = self.grid
        dp = lax.axis_index("dp")
        core = lax.axis_index("head")
        z, y, x = dp // (ny * nx), (dp // nx) % ny, dp % nx
        for at, half in enumerate(bound[name]):
            items = [item for item in all_items if item[0] == at]
            if not items:
                continue
            for last, pair in enumerate(half):
                for other in range(2):
                    ref = pair[other]
                    c = core if other == 0 else 1 - core
                    for first in range(ref.shape[0]):
                        for kz in range(nz):
                            zz = lax.rem(z + nz - kz, nz)
                            ky, kx = (first, last) if at == 0 else (last, first)
                            yy, xx = lax.rem(y + ny - ky, ny), lax.rem(x + nx - kx, nx)
                            owner = (zz * ny + yy) * nx + xx
                            for _, lane, width, place in items:
                                row, col = place(owner, c)
                                pltpu.make_async_copy(
                                    ref.at[first, kz, :, pl.ds(lane, width)],
                                    dst.at[pl.ds(row, ref.shape[2]), pl.ds(col, width)],
                                    sem,
                                ).start()


def wait_all(dst, sem):
    pltpu.make_async_copy(dst, dst, sem).wait()


def place_chip(rows, stride, base):
    def place(owner, c):
        return pl.multiple_of(owner * rows, 16), pl.multiple_of(c * stride + base, 128)

    return place


def place_core(rows, parts, part, base):
    def place(owner, c):
        return pl.multiple_of(((owner * 2 + c) * parts + part) * rows, 16), base

    return place


def tensor_items(name, rows, width, ff, parts):
    half = width // 2
    if name == "qkv":
        return [(half, lambda skip, i=i: place_chip(rows, half, i * width + skip)) for i in range(3)]
    if name == "out":
        return [(half, lambda skip: place_chip(rows, half, skip))]
    if name == "up":
        return [(ff // 2, lambda skip: place_chip(rows, ff // 2, skip))]
    return [(width, lambda skip, i=i: place_core(rows, parts, i, skip)) for i in range(parts)]


def cut_of(lanes):
    return (lanes // 2 + 127) // 128 * 128


def sds(shape, dtype):
    return jax.ShapeDtypeStruct(shape, dtype)


def kernel_call(body, outs, scratch, flops, scalars, blocks, raw, raw_outs=()):
    specs = [pl.BlockSpec(memory_space=pltpu.SMEM)] * len(scalars)
    specs += [pl.BlockSpec(memory_space=pltpu.VMEM)] * len(blocks)
    specs += [pl.BlockSpec(memory_space=pl.ANY)] * len(raw)
    moved = sum(v.size * v.dtype.itemsize for v in (*blocks, *raw, *outs))
    return pl.pallas_call(
        body,
        out_shape=tuple(outs),
        in_specs=specs,
        out_specs=tuple([pl.BlockSpec(memory_space=pltpu.VMEM)] * len(outs)),
        scratch_shapes=scratch,
        compiler_params=pltpu.CompilerParams(vmem_limit_bytes=VMEM_LIMIT),
        cost_estimate=pl.CostEstimate(flops=flops, bytes_accessed=moved, transcendentals=0),
    )(*scalars, *blocks, *raw)


def copy_in(src, dst, sem):
    pltpu.make_async_copy(src, dst, sem).start()


def mask_bias(len_ref, rows):
    length = len_ref[lax.axis_index("head")]
    near = lax.broadcasted_iota(jnp.int32, (rows, rows), 0) // length
    far = lax.broadcasted_iota(jnp.int32, (rows, rows), 1) // length
    return jnp.where(near == far, 0.0, -1e30).astype(F32)


def head_masks(rows):
    low = lax.broadcasted_iota(jnp.int32, (rows, 128), 1) < HEAD_DIM
    return low, jnp.zeros((rows, 128), BF)


def attend_forward(x, down, up, weights, layer, lengths):
    rows, width = x.shape
    keys = (("qkv", layer),)
    pairs = width // 128

    def body(len_ref, x_ref, down_ref, up_ref, *rest):
        bound, rest = weights.bind(keys, rest)
        q_ref, k_ref, v_ref, o_ref, lse_ref, mid_ref, w_ref, bias_ref, sem = rest
        weights.start(bound, keys[0], w_ref, sem)
        r = x_ref[...].astype(BF)
        mid = mm(r, down_ref[...]).astype(BF)
        mid_ref[...] = mid
        bias_ref[...] = mask_bias(len_ref, rows)
        wait_all(w_ref, sem)
        for at, out in enumerate((q_ref, k_ref, v_ref)):
            for j in range(0, width, TILE):
                c = at * width + j
                total = mm(r, w_ref[:, c : c + TILE])
                if at != 1:
                    total += mm(mid, up_ref[:, c : c + TILE])
                out[:, j : j + TILE] = total.astype(BF)
        low, zero = head_masks(rows)
        one_low = jnp.where(low, 1.0, 0.0).astype(BF)
        one_high = jnp.where(low, 0.0, 1.0).astype(BF)
        for p in range(pairs):
            lanes = slice(p * 128, p * 128 + 128)
            q2 = q_ref[:, lanes] * 0.125
            k2 = k_ref[:, lanes]
            v2 = v_ref[:, lanes]
            bias = bias_ref[...]
            s0 = mm_rt(q2, jnp.where(low, k2, zero)) + bias
            s1 = mm_rt(q2, jnp.where(low, zero, k2)) + bias
            m0 = jnp.max(s0, -1, keepdims=True)
            m1 = jnp.max(s1, -1, keepdims=True)
            e0 = jnp.exp(s0 - m0).astype(BF)
            e1 = jnp.exp(s1 - m1).astype(BF)
            v0 = jnp.concatenate([jnp.where(low, v2, zero), one_low], 1)
            v1 = jnp.concatenate([jnp.where(low, zero, v2), one_high], 1)
            both = mm(e0, v0) + mm(e1, v1)
            total = both[:, 128:]
            o_ref[:, lanes] = (both[:, :128] / total).astype(BF)
            flip = (jnp.where(low, m0, m1) + jnp.log(total)).T
            lse_ref[2 * p] = flip[0:8]
            lse_ref[2 * p + 1] = flip[64:72]

    act = sds((rows, width), BF)
    outs = (act, act, act, act, sds((2 * pairs, 8, rows), F32), sds((rows, 128), BF))
    return kernel_call(
        body,
        outs,
        [pltpu.VMEM((width, 3 * width), BF), pltpu.VMEM((rows, rows), F32), pltpu.SemaphoreType.DMA],
        6 * rows * width * width + 16 * rows * rows * width,
        (lengths,),
        (x, down, up),
        weights.leaves(keys),
    )


def normalize(values):
    center = values - jnp.mean(values, -1, keepdims=True)
    scale = lax.rsqrt(jnp.mean(center * center, -1, keepdims=True) + EPS)
    return center * scale, scale


def norm_backward(gn, n, scale):
    return (gn - jnp.mean(gn, -1, keepdims=True) - n * jnp.mean(gn * n, -1, keepdims=True)) * scale


def gelu_pair(u):
    below = 0.5 + 0.5 * lax.erf(u * ROOT_HALF)
    return u * below, below + u * (jnp.exp(-0.5 * (u * u)) * PHI_SCALE)


def dense_up(x, o_ref, wo_ref, wo_wait, wu_ref, wu_wait, gains, n1_ref, y_ref, yb_ref, slope_ref, a_ref):
    width, ff = wu_ref.shape
    wo_wait()
    for j in range(0, width, TILE):
        y_ref[:, j : j + TILE] = x(j) + mm(o_ref[...], wo_ref[:, j : j + TILE])
    n1, scale = normalize(y_ref[...])
    n1_ref[...] = n1.astype(BF)
    y = n1 * gains[0:1] + gains[1:2]
    y_ref[...] = y
    yb_ref[...] = y.astype(BF)
    wu_wait()
    for j in range(0, ff, TILE):
        value, slope = gelu_pair(mm(yb_ref[...], wu_ref[:, j : j + TILE]))
        slope_ref[:, j : j + TILE] = slope.astype(BF)
        a_ref[:, j : j + TILE] = value.astype(BF)
    return scale


def dense_forward(x, attended, rows8, weights, layer):
    rows, width = x.shape
    ff = weights.ff
    keys = (("out", layer), ("up", layer), ("down", layer))

    def body(x_ref, o_ref, rows_ref, *rest):
        bound, rest = weights.bind(keys, rest)
        n1_ref, rs_ref, slope_ref, out_ref, n2_ref, wo_ref, wu_ref, wd_ref, yb_ref, y_ref, a_ref, sem = rest
        for i, dst in enumerate((wo_ref, wu_ref, wd_ref)):
            weights.start(bound, keys[i], dst, sem.at[i])
        gains = rows_ref[...]
        rs1 = dense_up(
            lambda j: x_ref[:, j : j + TILE].astype(F32),
            o_ref,
            wo_ref,
            lambda: wait_all(wo_ref, sem.at[0]),
            wu_ref,
            lambda: wait_all(wu_ref, sem.at[1]),
            gains,
            n1_ref,
            y_ref,
            yb_ref,
            slope_ref,
            a_ref,
        )
        wait_all(wd_ref, sem.at[2])
        for j in range(0, width, TILE):
            y_ref[:, j : j + TILE] += mm(a_ref[...], wd_ref[:, j : j + TILE])
        n2, rs2 = normalize(y_ref[...])
        n2_ref[...] = n2.astype(BF)
        low = lax.broadcasted_iota(jnp.int32, (rows, 128), 1) < 64
        rs_ref[...] = jnp.where(low, rs1, rs2)
        out_ref[...] = n2 * gains[2:3] + gains[3:4]

    act, wide, hidden = sds((rows, width), BF), sds((rows, width), F32), sds((rows, ff), BF)
    return kernel_call(
        body,
        (act, sds((rows, 128), F32), hidden, wide, act),
        [
            pltpu.VMEM((width, width), BF),
            pltpu.VMEM((width, ff), BF),
            pltpu.VMEM((ff, width), BF),
            pltpu.VMEM((rows, width), BF),
            pltpu.VMEM((rows, width), F32),
            pltpu.VMEM((rows, ff), BF),
            pltpu.SemaphoreType.DMA((3,)),
        ],
        2 * rows * width * (width + 2 * ff),
        (),
        (x, attended, rows8),
        weights.leaves(keys),
    )


def attend_backward(q_ref, k_ref, v_ref, o_ref, go_ref, lse_ref, bias_ref, gq_ref, gk_ref, gv_ref):
    rows, width = q_ref.shape
    low, zero = head_masks(rows)
    for p in range(width // 128):
        lanes = slice(p * 128, p * 128 + 128)
        q2 = q_ref[:, lanes] * 0.125
        k2 = k_ref[:, lanes]
        v2 = v_ref[:, lanes]
        go2 = go_ref[:, lanes]
        flip = (go2.astype(F32) * o_ref[:, lanes].astype(F32)).T
        gq = gk = gv = None
        for h in range(2):
            keep = (lambda t: jnp.where(low, t, zero)) if h == 0 else (lambda t: jnp.where(low, zero, t))
            qh, kh, goh = keep(q2), keep(k2), keep(go2)
            dots = jnp.sum(flip[h * HEAD_DIM : (h + 1) * HEAD_DIM], 0, keepdims=True)
            prob = jnp.exp(mm_rt(k2, qh) + bias_ref[...] - lse_ref[2 * p + h][0:1])
            gs = (prob * (mm_rt(v2, goh) - dots)).astype(BF)
            to_q, to_k, to_v = mm_lt(gs, kh), mm(gs, qh), mm(prob.astype(BF), goh)
            gq = to_q if h == 0 else gq + to_q
            gk = to_k if h == 0 else gk + to_k
            gv = to_v if h == 0 else gv + to_v
        gq_ref[:, lanes] = (gq * 0.125).astype(BF)
        gk_ref[:, lanes] = gk.astype(BF)
        gv_ref[:, lanes] = gv.astype(BF)


def backward(saved, cotangent, rows8, downs, ups, weights, lengths):
    layers = len(saved)
    rows, width = cotangent.shape
    ff = weights.ff
    last = layers - 1
    keys = tuple((name, at) for at in reversed(range(layers)) for name in ("out", "up", "down", "qkv"))
    keys = keys[:-1]
    names = ("q", "k", "v", "o", "lse", "mid")
    early = ("n1", "rs", "slope", "n2", "r")
    raw = [cotangent, saved[last]["x"]]
    for at in reversed(range(layers)):
        raw += [saved[at][name] for name in names + (early if at < last else ())]

    def body(len_ref, rows_ref, down_ref, up_ref, *rest):
        cot_in, x_in = rest[:2]
        rest = rest[2:]
        given = [None] * layers
        for at in reversed(range(layers)):
            here = names + (early if at < last else ())
            given[at] = dict(zip(here, rest))
            rest = rest[len(here) :]
        bound, rest = weights.bind(keys, rest)
        out_ref, sums_ref, ghid_ref, gq_ref, gk_ref, gv_ref, gm_ref = rest[:7]
        (wd_ref, wu_ref, wo_ref, wq_ref, cot_ref, g_ref, a_ref, wide_ref, gb_ref, go_ref, bias_ref) = rest[7:18]
        keep = dict(zip(names + early, rest[18:29]))
        sem = rest[29]
        sems = {n: sem.at[i] for i, n in enumerate(names + early + ("down", "up", "out", "qkv", "cot", "x"))}

        def fetch(at, *which):
            for name in which:
                copy_in(given[at][name], keep[name], sems[name])

        def take(*which):
            for name in which:
                wait_all(keep[name], sems[name])

        copy_in(x_in, g_ref, sems["x"])
        fetch(last, "o")
        weights.start(bound, ("out", last), wo_ref, sems["out"])
        weights.start(bound, ("up", last), wu_ref, sems["up"])
        weights.start(bound, ("down", last), wd_ref, sems["down"])
        copy_in(cot_in, cot_ref, sems["cot"])
        fetch(last, "q", "k", "v", "lse", "mid")
        weights.start(bound, ("qkv", last), wq_ref, sems["qkv"])
        bias_ref[...] = mask_bias(len_ref, rows)
        for at in reversed(range(layers)):
            gains = rows_ref[8 * at : 8 * at + 8]
            if at == last:
                wait_all(g_ref, sems["x"])
                take("o")
                keep["r"][...] = g_ref[...].astype(BF)
                scale1 = dense_up(
                    lambda j: g_ref[:, j : j + TILE],
                    keep["o"],
                    wo_ref,
                    lambda: wait_all(wo_ref, sems["out"]),
                    wu_ref,
                    lambda: wait_all(wu_ref, sems["up"]),
                    gains,
                    keep["n1"],
                    wide_ref,
                    gb_ref,
                    keep["slope"],
                    a_ref,
                )
                keep["rs"][...] = jnp.broadcast_to(scale1, (rows, 128))
                wait_all(wd_ref, sems["down"])
                for j in range(0, width, TILE):
                    wide_ref[:, j : j + TILE] += mm(a_ref[...], wd_ref[:, j : j + TILE])
                n2, scale2 = normalize(wide_ref[...])
                out_ref[...] = (n2 * gains[2:3] + gains[3:4]).astype(out_ref.dtype)
                wait_all(cot_ref, sems["cot"])
                incoming = cot_ref[...].astype(F32)
            else:
                take("rs", "n2")
                n2, scale2 = keep["n2"][...].astype(F32), keep["rs"][:, 64:65]
                incoming = g_ref[...]
                wait_all(wd_ref, sems["down"])
                wait_all(wu_ref, sems["up"])
                wait_all(wo_ref, sems["out"])
                take("slope", "n1")
            gz = norm_backward(incoming * gains[2:3], n2, scale2)
            wide_ref[...] = gz
            gb_ref[...] = gz.astype(BF)
            for j in range(0, ff, TILE):
                ga = mm_rt(gb_ref[...], wd_ref[j : j + TILE, :])
                a_ref[:, j : j + TILE] = (ga * keep["slope"][:, j : j + TILE].astype(F32)).astype(BF)
            for j in range(0, width, TILE):
                wide_ref[:, j : j + TILE] += mm_rt(a_ref[...], wu_ref[j : j + TILE, :])
            scale1 = keep["rs"][:, 0:1]
            ghid = norm_backward(wide_ref[...] * gains[0:1], keep["n1"][...].astype(F32), scale1)
            ghid_ref[...] = ghid
            gb_ref[...] = ghid.astype(BF)
            for j in range(0, width, TILE):
                go_ref[:, j : j + TILE] = mm_rt(gb_ref[...], wo_ref[j : j + TILE, :]).astype(BF)
            if at > 0:
                weights.start(bound, ("down", at - 1), wd_ref, sems["down"])
                fetch(at - 1, "n2", "rs", "slope", "n1")
                weights.start(bound, ("up", at - 1), wu_ref, sems["up"])
                weights.start(bound, ("out", at - 1), wo_ref, sems["out"])
            take("q", "k", "v", "lse", *(() if at == last else ("o",)))
            attend_backward(
                keep["q"], keep["k"], keep["v"], keep["o"], go_ref, keep["lse"], bias_ref, gq_ref, gk_ref, gv_ref
            )
            if at > 0:
                fetch(at - 1, "q", "k", "v", "o", "lse")
            up = up_ref.at[at]
            gm = mm_rt(gq_ref[...], up[:, :width]) + mm_rt(gv_ref[...], up[:, 2 * width :])
            gm = gm.astype(BF)
            take("mid", *(() if at == last else ("r",)))
            base = 32 * at
            sums_ref[base : base + 16] = mm_lt(gm, keep["r"][...])[0:16]
            sums_ref[base + 16 : base + 24] = 2.0 * mm_lt(keep["mid"][...], gq_ref[...])[0:8]
            sums_ref[base + 24 : base + 32] = 2.0 * mm_lt(keep["mid"][...], gv_ref[...])[8:16]
            if at == 0:
                gm_ref[...] = gm
                continue
            fetch(at - 1, "mid", "r")
            wait_all(wq_ref, sems["qkv"])
            for j in range(0, width, TILE):
                rs = slice(j, j + TILE)
                total = ghid_ref[:, rs] + mm_rt(gm, down_ref[at, rs, :])
                total += mm_rt(gq_ref[...], wq_ref[rs, :width])
                total += mm_rt(gk_ref[...], wq_ref[rs, width : 2 * width])
                total += mm_rt(gv_ref[...], wq_ref[rs, 2 * width :])
                g_ref[:, rs] = total
            if at > 1:
                weights.start(bound, ("qkv", at - 1), wq_ref, sems["qkv"])

    act = sds((rows, width), BF)
    outs = (act, sds((32 * layers, width), F32), sds((rows, width), F32), act, act, act, sds((rows, 128), BF))
    scratch = [
        pltpu.VMEM((ff, width), BF),
        pltpu.VMEM((width, ff), BF),
        pltpu.VMEM((width, width), BF),
        pltpu.VMEM((width, 3 * width), BF),
        pltpu.VMEM((rows, width), cotangent.dtype),
        pltpu.VMEM((rows, width), F32),
        pltpu.VMEM((rows, ff), BF),
        pltpu.VMEM((rows, width), F32),
        pltpu.VMEM((rows, width), BF),
        pltpu.VMEM((rows, width), BF),
        pltpu.VMEM((rows, rows), F32),
    ]
    like = {**saved[last], **saved[0]}
    scratch += [pltpu.VMEM(like[name].shape, like[name].dtype) for name in names + early]
    scratch += [pltpu.SemaphoreType.DMA((len(names) + len(early) + 6,))]
    return kernel_call(
        body,
        outs,
        scratch,
        layers * (6 * rows * width * (2 * width + ff) + 40 * rows * rows * width),
        (lengths,),
        (rows8, downs, ups),
        raw + weights.leaves(keys),
    )


def input_grad(ghid, gq, gk, gv, gm, down, weights):
    rows, width = ghid.shape
    keys = (("qkv", 0),)

    def body(ghid_ref, gq_ref, gk_ref, gv_ref, gm_ref, down_ref, *rest):
        bound, rest = weights.bind(keys, rest)
        out_ref, w_ref, sem = rest
        weights.start(bound, keys[0], w_ref, sem)
        wait_all(w_ref, sem)
        for j in range(0, width, TILE):
            rs = slice(j, j + TILE)
            total = ghid_ref[:, rs] + mm_rt(gm_ref[...], down_ref[rs, :])
            total += mm_rt(gq_ref[...], w_ref[rs, :width])
            total += mm_rt(gk_ref[...], w_ref[rs, width : 2 * width])
            total += mm_rt(gv_ref[...], w_ref[rs, 2 * width :])
            out_ref[:, rs] = total

    return kernel_call(
        body,
        (sds((rows, width), F32),),
        [pltpu.VMEM((width, 3 * width), BF), pltpu.SemaphoreType.DMA],
        6 * rows * width * width,
        (),
        (ghid, gq, gk, gv, gm, down),
        weights.leaves(keys),
    )[0]


def whole_weights(grid, tensors):
    w_query, w_key, w_value, w_out, w_up, w_down = tensors
    groups, places = {}, {}
    half = w_query.shape[2]
    for at in range(w_query.shape[0]):
        qkv = jnp.concatenate([w[at].astype(BF) for w in (w_query, w_key, w_value)], 1)
        qkv = lax.all_gather(qkv, "dp", axis=0, tiled=True)
        qkv = lax.all_gather(qkv, "head", axis=0, tiled=False)
        heads, width = qkv.shape[0], qkv.shape[1]
        qkv = qkv.reshape(heads, width, 3, half).transpose(1, 2, 0, 3).reshape(width, 3 * heads * half)
        groups["qkv", at] = qkv
        for name, w in (("out", w_out), ("up", w_up), ("down", w_down)):
            groups[name, at] = lax.all_gather(w[at].astype(BF), ("dp", "head"), axis=0, tiled=True)
        for name in ("qkv", "out", "up", "down"):
            places[name, at] = ((name, at), [(0, groups[name, at].shape[1], 0)])
    return Gathered(grid, groups, places)


class Chunk:
    def __init__(self, packed, grid):
        self.grid = grid
        self.packed = packed
        self.cut = cut_of(packed.shape[1])

    def spread_z(self, *gates):
        packed = after(self.packed, *gates) if gates else self.packed
        self.line = [packed] + [shift(packed, self.grid, 0, k) for k in range(1, self.grid[0])]
        return self.line[1:]

    def spread_first(self, *gates):
        line = lax.optimization_barrier((*self.line, *gates))[: len(self.line)]
        parts = (jnp.stack([t[:, : self.cut] for t in line]), jnp.stack([t[:, self.cut :] for t in line]))
        self.first = []
        come = []
        for part, axis in zip(parts, (1, 2)):
            moved = [shift(part, self.grid, axis, k) for k in range(1, self.grid[axis])]
            come += moved
            self.first.append([part] + moved)
        return come

    def spread_second(self, *gates):
        split = len(self.first[0])
        flat = (*self.first[0], *self.first[1])
        flat = lax.optimization_barrier((*flat, *gates))[: len(flat)]
        lines = [jnp.stack(flat[:split]), jnp.stack(flat[split:])]
        self.halves = []
        come = []
        for line, axis in zip(lines, (2, 1)):
            moved = [shift(line, self.grid, axis, k) for k in range(1, self.grid[axis])]
            come += moved
            self.halves.append([line] + moved)
        return come

    def swap(self, *gates):
        if gates:
            leaves, tree = jax.tree.flatten(self.halves)
            leaves = lax.optimization_barrier((*leaves, *gates))[: len(leaves)]
            self.halves = jax.tree.unflatten(tree, leaves)
        return [[(own, swap_cores(own)) for own in half] for half in self.halves]


def gather_and_run(chunks, weights, tokens, attention, dense):
    def arrive(index, *gates):
        weights.groups[index] = c[index].swap(*gates)

    c = chunks
    z0 = c[0].spread_z()
    c[1].spread_z()
    first0 = c[0].spread_first()
    c[2].spread_z(*z0, c[1].packed)
    second0 = c[0].spread_second()
    first1 = c[1].spread_first(*second0)
    arrive(0)
    o = attention(0, tokens)
    second1 = c[1].spread_second()
    first2 = c[2].spread_first(*first1, o)
    c[2].spread_second(*second1)
    arrive(1)
    arrive(2)
    attention(1, dense(0, tokens, o))


def sum_over_devices(sums, grid):
    half = sums.shape[1] // 2
    core = lax.axis_index("head")
    mine = lax.dynamic_slice_in_dim(sums, core * half, half, 1)
    other = lax.dynamic_slice_in_dim(sums, (1 - core) * half, half, 1)
    total = mine + swap_cores(other)
    for axis in (2, 1, 0):
        parts = [total] + [shift(total, grid, axis, k) for k in range(1, grid[axis])]
        total = functools.reduce(jnp.add, parts)
    return total


def pack_chunks(tensors):
    w_query, w_key, w_value, w_out, w_up, w_down = tensors
    layers, rows, half = w_query.shape
    width, ff = 2 * half, w_up.shape[2]
    core = lax.axis_index("head")
    both = jnp.concatenate([w_out[0], w_up[0]], 1).astype(BF)

    def columns(which):
        return jnp.concatenate(
            [
                lax.dynamic_slice_in_dim(both, which * half, half, 1),
                lax.dynamic_slice_in_dim(both, width + which * (ff // 2), ff // 2, 1),
            ],
            1,
        )

    mine, come = columns(core), swap_cores(columns(1 - core))
    both = jnp.concatenate([jnp.where(core == 0, mine, come), jnp.where(core == 0, come, mine)], 0)
    parts = w_down.shape[1] // rows
    made = {("qkv", at): [w[at].astype(BF) for w in (w_query, w_key, w_value)] for at in range(layers)}
    made["out", 0] = [both[:, :half]]
    made["up", 0] = [both[:, half:]]
    made["down", 0] = [w_down[0, i * rows : (i + 1) * rows].astype(BF) for i in range(parts)]
    chunks = [[("qkv", 0)], [("out", 0), ("up", 0)], [("down", 0), ("qkv", 1)]]
    packs, places = [], {}
    for index, keys in enumerate(chunks):
        lanes = sum(block.shape[1] for key in keys for block in made[key])
        cut, at = cut_of(lanes), 0
        for key in keys:
            items = []
            for wide, placer in tensor_items(key[0], rows, width, ff, parts):
                for half_at, low, high in ((0, 0, cut), (1, cut, lanes)):
                    start, stop = max(at, low), min(at + wide, high)
                    if start < stop:
                        items.append((half_at, start - low, stop - start, placer(start - at)))
                at += wide
            places[key] = (index, items)
        packs.append(jnp.concatenate([block for key in keys for block in made[key]], 1))
    return packs, places


def gather_dense(w_out, w_up, w_down):
    rows, ff = w_up.shape
    width = w_out.shape[1]
    parts = w_down.shape[0] // rows
    up = w_up.astype(BF).reshape(rows, ff // (parts * rows), parts, rows).swapaxes(1, 2).reshape(rows, ff)
    blocks = [w_down[i * rows : (i + 1) * rows].astype(BF) for i in range(parts)]
    packed = jnp.concatenate([w_out.astype(BF), up, *blocks], 1)
    whole = lax.all_gather(packed, ("dp", "head"), axis=0, tiled=True)
    places = {
        "out": [(0, width, 0)],
        "up": [(width, ff, 0)],
        "down": [(width + ff + i * width, width, i * width) for i in range(parts)],
    }
    return whole, places


def body(
    tokens,
    seq_len,
    w_query,
    w_key,
    w_value,
    w_out,
    w_up,
    w_down,
    a_query,
    b_query,
    a_value,
    b_value,
    ln_gain,
    ln_bias,
    cotangent,
):
    layers, width = w_query.shape[0], tokens.shape[1]
    rank = a_query.shape[2]
    half = b_query.shape[2]
    grid = chip_grid(lax.axis_size("dp"))
    core = lax.axis_index("head")
    tensors = (w_query, w_key, w_value, w_out, w_up, w_down)

    own = jnp.stack([b_query, b_value], 1).astype(BF)
    other = swap_cores(own)
    up_all = jnp.concatenate([jnp.where(core == 0, own, other), jnp.where(core == 0, other, own)], -1)
    pair = jnp.concatenate([a_query, a_value], 2).astype(BF)
    downs = jnp.pad(pair, ((0, 0), (0, 0), (0, 128 - 2 * rank)))
    q_up = jnp.pad(2.0 * up_all[:, 0], ((0, 0), (0, 128 - rank), (0, 0)))
    v_up = jnp.pad(2.0 * up_all[:, 1], ((0, 0), (rank, 128 - 2 * rank), (0, 0)))
    ups = jnp.concatenate([q_up, jnp.zeros_like(q_up), v_up], 2)
    gains = jnp.stack([ln_gain[:, 0], ln_bias[:, 0], ln_gain[:, 1], ln_bias[:, 1]], 1)
    rows8 = jnp.pad(gains, ((0, 0), (0, 4), (0, 0)))

    pieces = w_query.shape[1] % 16 == 0 and lax.axis_size("head") == 2 and layers == 2
    saved = []
    if not pieces:
        weights = whole_weights(grid, tensors)
        weights.ff = w_up.shape[2]
    else:
        whole, whole_places = gather_dense(w_out[1], w_up[1], w_down[1])
        packs, places = pack_chunks(tensors)
        for name, lanes in whole_places.items():
            places[name, 1] = ("dense", lanes)
        chunks = [Chunk(packed, grid) for packed in packs]
        weights = Gathered(grid, {"dense": whole}, places)
        weights.ff = w_up.shape[2]

    def attention(at, stream):
        q, k, v, o, lse, mid = attend_forward(stream, downs[at], ups[at], weights, at, seq_len)
        saved.append({"q": q, "k": k, "v": v, "o": o, "lse": lse, "mid": mid, "x": stream})
        return o

    def dense(at, stream, attended):
        got = dense_forward(stream, attended, rows8[at], weights, at)
        saved[at].update(zip(("n1", "rs", "slope", "out", "n2"), got))
        saved[at]["r"] = stream.astype(BF)
        return saved[at]["out"]

    if not pieces:
        stream = tokens
        for at in range(layers):
            attended = attention(at, stream)
            if at < layers - 1:
                stream = dense(at, stream, attended)
    else:
        gather_and_run(chunks, weights, tokens, attention, dense)
    output, sums, ghid, gq, gk, gv, gm = backward(
        saved, cotangent, rows8.reshape(8 * layers, width), downs, ups, weights, seq_len
    )
    grad = input_grad(ghid, gq, gk, gv, gm, downs[0], weights)
    total = sum_over_devices(sums, grid).reshape(layers, 4, rank, half)
    lower = total[:, :2].reshape(layers * 2 * rank, half)
    far = swap_cores(lower)
    lower = jnp.concatenate([jnp.where(core == 0, lower, far), jnp.where(core == 0, far, lower)], 1)
    lower = lower.reshape(layers, 2, rank, width).transpose(0, 1, 3, 2)
    return (output, grad, lower[:, 0], total[:, 2], lower[:, 1], total[:, 3])


def solution(mesh):
    both = ("dp", "head")
    placed = (
        P(both, None),
        P("dp"),
        P(None, "dp", "head"),
        P(None, "dp", "head"),
        P(None, "dp", "head"),
        P(None, both, None),
        P(None, both, None),
        P(None, both, None),
        P(),
        P(None, None, "head"),
        P(),
        P(None, None, "head"),
        P(),
        P(),
        P(both, None),
    )
    return jax.shard_map(
        body,
        mesh=mesh,
        in_specs=placed,
        out_specs=(
            P(both, None),
            P(both, None),
            P(),
            P(None, None, "head"),
            P(),
            P(None, None, "head"),
        ),
        check_vma=False,
    )
```

time: 773 us -> 286 us (0.37)
  blocking collectives: 280 us -> 0 us
  matrix products: 218 us -> 0 us
  Pallas kernels: 0 us -> 108 us
  waiting for transfers between devices: 137 us -> 95.4 us
  other arithmetic: 46 us -> 4.92 us
  local copies, waits for them, and re-layouts: 53.2 us -> 16.8 us
  starting transfers between devices: 5.24 us -> 40.7 us
    all_gather x6 -> x0, blocking collectives: 265 us -> none  [the longest x2 90.1 us: gather_head(): lax.all_gather(pieces[1], 'dp', axis=0, tiled=True)]
    dot_general x76 -> x0, matrix products: 218 us -> none  [the longest x12 46.5 us: dot_right_t(): lax.dot_general(left, right, (((1,), (1,)), ((), ())), preferred_element_...]
    psum x1 -> x0, waiting for transfers between devices: 121 us -> none  [body(): lax.psum((wide_terms[0], wide_terms[1], wide_terms[2], wide_terms[3]), ('...]
    pallas_call x0 -> x5, Pallas kernels: none -> 108 us  [kernel_call(): pl.pallas_call(body, out_shape=tuple(outs), in_specs=specs, out_specs=tup...]
    ppermute x0 -> x42, waiting for transfers between devices: none -> 95.4 us  [the longest x26 86.4 us: shift(): return lax.ppermute(values, 'dp', pairs)]
    ppermute x0 -> x42, starting transfers between devices: none -> 40.7 us  [the longest x26 37.4 us: shift(): return lax.ppermute(values, 'dp', pairs)]
    reduce_sum x13 -> x0, other arithmetic: 18.6 us -> none  [the longest x4 8.28 us: layer_norm(): center = values - jnp.mean(values, -1, keepdims=True)]
    all_to_all x3 -> x0, blocking collectives: 15.7 us -> none  [the longest x2 9.16 us: layer_backward(): lax.all_to_all(grad_merged, 'head', split_axis=1, concat_axis=0, tiled=True)]
  transfers between devices with their start and end apart: 12 -> 43, of which waited for: 4 -> 13; matrix products, arithmetic and copies ran while one was open for 20% -> 4% of each run, Pallas kernels for 0% -> 18%
where the time goes in v2:
time: 286 us; the launch traced here: 281 us
  Pallas kernels  108 us (38%)
  waiting for transfers between devices  95.4 us (33%)
  starting transfers between devices  40.7 us (14%)
  local copies, waits for them, and re-layouts  16.8 us (6%)
  between operations  15.2 us (5%)
  other arithmetic  4.92 us (2%)
    pallas_call x5, Pallas kernels, kernel_call(): pl.pallas_call(body, out_shape=tuple(outs), in_specs=specs, out_specs=tup...  108 us
    ppermute x26, waiting for transfers between devices, shift(): return lax.ppermute(values, 'dp', pairs)  86.4 us
    ppermute x26, starting transfers between devices, shift(): return lax.ppermute(values, 'dp', pairs)  37.4 us
    ppermute x16, waiting for transfers between devices, swap_cores(): lax.ppermute(values, 'head', [(i, (i + 1) % size) for i in range(size)])  8.97 us
  transfers between devices with their start and end apart: 43, of which 13 were waited for; matrix products, arithmetic and copies ran while one was open for 4% of the time, Pallas kernels for 18%

profile of v2, /device:TPU:0, one launch (start us, length us, event | category | flops | bytes accessed | tf_op | source)
XLA Modules:
  0.0 280.6 jit_solution(18345281869166306797)
XLA Ops:
  7.2 1.0 convert.53
  8.2 1.1 convert.55
  9.4 1.2 convert_element_type.77
  10.8 1.3 reshape.52
  13.1 5.1 %collective-permute-start.3 = (bf16[48,1152]{1,0:T(8,128)(2,1)S(1)}, bf16[48,1152]{1,0:T(8,128)(2,1)S(1)}, u32[]{:S(2)}, u32[]{:S(2)}) collective-permute-start(bf16[48,1152]{1,0:T(8,128)(2,1)S(1)} %pad_maximum_fusion.13), channel_id=1, source_target_pairs={{0,24},{2,26},{4,28},{6,30},{8,0},{10,2},{12,4},{14,6},{16,8},{18,... | collective-permute-start | bytes 331784 | tf_op jit(solution)/shard_map/ppermute | solution.py:48
  18.2 1.0 collective-permute-start.1
  23.5 0.8 slice_bitcast_fusion.2
  24.5 3.4 %collective-permute-done.2 = bf16[48,1152]{1,0:T(8,128)(2,1)S(1)} collective-permute-done((bf16[48,1152]{1,0:T(8,128)(2,1)S(1)}, bf16[48,1152]{1,0:T(8,128)(2,1)S(1)}, u32[]{:S(2)}, u32[]{:S(2)}) %collective-permute-start.2) | collective-permute-done | bytes 110624 | tf_op jit(solution)/shard_map/ppermute | solution.py:48
  28.0 1.6 collective-permute-start.4
  29.7 1.6 collective-permute-start.5
  31.3 2.0 collective-permute-start.15
  33.2 5.7 %collective-permute-start.14 = (bf16[48,1920]{1,0:T(8,128)(2,1)S(1)}, bf16[48,1920]{1,0:T(8,128)(2,1)S(1)}, u32[]{:S(2)}, u32[]{:S(2)}) collective-permute-start(bf16[48,1920]{1,0:T(8,128)(2,1)S(1)} %pad_maximum_fusion.12), channel_id=1, source_target_pairs={{0,16},{2,18},{4,20},{6,22},{8,24},{10,26},{12,28},{14,30},{16,0},... | collective-permute-start | bytes 552968 | tf_op jit(solution)/shard_map/ppermute | solution.py:48
  38.9 1.9 collective-permute-start.13
  41.3 12.2 %collective-permute-done.14 = bf16[48,1920]{1,0:T(8,128)(2,1)S(1)} collective-permute-done((bf16[48,1920]{1,0:T(8,128)(2,1)S(1)}, bf16[48,1920]{1,0:T(8,128)(2,1)S(1)}, u32[]{:S(2)}, u32[]{:S(2)}) %collective-permute-start.14) | collective-permute-done | bytes 184352 | tf_op jit(solution)/shard_map/ppermute | solution.py:48
  54.2 1.0 collective-permute-start.17
  55.3 1.0 collective-permute-start.16
  56.3 13.8 %collective-permute-done.17 = bf16[4,48,896]{2,1,0:T(8,128)(2,1)S(1)} collective-permute-done((bf16[4,48,896]{2,1,0:T(8,128)(2,1)S(1)}, bf16[4,48,896]{2,1,0:T(8,128)(2,1)S(1)}, u32[]{:S(2)}, u32[]{:S(2)}) %collective-permute-start.17) | collective-permute-done | bytes 344096 | tf_op jit(solution)/shard_map/ppermute | solution.py:48
  70.1 1.1 slice_bitcast_fusion
  71.4 2.2 collective-permute-start.25
  73.6 2.0 collective-permute-start.24
  75.6 1.2 collective-permute-start.22
  76.9 1.3 collective-permute-start.19
  78.2 13.9 %shard_map.190 = (bf16[512,768]{1,0:T(8,128)(2,1)}, bf16[512,768]{1,0:T(8,128)(2,1)}, bf16[512,768]{1,0:T(8,128)(2,1)}, bf16[512,768]{1,0:T(8,128)(2,1)}, f32[12...) custom-call(s32[2]{0:T(128)} %len_ref.5, bf16[512,768]{1,0:T(8,128)(2,1)} %rest_18_.1, ...), custom_call_target="tpu_custom_call" | custom-call | flops 5033164800 | bytes 8585216 | tf_op jit(solution)/shard_map/pallas_call | solution.py:164
  92.2 15.1 %collective-permute-done.25 = bf16[48,2688]{1,0:T(8,128)(2,1)S(1)} collective-permute-done((bf16[48,2688]{1,0:T(8,128)(2,1)}, bf16[48,2688]{1,0:T(8,128)(2,1)S(1)}, u32[]{:S(2)}, u32[]{:S(2)}) %collective-permute-start.25) | collective-permute-done | bytes 258080 | tf_op jit(solution)/shard_map/ppermute | solution.py:48
  107.2 0.9 slice_bitcast_fusion.12
  108.1 0.9 slice_bitcast_fusion.8
  109.3 1.5 collective-permute-start.27
  110.9 14.9 %collective-permute-done.28 = bf16[4,48,1280]{2,1,0:T(8,128)(2,1)S(1)} collective-permute-done((bf16[4,48,1280]{2,1,0:T(8,128)(2,1)S(1)}, bf16[4,48,1280]{2,1,0:T(8,128)(2,1)S(1)}, u32[]{:S(2)}, u32[]{:S(2)}) %collective-permute-start.28) | collective-permute-done | bytes 491552 | tf_op jit(solution)/shard_map/ppermute | solution.py:48
  125.8 1.1 collective-permute-done.27
  127.0 1.5 collective-permute-start.30
  129.9 4.7 %collective-permute-done.21.rest_5_.rest_33_ = bf16[2,4,48,896]{3,2,1,0:T(8,128)(2,1)S(1)} collective-permute-done((bf16[2,4,48,896]{3,2,1,0:T(8,128)(2,1)S(1)}, bf16[2,4,48,896]{3,2,1,0:T(8,128)(2,1)S(1)}, u32[]{:S(2)}, u32[]{:S(2)}) %collective-permute-start.21) | collective-permute-done | bytes 688160 | tf_op jit(solution)/shard_map/ppermute | solution.py:53
  134.8 18.1 %collective-permute-done.30.rest_10_.rest_2_.rest_22_ = bf16[2,4,48,1408]{3,2,1,0:T(8,128)(2,1)} collective-permute-done((bf16[2,4,48,1408]{3,2,1,0:T(8,128)(2,1)S(1)}, bf16[2,4,48,1408]{3,2,1,0:T(8,128)(2,1)}, u32[]{:S(2)}, u32[]{:S(2)}) %collective-permute-start.30) | collective-permute-done | bytes 1081376 | tf_op jit(solution)/shard_map/ppermute | solution.py:48
  154.4 0.9 copy-done.28
  155.3 0.8 pad.17.down_ref
  157.4 2.5 collective-permute-done.20.rest_3_.rest_31_
  159.9 0.9 copy-done.25
  160.8 14.8 %shard_map.191 = (bf16[512,768]{1,0:T(8,128)(2,1)}, f32[512,128]{1,0:T(8,128)}, bf16[512,3072]{1,0:T(8,128)(2,1)}, f32[512,768]{1,0:T(8,128)}, bf16[512,768]{1,0:T(8,128)(2,1)}) custom-call(bf16[512,768]{1,0:T(8,128)(2,1)} %rest_18_.1, bf16[512,768]{1,0:T(8,128)(2,1)} %get-tuple-element.63.o_ref.rest_11_, f32[8,768]{1,0:T(8,128)} %slice_bitcast_fusion.47.rows_ref, ...), custom_call_target="tpu_custom_call" | custom-call | flops 5435817984 | bytes 22306816 | tf_op jit(solution)/shard_map/pallas_call | solution.py:164
  175.6 14.6 %shard_map.192 = (bf16[512,768]{1,0:T(8,128)(2,1)}, bf16[512,768]{1,0:T(8,128)(2,1)}, bf16[512,768]{1,0:T(8,128)(2,1)}, bf16[512,768]{1,0:T(8,128)(2,1)}, f32[12...) custom-call(s32[2]{0:T(128)} %len_ref.5, f32[512,768]{1,0:T(8,128)} %get-tuple-element.81.x_ref.rest_1_, ...), custom_call_target="tpu_custom_call" | custom-call | flops 5033164800 | bytes 14090240 | tf_op jit(solution)/shard_map/pallas_call | solution.py:164
  190.3 56.8 %shard_map.193 = (bf16[512,768]{1,0:T(8,128)(2,1)}, f32[64,768]{1,0:T(8,128)}, f32[512,768]{1,0:T(8,128)}, bf16[512,768]{1,0:T(8,128)(2,1)}, bf16[512,768]{1,0:T...) custom-call(s32[2]{0:T(128)} %len_ref.5, f32[16,768]{1,0:T(8,128)} %get-tuple-element.127.rows_ref, ...), custom_call_target="tpu_custom_call" | custom-call | flops 37849399296 | bytes 46514176 | tf_op jit(solution)/shard_map/pallas_call | solution.py:164
  247.1 0.9 constant_dynamic-slice_fusion
  248.1 1.2 collective-permute-done.35
  249.3 0.9 dynamic-slice_add_fusion
  250.2 1.3 collective-permute-start.36
  251.6 3.6 %collective-permute-done.36 = f32[64,384]{1,0:T(8,128)S(1)} collective-permute-done((f32[64,384]{1,0:T(8,128)S(1)}, f32[64,384]{1,0:T(8,128)S(1)}, u32[]{:S(2)}, u32[]{:S(2)}) %collective-permute-start.36) | collective-permute-done | bytes 98336 | tf_op jit(solution)/shard_map/ppermute | solution.py:48
  255.5 4.3 %collective-permute-done.37 = f32[64,384]{1,0:T(8,128)S(1)} collective-permute-done((f32[64,384]{1,0:T(8,128)S(1)}, f32[64,384]{1,0:T(8,128)S(1)}, u32[]{:S(2)}, u32[]{:S(2)}) %collective-permute-start.37) | collective-permute-done | bytes 98336 | tf_op jit(solution)/shard_map/ppermute | solution.py:48
  259.9 2.6 collective-permute-start.39
  262.6 1.5 collective-permute-start.38
  264.1 7.5 %shard_map.194 = f32[512,768]{1,0:T(8,128)} custom-call(f32[512,768]{1,0:T(8,128)} %get-tuple-element.98.ghid_ref, bf16[512,768]{1,0:T(8,128)(2,1)} %get-tuple-element.99.gq_ref, bf16[512,768]{1,0:T(8,128)(2,1)} %get-tuple-element.100.gk_ref, bf16[512,768]{1,0:T(8,128)(2,1)} %get-tuple-element.101.gv_ref, bf16[512,128]{1,0:T(8,128)(2,1)} %get-tuple-element.102.gm_ref, ...), custom_call_target="tpu_custom_call" | custom-call | flops 1811939328 | bytes 9371648 | tf_op jit(solution)/shard_map/pallas_call | solution.py:164
  (195 shorter events, 14.2 us)
Async XLA Ops:
  7.2 183.1 %all-gather.2.cloned.1.call-start = ((), (), s32[]{:S(2)}) async-start(), calls=%async_computation | async-start | bytes 10948608 | tf_op jit(solution)/shard_map/all_gather | solution.py:690
  13.1 11.4 %collective-permute-start.3 = (bf16[48,1152]{1,0:T(8,128)(2,1)S(1)}, bf16[48,1152]{1,0:T(8,128)(2,1)S(1)}, u32[]{:S(2)}, u32[]{:S(2)}) collective-permute-start(bf16[48,1152]{1,0:T(8,128)(2,1)S(1)} %pad_maximum_fusion.13), channel_id=1, source_target_pairs={{0,24},{2,26},{4,28},{6,30},{8,0},{10,2},{12,4},{14,6},{16,8},{18,... | collective-permute-start | bytes 331784 | tf_op jit(solution)/shard_map/ppermute | solution.py:48
  18.2 9.7 %collective-permute-start.2 = (bf16[48,1152]{1,0:T(8,128)(2,1)S(1)}, bf16[48,1152]{1,0:T(8,128)(2,1)S(1)}, u32[]{:S(2)}, u32[]{:S(2)}) collective-permute-start(bf16[48,1152]{1,0:T(8,128)(2,1)S(1)} %pad_maximum_fusion.13), channel_id=1, source_target_pairs={{0,16},{2,18},{4,20},{6,22},{8,24},{10,26},{12,28},{14,30},{16,0},... | collective-permute-start | bytes 331784 | tf_op jit(solution)/shard_map/ppermute | solution.py:48
  18.2 9.7 %collective-permute-start.1 = (bf16[48,1152]{1,0:T(8,128)(2,1)S(1)}, bf16[48,1152]{1,0:T(8,128)(2,1)S(1)}, u32[]{:S(2)}, u32[]{:S(2)}) collective-permute-start(bf16[48,1152]{1,0:T(8,128)(2,1)S(1)} %pad_maximum_fusion.13), channel_id=1, source_target_pairs={{0,8},{2,10},{4,12},{6,14},{8,16},{10,18},{12,20},{14,22},{16,24},... | collective-permute-start | bytes 331784 | tf_op jit(solution)/shard_map/ppermute | solution.py:48
  19.2 5.1 %collective-permute-start = (bf16[2,2,8,384]{3,2,0,1:T(8,128)(2,1)S(1)}, bf16[2,2,8,384]{3,2,0,1:T(8,128)(2,1)S(1)}, u32[]{:S(2)}, u32[]{:S(2)}) collective-permute-start(bf16[2,2,8,384]{3,2,0,1:T(8,128)(2,1)S(1)} %pad_maximum_fusion.19), channel_id=1, source_target_pairs={{0,1},{1,0},{2,3},{3,2},{4,5},{5,4},{6,7},{7,6},{8,9},{9,8},{10,11... | collective-permute-start | bytes 73736 | tf_op jit(solution)/shard_map/ppermute | solution.py:53
  19.5 4.9 %collective-permute-start.12 = (bf16[24,1920]{1,0:T(8,128)(2,1)S(1)}, bf16[24,1920]{1,0:T(8,128)(2,1)S(1)}, u32[]{:S(2)}, u32[]{:S(2)}) collective-permute-start(bf16[24,1920]{1,0:T(8,128)(2,1)S(1)} %pad_maximum_fusion.16), channel_id=1, source_target_pairs={{0,1},{1,0},{2,3},{3,2},{4,5},{5,4},{6,7},{7,6},{8,9},{9,8},{10,11... | collective-permute-start | bytes 276488 | tf_op jit(solution)/shard_map/ppermute | solution.py:53
  28.0 12.8 %collective-permute-start.4 = (bf16[4,48,640]{2,1,0:T(8,128)(2,1)S(1)}, bf16[4,48,640]{2,1,0:T(8,128)(2,1)S(1)}, u32[]{:S(2)}, u32[]{:S(2)}) collective-permute-start(bf16[4,48,640]{2,1,0:T(8,128)(2,1)S(1)} %pad_maximum_fusion.10), channel_id=1, source_target_pairs={{0,4},{2,6},{4,0},{6,2},{8,12},{10,14},{12,8},{14,10},{16,20},{18,... | collective-permute-start | bytes 737288 | tf_op jit(solution)/shard_map/ppermute | solution.py:48
  29.7 11.2 %collective-permute-start.5 = (bf16[4,48,512]{2,1,0:T(8,128)(2,1)S(1)}, bf16[4,48,512]{2,1,0:T(8,128)(2,1)S(1)}, u32[]{:S(2)}, u32[]{:S(2)}) collective-permute-start(bf16[4,48,512]{2,1,0:T(8,128)(2,1)S(1)} %pad_maximum_fusion.11), channel_id=1, source_target_pairs={{0,2},{2,0},{4,6},{6,4},{8,10},{10,8},{12,14},{14,12},{16,18},{18,... | collective-permute-start | bytes 589832 | tf_op jit(solution)/shard_map/ppermute | solution.py:48
  31.3 10.0 %collective-permute-start.15 = (bf16[48,1920]{1,0:T(8,128)(2,1)S(1)}, bf16[48,1920]{1,0:T(8,128)(2,1)S(1)}, u32[]{:S(2)}, u32[]{:S(2)}) collective-permute-start(bf16[48,1920]{1,0:T(8,128)(2,1)S(1)} %pad_maximum_fusion.12), channel_id=1, source_target_pairs={{0,24},{2,26},{4,28},{6,30},{8,0},{10,2},{12,4},{14,6},{16,8},{18,... | collective-permute-start | bytes 552968 | tf_op jit(solution)/shard_map/ppermute | solution.py:48
  33.2 20.3 %collective-permute-start.14 = (bf16[48,1920]{1,0:T(8,128)(2,1)S(1)}, bf16[48,1920]{1,0:T(8,128)(2,1)S(1)}, u32[]{:S(2)}, u32[]{:S(2)}) collective-permute-start(bf16[48,1920]{1,0:T(8,128)(2,1)S(1)} %pad_maximum_fusion.12), channel_id=1, source_target_pairs={{0,16},{2,18},{4,20},{6,22},{8,24},{10,26},{12,28},{14,30},{16,0},... | collective-permute-start | bytes 552968 | tf_op jit(solution)/shard_map/ppermute | solution.py:48
  38.9 15.1 %collective-permute-start.13 = (bf16[48,1920]{1,0:T(8,128)(2,1)S(1)}, bf16[48,1920]{1,0:T(8,128)(2,1)S(1)}, u32[]{:S(2)}, u32[]{:S(2)}) collective-permute-start(bf16[48,1920]{1,0:T(8,128)(2,1)S(1)} %pad_maximum_fusion.12), channel_id=1, source_target_pairs={{0,8},{2,10},{4,12},{6,14},{8,16},{10,18},{12,20},{14,22},{16,24},... | collective-permute-start | bytes 552968 | tf_op jit(solution)/shard_map/ppermute | solution.py:48
  40.9 12.6 %collective-permute-start.10 = (bf16[2,4,48,512]{3,2,1,0:T(8,128)(2,1)S(1)}, bf16[2,4,48,512]{3,2,1,0:T(8,128)(2,1)S(1)}, u32[]{:S(2)}, u32[]{:S(2)}) collective-permute-start(bf16[2,4,48,512]{3,2,1,0:T(8,128)(2,1)S(1)} %pad_maximum_fusion.7.rest_4_), channel_id=1, source_target_pairs={{0,4},{2,6},{4,0},{6,2},{8,12},{10,14},{12,8},{14,10},{16,20},{18,... | collective-permute-start | bytes 1179656 | tf_op jit(solution)/shard_map/ppermute | solution.py:48
  41.1 13.0 %collective-permute-start.7 = (bf16[2,4,48,640]{3,2,1,0:T(8,128)(2,1)S(1)}, bf16[2,4,48,640]{3,2,1,0:T(8,128)(2,1)S(1)}, u32[]{:S(2)}, u32[]{:S(2)}) collective-permute-start(bf16[2,4,48,640]{3,2,1,0:T(8,128)(2,1)S(1)} %pad_maximum_fusion.5.rest_0_), channel_id=1, source_target_pairs={{0,2},{2,0},{4,6},{6,4},{8,10},{10,8},{12,14},{14,12},{16,18},{18,... | collective-permute-start | bytes 1474568 | tf_op jit(solution)/shard_map/ppermute | solution.py:48
  41.2 28.9 %copy-start = (bf16[2,128,2304]{2,1,0:T(8,128)(2,1)}, bf16[2,128,2304]{2,1,0:T(8,128)(2,1)S(1)}, u32[]{:S(2)}) copy-start(bf16[2,128,2304]{2,1,0:T(8,128)(2,1)S(1)} %fusion.2.up_ref) | copy-start | bytes 3538948
  41.2 30.1 %collective-permute-start.9 = (bf16[2,4,48,512]{3,2,1,0:T(8,128)(2,1)S(1)}, bf16[2,4,48,512]{3,2,1,0:T(8,128)(2,1)S(1)}, u32[]{:S(2)}, u32[]{:S(2)}) collective-permute-start(bf16[2,4,48,512]{3,2,1,0:T(8,128)(2,1)S(1)} %pad_maximum_fusion.7.rest_4_), channel_id=1, source_target_pairs={{0,1},{1,0},{2,3},{3,2},{4,5},{5,4},{6,7},{7,6},{8,9},{9,8},{10,11... | collective-permute-start | bytes 1179656 | tf_op jit(solution)/shard_map/ppermute | solution.py:53
  53.5 20.1 %collective-permute-start.6 = (bf16[2,4,48,640]{3,2,1,0:T(8,128)(2,1)S(1)}, bf16[2,4,48,640]{3,2,1,0:T(8,128)(2,1)S(1)}, u32[]{:S(2)}, u32[]{:S(2)}) collective-permute-start(bf16[2,4,48,640]{3,2,1,0:T(8,128)(2,1)S(1)} %pad_maximum_fusion.5.rest_0_), channel_id=1, source_target_pairs={{0,1},{1,0},{2,3},{3,2},{4,5},{5,4},{6,7},{7,6},{8,9},{9,8},{10,11... | collective-permute-start | bytes 1474568 | tf_op jit(solution)/shard_map/ppermute | solution.py:53
  53.5 22.1 %collective-permute-start.11 = (bf16[2,4,48,512]{3,2,1,0:T(8,128)(2,1)S(1)}, bf16[2,4,48,512]{3,2,1,0:T(8,128)(2,1)S(1)}, u32[]{:S(2)}, u32[]{:S(2)}) collective-permute-start(bf16[2,4,48,512]{3,2,1,0:T(8,128)(2,1)S(1)} %collective-permute-done.10.rest_6_), channel_id=1, source_target_pairs={{0,1},{1,0},{2,3},{3,2},{4,5},{5,4},{6,7},{7,6},{8,9},{9,8},{10,11... | collective-permute-start | bytes 1179656 | tf_op jit(solution)/shard_map/ppermute | solution.py:53
  54.2 15.9 %collective-permute-start.17 = (bf16[4,48,896]{2,1,0:T(8,128)(2,1)S(1)}, bf16[4,48,896]{2,1,0:T(8,128)(2,1)S(1)}, u32[]{:S(2)}, u32[]{:S(2)}) collective-permute-start(bf16[4,48,896]{2,1,0:T(8,128)(2,1)S(1)} %pad_maximum_fusion.9), channel_id=1, source_target_pairs={{0,2},{2,0},{4,6},{6,4},{8,10},{10,8},{12,14},{14,12},{16,18},{18,... | collective-permute-start | bytes 1032200 | tf_op jit(solution)/shard_map/ppermute | solution.py:48
  55.3 15.9 %collective-permute-start.16 = (bf16[4,48,1024]{2,1,0:T(8,128)(2,1)S(1)}, bf16[4,48,1024]{2,1,0:T(8,128)(2,1)S(1)}, u32[]{:S(2)}, u32[]{:S(2)}) collective-permute-start(bf16[4,48,1024]{2,1,0:T(8,128)(2,1)S(1)} %pad_maximum_fusion.8), channel_id=1, source_target_pairs={{0,4},{2,6},{4,0},{6,2},{8,12},{10,14},{12,8},{14,10},{16,20},{18,... | collective-permute-start | bytes 1179656 | tf_op jit(solution)/shard_map/ppermute | solution.py:48
  70.1 6.8 %collective-permute-start.8 = (bf16[2,4,48,640]{3,2,1,0:T(8,128)(2,1)S(1)}, bf16[2,4,48,640]{3,2,1,0:T(8,128)(2,1)S(1)}, u32[]{:S(2)}, u32[]{:S(2)}) collective-permute-start(bf16[2,4,48,640]{3,2,1,0:T(8,128)(2,1)S(1)} %collective-permute-done.7.rest_2_), channel_id=1, source_target_pairs={{0,1},{1,0},{2,3},{3,2},{4,5},{5,4},{6,7},{7,6},{8,9},{9,8},{10,11... | collective-permute-start | bytes 1474568 | tf_op jit(solution)/shard_map/ppermute | solution.py:53
  71.2 20.9 %collective-permute-start.26 = (bf16[48,2688]{1,0:T(8,128)(2,1)}, bf16[48,2688]{1,0:T(8,128)(2,1)S(1)}, u32[]{:S(2)}, u32[]{:S(2)}) collective-permute-start(bf16[48,2688]{1,0:T(8,128)(2,1)} %fusion.13), channel_id=1, source_target_pairs={{0,24},{2,26},{4,28},{6,30},{8,0},{10,2},{12,4},{14,6},{16,8},{18,... | collective-permute-start | bytes 774152 | tf_op jit(solution)/shard_map/ppermute | solution.py:48
  71.4 57.9 %copy-start.5 = (bf16[2,4,48,1024]{3,2,1,0:T(8,128)(2,1)}, bf16[2,4,48,1024]{3,2,1,0:T(8,128)(2,1)S(1)}, u32[]{:S(2)}) copy-start(bf16[2,4,48,1024]{3,2,1,0:T(8,128)(2,1)S(1)} %pad_maximum_fusion.2.rest_0_.rest_28_) | copy-start | bytes 2359300
  71.4 35.8 %collective-permute-start.25 = (bf16[48,2688]{1,0:T(8,128)(2,1)}, bf16[48,2688]{1,0:T(8,128)(2,1)S(1)}, u32[]{:S(2)}, u32[]{:S(2)}) collective-permute-start(bf16[48,2688]{1,0:T(8,128)(2,1)} %fusion.13), channel_id=1, source_target_pairs={{0,16},{2,18},{4,20},{6,22},{8,24},{10,26},{12,28},{14,30},{16,0},... | collective-permute-start | bytes 774152 | tf_op jit(solution)/shard_map/ppermute | solution.py:48
  73.6 33.6 %collective-permute-start.24 = (bf16[48,2688]{1,0:T(8,128)(2,1)}, bf16[48,2688]{1,0:T(8,128)(2,1)S(1)}, u32[]{:S(2)}, u32[]{:S(2)}) collective-permute-start(bf16[48,2688]{1,0:T(8,128)(2,1)} %fusion.13), channel_id=1, source_target_pairs={{0,8},{2,10},{4,12},{6,14},{8,16},{10,18},{12,20},{14,22},{16,24},... | collective-permute-start | bytes 774152 | tf_op jit(solution)/shard_map/ppermute | solution.py:48
  75.6 51.3 %collective-permute-start.22 = (bf16[2,4,48,896]{3,2,1,0:T(8,128)(2,1)S(1)}, bf16[2,4,48,896]{3,2,1,0:T(8,128)(2,1)}, u32[]{:S(2)}, u32[]{:S(2)}) collective-permute-start(bf16[2,4,48,896]{3,2,1,0:T(8,128)(2,1)S(1)} %pad_maximum_fusion.3.rest_4_.rest_32_), channel_id=1, source_target_pairs={{0,4},{2,6},{4,0},{6,2},{8,12},{10,14},{12,8},{14,10},{16,20},{18,... | collective-permute-start | bytes 2064392 | tf_op jit(solution)/shard_map/ppermute | solution.py:48
  76.9 50.0 %collective-permute-start.19 = (bf16[2,4,48,1024]{3,2,1,0:T(8,128)(2,1)S(1)}, bf16[2,4,48,1024]{3,2,1,0:T(8,128)(2,1)}, u32[]{:S(2)}, u32[]{:S(2)}) collective-permute-start(bf16[2,4,48,1024]{3,2,1,0:T(8,128)(2,1)S(1)} %pad_maximum_fusion.2.rest_0_.rest_28_), channel_id=1, source_target_pairs={{0,2},{2,0},{4,6},{6,4},{8,10},{10,8},{12,14},{14,12},{16,18},{18,... | collective-permute-start | bytes 2359304 | tf_op jit(solution)/shard_map/ppermute | solution.py:48
  109.3 17.6 %collective-permute-start.27 = (bf16[4,48,1408]{2,1,0:T(8,128)(2,1)S(1)}, bf16[4,48,1408]{2,1,0:T(8,128)(2,1)S(1)}, u32[]{:S(2)}, u32[]{:S(2)}) collective-permute-start(bf16[4,48,1408]{2,1,0:T(8,128)(2,1)S(1)} %pad_maximum_fusion.4), channel_id=1, source_target_pairs={{0,4},{2,6},{4,0},{6,2},{8,12},{10,14},{12,8},{14,10},{16,20},{18,... | collective-permute-start | bytes 1622024 | tf_op jit(solution)/shard_map/ppermute | solution.py:48
  110.8 15.0 %collective-permute-start.28 = (bf16[4,48,1280]{2,1,0:T(8,128)(2,1)S(1)}, bf16[4,48,1280]{2,1,0:T(8,128)(2,1)S(1)}, u32[]{:S(2)}, u32[]{:S(2)}) collective-permute-start(bf16[4,48,1280]{2,1,0:T(8,128)(2,1)S(1)} %pad_maximum_fusion.6), channel_id=1, source_target_pairs={{0,2},{2,0},{4,6},{6,4},{8,10},{10,8},{12,14},{14,12},{16,18},{18,... | collective-permute-start | bytes 1474568 | tf_op jit(solution)/shard_map/ppermute | solution.py:48
  127.0 29.1 %copy-start.3 = (bf16[2,4,48,1408]{3,2,1,0:T(8,128)(2,1)}, bf16[2,4,48,1408]{3,2,1,0:T(8,128)(2,1)S(1)}, u32[]{:S(2)}) copy-start(bf16[2,4,48,1408]{3,2,1,0:T(8,128)(2,1)S(1)} %pad_maximum_fusion.rest_8_.rest_0_.rest_20_) | copy-start | bytes 3244036
  127.0 25.9 %collective-permute-start.30 = (bf16[2,4,48,1408]{3,2,1,0:T(8,128)(2,1)S(1)}, bf16[2,4,48,1408]{3,2,1,0:T(8,128)(2,1)}, u32[]{:S(2)}, u32[]{:S(2)}) collective-permute-start(bf16[2,4,48,1408]{3,2,1,0:T(8,128)(2,1)S(1)} %pad_maximum_fusion.rest_8_.rest_0_.rest_20_), channel_id=1, source_target_pairs={{0,2},{2,0},{4,6},{6,4},{8,10},{10,8},{12,14},{14,12},{16,18},{18,... | collective-permute-start | bytes 3244040 | tf_op jit(solution)/shard_map/ppermute | solution.py:48
  128.6 27.5 %copy-start.24 = (f32[2,2,768]{2,1,0:T(2,128)S(1)}, f32[2,2,768]{2,1,0:T(2,128)}, u32[]{:S(2)}) copy-start(f32[2,2,768]{2,1,0:T(2,128)} %param.28) | copy-start | bytes 36868
  128.6 31.3 %copy-start.4 = (bf16[2,4,48,1280]{3,2,1,0:T(8,128)(2,1)}, bf16[2,4,48,1280]{3,2,1,0:T(8,128)(2,1)S(1)}, u32[]{:S(2)}) copy-start(bf16[2,4,48,1280]{3,2,1,0:T(8,128)(2,1)S(1)} %pad_maximum_fusion.1.rest_12_.rest_4_.rest_24_) | copy-start | bytes 2949124
  128.7 24.8 %collective-permute-start.33 = (bf16[2,4,48,1280]{3,2,1,0:T(8,128)(2,1)S(1)}, bf16[2,4,48,1280]{3,2,1,0:T(8,128)(2,1)}, u32[]{:S(2)}, u32[]{:S(2)}) collective-permute-start(bf16[2,4,48,1280]{3,2,1,0:T(8,128)(2,1)S(1)} %pad_maximum_fusion.1.rest_12_.rest_4_.rest_24_), channel_id=1, source_target_pairs={{0,4},{2,6},{4,0},{6,2},{8,12},{10,14},{12,8},{14,10},{16,20},{18,... | collective-permute-start | bytes 2949128 | tf_op jit(solution)/shard_map/ppermute | solution.py:48
  129.3 23.6 %collective-permute-start.18 = (bf16[2,4,48,1024]{3,2,1,0:T(8,128)(2,1)S(1)}, bf16[2,4,48,1024]{3,2,1,0:T(8,128)(2,1)S(1)}, u32[]{:S(2)}, u32[]{:S(2)}) collective-permute-start(bf16[2,4,48,1024]{3,2,1,0:T(8,128)(2,1)S(1)} %pad_maximum_fusion.2.rest_0_.rest_28_), channel_id=1, source_target_pairs={{0,1},{1,0},{2,3},{3,2},{4,5},{5,4},{6,7},{7,6},{8,9},{9,8},{10,11... | collective-permute-start | bytes 2359304 | tf_op jit(solution)/shard_map/ppermute | solution.py:53
  129.3 5.2 %collective-permute-start.21 = (bf16[2,4,48,896]{3,2,1,0:T(8,128)(2,1)S(1)}, bf16[2,4,48,896]{3,2,1,0:T(8,128)(2,1)S(1)}, u32[]{:S(2)}, u32[]{:S(2)}) collective-permute-start(bf16[2,4,48,896]{3,2,1,0:T(8,128)(2,1)S(1)} %copy-done.7), channel_id=1, source_target_pairs={{0,1},{1,0},{2,3},{3,2},{4,5},{5,4},{6,7},{7,6},{8,9},{9,8},{10,11... | collective-permute-start | bytes 2064392 | tf_op jit(solution)/shard_map/ppermute | solution.py:53
  129.8 24.6 %collective-permute-start.23 = (bf16[2,4,48,896]{3,2,1,0:T(8,128)(2,1)}, bf16[2,4,48,896]{3,2,1,0:T(8,128)(2,1)S(1)}, u32[]{:S(2)}, u32[]{:S(2)}) collective-permute-start(bf16[2,4,48,896]{3,2,1,0:T(8,128)(2,1)} %collective-permute-done.22.rest_6_.rest_34_), channel_id=1, source_target_pairs={{0,1},{1,0},{2,3},{3,2},{4,5},{5,4},{6,7},{7,6},{8,9},{9,8},{10,11... | collective-permute-start | bytes 2064392 | tf_op jit(solution)/shard_map/ppermute | solution.py:53
  134.5 25.4 %collective-permute-start.29 = (bf16[2,4,48,1408]{3,2,1,0:T(8,128)(2,1)S(1)}, bf16[2,4,48,1408]{3,2,1,0:T(8,128)(2,1)}, u32[]{:S(2)}, u32[]{:S(2)}) collective-permute-start(bf16[2,4,48,1408]{3,2,1,0:T(8,128)(2,1)S(1)} %pad_maximum_fusion.rest_8_.rest_0_.rest_20_), channel_id=1, source_target_pairs={{0,1},{1,0},{2,3},{3,2},{4,5},{5,4},{6,7},{7,6},{8,9},{9,8},{10,11... | collective-permute-start | bytes 3244040 | tf_op jit(solution)/shard_map/ppermute | solution.py:53
  152.9 7.0 %collective-permute-start.31 = (bf16[2,4,48,1408]{3,2,1,0:T(8,128)(2,1)}, bf16[2,4,48,1408]{3,2,1,0:T(8,128)(2,1)}, u32[]{:S(2)}, u32[]{:S(2)}) collective-permute-start(bf16[2,4,48,1408]{3,2,1,0:T(8,128)(2,1)} %collective-permute-done.30.rest_10_.rest_2_.rest_22_), channel_id=1, source_target_pairs={{0,1},{1,0},{2,3},{3,2},{4,5},{5,4},{6,7},{7,6},{8,9},{9,8},{10,11... | collective-permute-start | bytes 3244040 | tf_op jit(solution)/shard_map/ppermute | solution.py:53
  152.9 7.0 %collective-permute-start.32 = (bf16[2,4,48,1280]{3,2,1,0:T(8,128)(2,1)S(1)}, bf16[2,4,48,1280]{3,2,1,0:T(8,128)(2,1)S(1)}, u32[]{:S(2)}, u32[]{:S(2)}) collective-permute-start(bf16[2,4,48,1280]{3,2,1,0:T(8,128)(2,1)S(1)} %pad_maximum_fusion.1.rest_12_.rest_4_.rest_24_), channel_id=1, source_target_pairs={{0,1},{1,0},{2,3},{3,2},{4,5},{5,4},{6,7},{7,6},{8,9},{9,8},{10,11... | collective-permute-start | bytes 2949128 | tf_op jit(solution)/shard_map/ppermute | solution.py:53
  153.8 6.1 %collective-permute-start.34 = (bf16[2,4,48,1280]{3,2,1,0:T(8,128)(2,1)}, bf16[2,4,48,1280]{3,2,1,0:T(8,128)(2,1)}, u32[]{:S(2)}, u32[]{:S(2)}) collective-permute-start(bf16[2,4,48,1280]{3,2,1,0:T(8,128)(2,1)} %collective-permute-done.33.rest_14_.rest_6_.rest_26_), channel_id=1, source_target_pairs={{0,1},{1,0},{2,3},{3,2},{4,5},{5,4},{6,7},{7,6},{8,9},{9,8},{10,11... | collective-permute-start | bytes 2949128 | tf_op jit(solution)/shard_map/ppermute | solution.py:53
  155.3 4.6 %collective-permute-start.20 = (bf16[2,4,48,1024]{3,2,1,0:T(8,128)(2,1)}, bf16[2,4,48,1024]{3,2,1,0:T(8,128)(2,1)}, u32[]{:S(2)}, u32[]{:S(2)}) collective-permute-start(bf16[2,4,48,1024]{3,2,1,0:T(8,128)(2,1)} %collective-permute-done.19.rest_2_.rest_30_), channel_id=1, source_target_pairs={{0,1},{1,0},{2,3},{3,2},{4,5},{5,4},{6,7},{7,6},{8,9},{9,8},{10,11... | collective-permute-start | bytes 2359304 | tf_op jit(solution)/shard_map/ppermute | solution.py:53
  248.0 1.3 collective-permute-start.35
  250.2 4.9 %collective-permute-start.36 = (f32[64,384]{1,0:T(8,128)S(1)}, f32[64,384]{1,0:T(8,128)S(1)}, u32[]{:S(2)}, u32[]{:S(2)}) collective-permute-start(f32[64,384]{1,0:T(8,128)S(1)} %dynamic-slice_add_fusion), channel_id=1, source_target_pairs={{0,2},{2,0},{4,6},{6,4},{8,10},{10,8},{12,14},{14,12},{16,18},{18,... | collective-permute-start | bytes 294920 | tf_op jit(solution)/shard_map/ppermute | solution.py:48
  255.2 4.7 %collective-permute-start.37 = (f32[64,384]{1,0:T(8,128)S(1)}, f32[64,384]{1,0:T(8,128)S(1)}, u32[]{:S(2)}, u32[]{:S(2)}) collective-permute-start(f32[64,384]{1,0:T(8,128)S(1)} %add.63), channel_id=1, source_target_pairs={{0,4},{2,6},{4,0},{6,2},{8,12},{10,14},{12,8},{14,10},{16,20},{18,... | collective-permute-start | bytes 294920 | tf_op jit(solution)/shard_map/ppermute | solution.py:48
  259.9 11.7 %collective-permute-start.40 = (f32[64,384]{1,0:T(8,128)S(1)}, f32[64,384]{1,0:T(8,128)S(1)}, u32[]{:S(2)}, u32[]{:S(2)}) collective-permute-start(f32[64,384]{1,0:T(8,128)S(1)} %add.64), channel_id=1, source_target_pairs={{0,24},{2,26},{4,28},{6,30},{8,0},{10,2},{12,4},{14,6},{16,8},{18,... | collective-permute-start | bytes 294920 | tf_op jit(solution)/shard_map/ppermute | solution.py:48
  259.9 11.7 %collective-permute-start.39 = (f32[64,384]{1,0:T(8,128)S(1)}, f32[64,384]{1,0:T(8,128)S(1)}, u32[]{:S(2)}, u32[]{:S(2)}) collective-permute-start(f32[64,384]{1,0:T(8,128)S(1)} %add.64), channel_id=1, source_target_pairs={{0,16},{2,18},{4,20},{6,22},{8,24},{10,26},{12,28},{14,30},{16,0},... | collective-permute-start | bytes 294920 | tf_op jit(solution)/shard_map/ppermute | solution.py:48
  262.6 9.0 %collective-permute-start.38 = (f32[64,384]{1,0:T(8,128)S(1)}, f32[64,384]{1,0:T(8,128)S(1)}, u32[]{:S(2)}, u32[]{:S(2)}) collective-permute-start(f32[64,384]{1,0:T(8,128)S(1)} %add.64), channel_id=1, source_target_pairs={{0,8},{2,10},{4,12},{6,14},{8,16},{10,18},{12,20},{14,22},{16,24},... | collective-permute-start | bytes 294920 | tf_op jit(solution)/shard_map/ppermute | solution.py:48
  271.6 1.3 collective-permute-start.41
  (24 other events, 170.7 us)
Sparse Core Ops, SparseCore 0:
  13.1 123.2 all-gather.1

commit v3 on v2

--- a/solution.py
+++ b/solution.py
@@ -1,4 +1,5 @@
 import functools
+import itertools
 
 import jax
 import jax.numpy as jnp
@@ -37,13 +38,16 @@
 
 
 def shift(values, grid, axis, by):
+    return move(values, grid, [by if i == axis else 0 for i in range(3)])
+
+
+def move(values, grid, by):
     nz, ny, nx = grid
     pairs = []
     for z in range(nz):
         for y in range(ny):
             for x in range(nx):
-                to = [z, y, x]
-                to[axis] = (to[axis] + by) % grid[axis]
+                to = [(at + step) % size for at, step, size in zip((z, y, x), by, grid)]
                 pairs.append(((z * ny + y) * nx + x, (to[0] * ny + to[1]) * nx + to[2]))
     return lax.ppermute(values, "dp", pairs)
 
@@ -82,23 +86,22 @@
             at += len(leaves)
         return bound, refs[at:]
 
-    def start(self, bound, key, dst, sem):
+    def start(self, bound, key, dst, sems):
         name, items = self.places[key]
         if not isinstance(bound[name], list):
-            ref = bound[name]
-            for lane, width, row in items:
-                pltpu.make_async_copy(
-                    ref.at[:, pl.ds(lane, width)], dst.at[pl.ds(row, ref.shape[0]), :], sem
-                ).start()
+            run = dst.shape[1] // len(sems)
+            for i, sem in enumerate(sems):
+                lanes = pl.ds(i * run, run)
+                pltpu.make_async_copy(bound[name].at[:, lanes], dst.at[:, lanes], sem).start()
             return
-        all_items = items
         nz, ny, nx = self.grid
         dp = lax.axis_index("dp")
         core = lax.axis_index("head")
         z, y, x = dp // (ny * nx), (dp // nx) % ny, dp % nx
-        for at, half in enumerate(bound[name]):
-            items = [item for item in all_items if item[0] == at]
-            if not items:
+        runs = range(len(sems)) if len(sems) > 1 else (None,)
+        for wanted, (at, half) in itertools.product(runs, enumerate(bound[name])):
+            here = [item for item in items if item[0] == at and wanted in (None, item[4])]
+            if not here:
                 continue
             for last, pair in enumerate(half):
                 for other in range(2):
@@ -110,12 +113,12 @@
                             ky, kx = (first, last) if at == 0 else (last, first)
                             yy, xx = lax.rem(y + ny - ky, ny), lax.rem(x + nx - kx, nx)
                             owner = (zz * ny + yy) * nx + xx
-                            for _, lane, width, place in items:
+                            for _, lane, width, place, run in here:
                                 row, col = place(owner, c)
                                 pltpu.make_async_copy(
                                     ref.at[first, kz, :, pl.ds(lane, width)],
                                     dst.at[pl.ds(row, ref.shape[2]), pl.ds(col, width)],
-                                    sem,
+                                    sems[run if len(sems) > 1 else 0],
                                 ).start()
 
 
@@ -156,7 +159,7 @@
     return jax.ShapeDtypeStruct(shape, dtype)
 
 
-def kernel_call(body, outs, scratch, flops, scalars, blocks, raw, raw_outs=()):
+def kernel_call(body, outs, scratch, flops, scalars, blocks, raw, raw_outs=0):
     specs = [pl.BlockSpec(memory_space=pltpu.SMEM)] * len(scalars)
     specs += [pl.BlockSpec(memory_space=pltpu.VMEM)] * len(blocks)
     specs += [pl.BlockSpec(memory_space=pl.ANY)] * len(raw)
@@ -165,7 +168,9 @@
         body,
         out_shape=tuple(outs),
         in_specs=specs,
-        out_specs=tuple([pl.BlockSpec(memory_space=pltpu.VMEM)] * len(outs)),
+        out_specs=tuple(
+            pl.BlockSpec(memory_space=pl.ANY if i < raw_outs else pltpu.VMEM) for i in range(len(outs))
+        ),
         scratch_shapes=scratch,
         compiler_params=pltpu.CompilerParams(vmem_limit_bytes=VMEM_LIMIT),
         cost_estimate=pl.CostEstimate(flops=flops, bytes_accessed=moved, transcendentals=0),
@@ -188,61 +193,120 @@
     return low, jnp.zeros((rows, 128), BF)
 
 
-def attend_forward(x, down, up, weights, layer, lengths):
+def project(r, down, up_ref, w_ref, w_wait, mid_ref, outs, done):
+    width = w_ref.shape[0]
+    mid = mm(r, down).astype(BF)
+    mid_ref[...] = mid
+    for at in range(3):
+        w_wait(at)
+        for j in range(0, width, TILE):
+            c = at * width + j
+            total = mm(r, w_ref[:, c : c + TILE])
+            if at != 1:
+                total += mm(mid, up_ref(slice(c, c + TILE)))
+            outs[at][:, j : j + TILE] = total.astype(BF)
+        done(at)
+
+
+def attend(q_ref, k_ref, v_ref, o_ref, lse_ref, bias_ref):
+    rows, width = q_ref.shape
+    low, zero = head_masks(rows)
+    one_low = jnp.where(low, 1.0, 0.0).astype(BF)
+    one_high = jnp.where(low, 0.0, 1.0).astype(BF)
+    for p in range(width // 128):
+        lanes = slice(p * 128, p * 128 + 128)
+        q2 = q_ref[:, lanes] * 0.125
+        k2 = k_ref[:, lanes]
+        v2 = v_ref[:, lanes]
+        bias = bias_ref[...]
+        s0 = mm_rt(q2, jnp.where(low, k2, zero)) + bias
+        s1 = mm_rt(q2, jnp.where(low, zero, k2)) + bias
+        m0 = jnp.max(s0, -1, keepdims=True)
+        m1 = jnp.max(s1, -1, keepdims=True)
+        e0 = jnp.exp(s0 - m0).astype(BF)
+        e1 = jnp.exp(s1 - m1).astype(BF)
+        v0 = jnp.concatenate([jnp.where(low, v2, zero), one_low], 1)
+        v1 = jnp.concatenate([jnp.where(low, zero, v2), one_high], 1)
+        both = mm(e0, v0) + mm(e1, v1)
+        total = both[:, 128:]
+        o_ref[:, lanes] = (both[:, :128] / total).astype(BF)
+        flip = (jnp.where(low, m0, m1) + jnp.log(total)).T
+        lse_ref[2 * p] = flip[0:8]
+        lse_ref[2 * p + 1] = flip[64:72]
+
+
+def third(ref, at):
+    width = ref.shape[0]
+    return ref.at[:, pl.ds(at * width, width)]
+
+
+def project_forward(x, down, up, weights, layer):
     rows, width = x.shape
     keys = (("qkv", layer),)
-    pairs = width // 128
-
-    def body(len_ref, x_ref, down_ref, up_ref, *rest):
+
+    def body(x_in, down_in, up_in, *rest):
         bound, rest = weights.bind(keys, rest)
-        q_ref, k_ref, v_ref, o_ref, lse_ref, mid_ref, w_ref, bias_ref, sem = rest
-        weights.start(bound, keys[0], w_ref, sem)
-        r = x_ref[...].astype(BF)
-        mid = mm(r, down_ref[...]).astype(BF)
-        mid_ref[...] = mid
-        bias_ref[...] = mask_bias(len_ref, rows)
-        wait_all(w_ref, sem)
-        for at, out in enumerate((q_ref, k_ref, v_ref)):
-            for j in range(0, width, TILE):
-                c = at * width + j
-                total = mm(r, w_ref[:, c : c + TILE])
-                if at != 1:
-                    total += mm(mid, up_ref[:, c : c + TILE])
-                out[:, j : j + TILE] = total.astype(BF)
-        low, zero = head_masks(rows)
-        one_low = jnp.where(low, 1.0, 0.0).astype(BF)
-        one_high = jnp.where(low, 0.0, 1.0).astype(BF)
-        for p in range(pairs):
-            lanes = slice(p * 128, p * 128 + 128)
-            q2 = q_ref[:, lanes] * 0.125
-            k2 = k_ref[:, lanes]
-            v2 = v_ref[:, lanes]
-            bias = bias_ref[...]
-            s0 = mm_rt(q2, jnp.where(low, k2, zero)) + bias
-            s1 = mm_rt(q2, jnp.where(low, zero, k2)) + bias
-            m0 = jnp.max(s0, -1, keepdims=True)
-            m1 = jnp.max(s1, -1, keepdims=True)
-            e0 = jnp.exp(s0 - m0).astype(BF)
-            e1 = jnp.exp(s1 - m1).astype(BF)
-            v0 = jnp.concatenate([jnp.where(low, v2, zero), one_low], 1)
-            v1 = jnp.concatenate([jnp.where(low, zero, v2), one_high], 1)
-            both = mm(e0, v0) + mm(e1, v1)
-            total = both[:, 128:]
-            o_ref[:, lanes] = (both[:, :128] / total).astype(BF)
-            flip = (jnp.where(low, m0, m1) + jnp.log(total)).T
-            lse_ref[2 * p] = flip[0:8]
-            lse_ref[2 * p + 1] = flip[64:72]
+        far, mid_ref, near = rest[:3], rest[3], rest[4:7]
+        w_ref, x_ref, down_ref, up_ref, sem, sem_out = rest[7:]
+
+        def give(at, op="start"):
+            getattr(pltpu.make_async_copy(near[at], far[at], sem_out.at[at]), op)()
+
+        copy_in(x_in, x_ref, sem.at[3])
+        copy_in(down_in, down_ref, sem.at[4])
+        copy_in(up_in, up_ref, sem.at[5])
+        weights.start(bound, keys[0], w_ref, [sem.at[at] for at in range(3)])
+        for ref, at in ((x_ref, 3), (down_ref, 4), (up_ref, 5)):
+            wait_all(ref, sem.at[at])
+        project(
+            x_ref[...].astype(BF),
+            down_ref[...],
+            lambda columns: up_ref[:, columns],
+            w_ref,
+            lambda at: wait_all(third(w_ref, at), sem.at[at]),
+            mid_ref,
+            near,
+            give,
+        )
+        for at in range(3):
+            give(at, "wait")
 
     act = sds((rows, width), BF)
-    outs = (act, act, act, act, sds((2 * pairs, 8, rows), F32), sds((rows, 128), BF))
     return kernel_call(
         body,
-        outs,
-        [pltpu.VMEM((width, 3 * width), BF), pltpu.VMEM((rows, rows), F32), pltpu.SemaphoreType.DMA],
-        6 * rows * width * width + 16 * rows * rows * width,
+        (act, act, act, sds((rows, 128), BF)),
+        [pltpu.VMEM((rows, width), BF)] * 3
+        + [
+            pltpu.VMEM((width, 3 * width), BF),
+            pltpu.VMEM(x.shape, x.dtype),
+            pltpu.VMEM(down.shape, BF),
+            pltpu.VMEM(up.shape, BF),
+            pltpu.SemaphoreType.DMA((6,)),
+            pltpu.SemaphoreType.DMA((3,)),
+        ],
+        6 * rows * width * width,
+        (),
+        (),
+        [x, down, up] + weights.leaves(keys),
+        raw_outs=3,
+    )
+
+
+def attend_forward(q, k, v, lengths):
+    rows, width = q.shape
+
+    def body(len_ref, q_ref, k_ref, v_ref, o_ref, lse_ref, bias_ref):
+        bias_ref[...] = mask_bias(len_ref, rows)
+        attend(q_ref, k_ref, v_ref, o_ref, lse_ref, bias_ref)
+
+    return kernel_call(
+        body,
+        (sds((rows, width), BF), sds((width // HEAD_DIM, 8, rows), F32)),
+        [pltpu.VMEM((rows, rows), F32)],
+        16 * rows * rows * width,
         (lengths,),
-        (x, down, up),
-        weights.leaves(keys),
+        (q, k, v),
+        [],
     )
 
 
@@ -271,8 +335,8 @@
     y = n1 * gains[0:1] + gains[1:2]
     y_ref[...] = y
     yb_ref[...] = y.astype(BF)
-    wu_wait()
     for j in range(0, ff, TILE):
+        wu_wait(j)
         value, slope = gelu_pair(mm(yb_ref[...], wu_ref[:, j : j + TILE]))
         slope_ref[:, j : j + TILE] = slope.astype(BF)
         a_ref[:, j : j + TILE] = value.astype(BF)
@@ -288,7 +352,7 @@
         bound, rest = weights.bind(keys, rest)
         n1_ref, rs_ref, slope_ref, out_ref, n2_ref, wo_ref, wu_ref, wd_ref, yb_ref, y_ref, a_ref, sem = rest
         for i, dst in enumerate((wo_ref, wu_ref, wd_ref)):
-            weights.start(bound, keys[i], dst, sem.at[i])
+            weights.start(bound, keys[i], dst, [sem.at[i]])
         gains = rows_ref[...]
         rs1 = dense_up(
             lambda j: x_ref[:, j : j + TILE].astype(F32),
@@ -296,7 +360,7 @@
             wo_ref,
             lambda: wait_all(wo_ref, sem.at[0]),
             wu_ref,
-            lambda: wait_all(wu_ref, sem.at[1]),
+            lambda j: wait_all(wu_ref, sem.at[1]) if j == 0 else None,
             gains,
             n1_ref,
             y_ref,
@@ -359,33 +423,39 @@
         gv_ref[:, lanes] = gv.astype(BF)
 
 
-def backward(saved, cotangent, rows8, downs, ups, weights, lengths):
-    layers = len(saved)
+def last_and_back(stream, saved, cotangent, rows8, downs, ups, weights, lengths):
+    last = len(saved)
+    layers = last + 1
     rows, width = cotangent.shape
     ff = weights.ff
-    last = layers - 1
-    keys = tuple((name, at) for at in reversed(range(layers)) for name in ("out", "up", "down", "qkv"))
-    keys = keys[:-1]
-    names = ("q", "k", "v", "o", "lse", "mid")
-    early = ("n1", "rs", "slope", "n2", "r")
-    raw = [cotangent, saved[last]["x"]]
-    for at in reversed(range(layers)):
-        raw += [saved[at][name] for name in names + (early if at < last else ())]
-
-    def body(len_ref, rows_ref, down_ref, up_ref, *rest):
-        cot_in, x_in = rest[:2]
-        rest = rest[2:]
+    keys = tuple((name, at) for at in reversed(range(layers)) for name in ("qkv", "out", "up", "down"))
+    keys = tuple(key for key in keys if key != ("qkv", 0))
+    names = ("q", "k", "v", "o", "lse", "mid", "n1", "rs", "slope", "n2", "r")
+    raw = [cotangent, stream, downs, ups]
+    for at in reversed(range(last)):
+        raw += [saved[at][name] for name in names]
+
+    def body(len_ref, rows_ref, *rest):
+        cot_in, x_in, down_in, up_in = rest[:4]
+        rest = rest[4:]
         given = [None] * layers
-        for at in reversed(range(layers)):
-            here = names + (early if at < last else ())
-            given[at] = dict(zip(here, rest))
-            rest = rest[len(here) :]
+        for at in reversed(range(last)):
+            given[at] = dict(zip(names, rest))
+            rest = rest[len(names) :]
         bound, rest = weights.bind(keys, rest)
-        out_ref, sums_ref, ghid_ref, gq_ref, gk_ref, gv_ref, gm_ref = rest[:7]
-        (wd_ref, wu_ref, wo_ref, wq_ref, cot_ref, g_ref, a_ref, wide_ref, gb_ref, go_ref, bias_ref) = rest[7:18]
-        keep = dict(zip(names + early, rest[18:29]))
-        sem = rest[29]
-        sems = {n: sem.at[i] for i, n in enumerate(names + early + ("down", "up", "out", "qkv", "cot", "x"))}
+        far, (mine_ref, send_ref, gm_ref), rest = rest[:5], rest[5:8], rest[8:]
+        near, rest = rest[:5], rest[5:]
+        out_ref, ghid_ref, gq_ref, gk_ref, gv_ref = near
+        (sums_ref, wd_ref, wu_ref, wo_ref, wq_ref, cot_ref, g_ref, a_ref, wide_ref, gb_ref, go_ref, bias_ref) = rest[:12]
+        down_ref, up_ref = rest[12:14]
+        keep = dict(zip(names, rest[14:25]))
+        sem, sem_out = rest[25:]
+
+        def give(i, op="start"):
+            getattr(pltpu.make_async_copy(near[i], far[i], sem_out.at[i]), op)()
+
+        extra = ("down", "up", "out", "qkv", "cot", "x", "qkv1", "qkv2", "downs", "ups")
+        sems = {n: sem.at[i] for i, n in enumerate(names + extra)}
 
         def fetch(at, *which):
             for name in which:
@@ -395,28 +465,41 @@
             for name in which:
                 wait_all(keep[name], sems[name])
 
+        qkv_sem = [sems[name] for name in ("qkv", "qkv1", "qkv2")]
         copy_in(x_in, g_ref, sems["x"])
-        fetch(last, "o")
-        weights.start(bound, ("out", last), wo_ref, sems["out"])
-        weights.start(bound, ("up", last), wu_ref, sems["up"])
-        weights.start(bound, ("down", last), wd_ref, sems["down"])
+        copy_in(down_in, down_ref, sems["downs"])
+        copy_in(up_in, up_ref, sems["ups"])
+        weights.start(bound, ("qkv", last), wq_ref, qkv_sem)
+        weights.start(bound, ("out", last), wo_ref, [sems["out"]])
+        weights.start(bound, ("up", last), wu_ref, [sems["up"]])
+        weights.start(bound, ("down", last), wd_ref, [sems["down"]])
         copy_in(cot_in, cot_ref, sems["cot"])
-        fetch(last, "q", "k", "v", "lse", "mid")
-        weights.start(bound, ("qkv", last), wq_ref, sems["qkv"])
         bias_ref[...] = mask_bias(len_ref, rows)
         for at in reversed(range(layers)):
             gains = rows_ref[8 * at : 8 * at + 8]
             if at == last:
                 wait_all(g_ref, sems["x"])
-                take("o")
                 keep["r"][...] = g_ref[...].astype(BF)
+                wait_all(down_ref, sems["downs"])
+                wait_all(up_ref, sems["ups"])
+                project(
+                    keep["r"][...],
+                    down_ref[at],
+                    lambda columns: up_ref[last, :, columns],
+                    wq_ref,
+                    lambda i: wait_all(third(wq_ref, i), qkv_sem[i]),
+                    keep["mid"],
+                    [keep[name] for name in "qkv"],
+                    lambda i: None,
+                )
+                attend(*[keep[name] for name in ("q", "k", "v", "o", "lse")], bias_ref)
                 scale1 = dense_up(
                     lambda j: g_ref[:, j : j + TILE],
                     keep["o"],
                     wo_ref,
                     lambda: wait_all(wo_ref, sems["out"]),
                     wu_ref,
-                    lambda: wait_all(wu_ref, sems["up"]),
+                    lambda j: wait_all(wu_ref, sems["up"]) if j == 0 else None,
                     gains,
                     keep["n1"],
                     wide_ref,
@@ -430,6 +513,7 @@
                     wide_ref[:, j : j + TILE] += mm(a_ref[...], wd_ref[:, j : j + TILE])
                 n2, scale2 = normalize(wide_ref[...])
                 out_ref[...] = (n2 * gains[2:3] + gains[3:4]).astype(out_ref.dtype)
+                give(0)
                 wait_all(cot_ref, sems["cot"])
                 incoming = cot_ref[...].astype(F32)
             else:
@@ -451,33 +535,48 @@
             scale1 = keep["rs"][:, 0:1]
             ghid = norm_backward(wide_ref[...] * gains[0:1], keep["n1"][...].astype(F32), scale1)
             ghid_ref[...] = ghid
+            if at == 0:
+                give(1)
             gb_ref[...] = ghid.astype(BF)
             for j in range(0, width, TILE):
                 go_ref[:, j : j + TILE] = mm_rt(gb_ref[...], wo_ref[j : j + TILE, :]).astype(BF)
             if at > 0:
-                weights.start(bound, ("down", at - 1), wd_ref, sems["down"])
+                weights.start(bound, ("down", at - 1), wd_ref, [sems["down"]])
                 fetch(at - 1, "n2", "rs", "slope", "n1")
-                weights.start(bound, ("up", at - 1), wu_ref, sems["up"])
-                weights.start(bound, ("out", at - 1), wo_ref, sems["out"])
-            take("q", "k", "v", "lse", *(() if at == last else ("o",)))
+                weights.start(bound, ("up", at - 1), wu_ref, [sems["up"]])
+                weights.start(bound, ("out", at - 1), wo_ref, [sems["out"]])
+            if at < last:
+                take("q", "k", "v", "lse", "o")
             attend_backward(
                 keep["q"], keep["k"], keep["v"], keep["o"], go_ref, keep["lse"], bias_ref, gq_ref, gk_ref, gv_ref
             )
             if at > 0:
                 fetch(at - 1, "q", "k", "v", "o", "lse")
+            else:
+                for i in (2, 3, 4):
+                    give(i)
             up = up_ref.at[at]
             gm = mm_rt(gq_ref[...], up[:, :width]) + mm_rt(gv_ref[...], up[:, 2 * width :])
             gm = gm.astype(BF)
-            take("mid", *(() if at == last else ("r",)))
+            if at < last:
+                take("mid", "r")
             base = 32 * at
             sums_ref[base : base + 16] = mm_lt(gm, keep["r"][...])[0:16]
             sums_ref[base + 16 : base + 24] = 2.0 * mm_lt(keep["mid"][...], gq_ref[...])[0:8]
             sums_ref[base + 24 : base + 32] = 2.0 * mm_lt(keep["mid"][...], gv_ref[...])[8:16]
             if at == 0:
                 gm_ref[...] = gm
+                half = width // 2
+                first = lax.axis_index("head") == 0
+                left, right = sums_ref[:, :half], sums_ref[:, half:]
+                mine_ref[...] = jnp.where(first, left, right)
+                send_ref[...] = jnp.where(first, right, left).astype(BF)
+                for i in range(5):
+                    give(i, "wait")
                 continue
             fetch(at - 1, "mid", "r")
-            wait_all(wq_ref, sems["qkv"])
+            if at < last:
+                wait_all(wq_ref, sems["qkv"])
             for j in range(0, width, TILE):
                 rs = slice(j, j + TILE)
                 total = ghid_ref[:, rs] + mm_rt(gm, down_ref[at, rs, :])
@@ -486,11 +585,14 @@
                 total += mm_rt(gv_ref[...], wq_ref[rs, 2 * width :])
                 g_ref[:, rs] = total
             if at > 1:
-                weights.start(bound, ("qkv", at - 1), wq_ref, sems["qkv"])
+                weights.start(bound, ("qkv", at - 1), wq_ref, [sems["qkv"]])
 
     act = sds((rows, width), BF)
-    outs = (act, sds((32 * layers, width), F32), sds((rows, width), F32), act, act, act, sds((rows, 128), BF))
-    scratch = [
+    sums = (32 * layers, width // 2)
+    outs = (act, sds((rows, width), F32), act, act, act, sds(sums, F32), sds(sums, BF), sds((rows, 128), BF))
+    scratch = [pltpu.VMEM(out.shape, out.dtype) for out in outs[:5]]
+    scratch += [
+        pltpu.VMEM((32 * layers, width), F32),
         pltpu.VMEM((ff, width), BF),
         pltpu.VMEM((width, ff), BF),
         pltpu.VMEM((width, width), BF),
@@ -502,30 +604,40 @@
         pltpu.VMEM((rows, width), BF),
         pltpu.VMEM((rows, width), BF),
         pltpu.VMEM((rows, rows), F32),
+        pltpu.VMEM(downs.shape, BF),
+        pltpu.VMEM(ups.shape, BF),
     ]
-    like = {**saved[last], **saved[0]}
-    scratch += [pltpu.VMEM(like[name].shape, like[name].dtype) for name in names + early]
-    scratch += [pltpu.SemaphoreType.DMA((len(names) + len(early) + 6,))]
+    scratch += [pltpu.VMEM(saved[0][name].shape, saved[0][name].dtype) for name in names]
+    scratch += [pltpu.SemaphoreType.DMA((len(names) + 10,)), pltpu.SemaphoreType.DMA((5,))]
     return kernel_call(
         body,
         outs,
         scratch,
         layers * (6 * rows * width * (2 * width + ff) + 40 * rows * rows * width),
         (lengths,),
-        (rows8, downs, ups),
+        (rows8,),
         raw + weights.leaves(keys),
+        raw_outs=5,
     )
 
 
 def input_grad(ghid, gq, gk, gv, gm, down, weights):
     rows, width = ghid.shape
     keys = (("qkv", 0),)
-
-    def body(ghid_ref, gq_ref, gk_ref, gv_ref, gm_ref, down_ref, *rest):
+    given = (gq, gk, gv, gm, down, ghid)
+
+    def body(*rest):
+        far, rest = rest[: len(given)], rest[len(given) :]
         bound, rest = weights.bind(keys, rest)
-        out_ref, w_ref, sem = rest
-        weights.start(bound, keys[0], w_ref, sem)
-        wait_all(w_ref, sem)
+        out_ref, w_ref, sem = rest[0], rest[1], rest[-1]
+        near = rest[2:-1]
+        gq_ref, gk_ref, gv_ref, gm_ref, down_ref, ghid_ref = near
+        weights.start(bound, keys[0], w_ref, [sem.at[0]])
+        for i, ref in enumerate(near):
+            copy_in(far[i], ref, sem.at[1 + i])
+        for i, ref in enumerate(near):
+            wait_all(ref, sem.at[1 + i])
+        wait_all(w_ref, sem.at[0])
         for j in range(0, width, TILE):
             rs = slice(j, j + TILE)
             total = ghid_ref[:, rs] + mm_rt(gm_ref[...], down_ref[rs, :])
@@ -537,11 +649,13 @@
     return kernel_call(
         body,
         (sds((rows, width), F32),),
-        [pltpu.VMEM((width, 3 * width), BF), pltpu.SemaphoreType.DMA],
+        [pltpu.VMEM((width, 3 * width), BF)]
+        + [pltpu.VMEM(v.shape, v.dtype) for v in given]
+        + [pltpu.SemaphoreType.DMA((1 + len(given),))],
         6 * rows * width * width,
         (),
-        (ghid, gq, gk, gv, gm, down),
-        weights.leaves(keys),
+        (),
+        list(given) + weights.leaves(keys),
     )[0]
 
 
@@ -559,7 +673,7 @@
         for name, w in (("out", w_out), ("up", w_up), ("down", w_down)):
             groups[name, at] = lax.all_gather(w[at].astype(BF), ("dp", "head"), axis=0, tiled=True)
         for name in ("qkv", "out", "up", "down"):
-            places[name, at] = ((name, at), [(0, groups[name, at].shape[1], 0)])
+            places[name, at] = ((name, at), ())
     return Gathered(grid, groups, places)
 
 
@@ -606,36 +720,37 @@
         return [[(own, swap_cores(own)) for own in half] for half in self.halves]
 
 
-def gather_and_run(chunks, weights, tokens, attention, dense):
+def gather_and_run(chunks, weights, tokens, small, projection, attention, dense):
     def arrive(index, *gates):
         weights.groups[index] = c[index].swap(*gates)
 
     c = chunks
-    z0 = c[0].spread_z()
-    c[1].spread_z()
-    first0 = c[0].spread_first()
-    c[2].spread_z(*z0, c[1].packed)
-    second0 = c[0].spread_second()
-    first1 = c[1].spread_first(*second0)
+    c[0].spread_z()
+    line1 = c[1].spread_z()
+    first0 = c[0].spread_first(c[1].packed)
+    line2 = c[2].spread_z(*first0, c[1].packed)
+    c[0].spread_second()
     arrive(0)
-    o = attention(0, tokens)
-    second1 = c[1].spread_second()
-    first2 = c[2].spread_first(*first1, o)
-    c[2].spread_second(*second1)
+    first1 = c[1].spread_first()
+    q = projection(0, after(tokens, *line1, *small))
+    c[1].spread_second(q)
+    o = attention(0, line2[0])
+    c[2].spread_first(*first1, o)
     arrive(1)
+    stream = dense(0, tokens, o)
+    c[2].spread_second(stream)
     arrive(2)
-    attention(1, dense(0, tokens, o))
-
-
-def sum_over_devices(sums, grid):
-    half = sums.shape[1] // 2
-    core = lax.axis_index("head")
-    mine = lax.dynamic_slice_in_dim(sums, core * half, half, 1)
-    other = lax.dynamic_slice_in_dim(sums, (1 - core) * half, half, 1)
-    total = mine + swap_cores(other)
-    for axis in (2, 1, 0):
-        parts = [total] + [shift(total, grid, axis, k) for k in range(1, grid[axis])]
-        total = functools.reduce(jnp.add, parts)
+    return stream
+
+
+def sum_over_devices(mine, send, grid):
+    total = mine + swap_cores(send).astype(F32)
+    nz, ny, nx = grid
+    plane = [(0, ky, kx) for ky in range(ny) for kx in range(nx)]
+    for steps in (plane[1:], [(k, 0, 0) for k in range(1, nz)]):
+        rounded = total.astype(BF)
+        parts = [move(rounded, grid, step).astype(F32) for step in steps]
+        total = functools.reduce(jnp.add, parts, rounded.astype(F32))
     return total
 
 
@@ -644,56 +759,43 @@
     layers, rows, half = w_query.shape
     width, ff = 2 * half, w_up.shape[2]
     core = lax.axis_index("head")
-    both = jnp.concatenate([w_out[0], w_up[0]], 1).astype(BF)
+    both = jnp.concatenate([w_out, w_up], 2).astype(BF)
 
     def columns(which):
         return jnp.concatenate(
             [
-                lax.dynamic_slice_in_dim(both, which * half, half, 1),
-                lax.dynamic_slice_in_dim(both, width + which * (ff // 2), ff // 2, 1),
+                lax.dynamic_slice_in_dim(both, which * half, half, 2),
+                lax.dynamic_slice_in_dim(both, width + which * (ff // 2), ff // 2, 2),
             ],
-            1,
+            2,
         )
 
     mine, come = columns(core), swap_cores(columns(1 - core))
-    both = jnp.concatenate([jnp.where(core == 0, mine, come), jnp.where(core == 0, come, mine)], 0)
+    both = jnp.concatenate([jnp.where(core == 0, mine, come), jnp.where(core == 0, come, mine)], 1)
     parts = w_down.shape[1] // rows
-    made = {("qkv", at): [w[at].astype(BF) for w in (w_query, w_key, w_value)] for at in range(layers)}
-    made["out", 0] = [both[:, :half]]
-    made["up", 0] = [both[:, half:]]
-    made["down", 0] = [w_down[0, i * rows : (i + 1) * rows].astype(BF) for i in range(parts)]
-    chunks = [[("qkv", 0)], [("out", 0), ("up", 0)], [("down", 0), ("qkv", 1)]]
+    made = {}
+    for at in range(layers):
+        made["qkv", at] = [w[at].astype(BF) for w in (w_query, w_key, w_value)]
+        made["out", at] = [both[at, :, :half]]
+        made["up", at] = [both[at, :, half:]]
+        made["down", at] = [w_down[at, i * rows : (i + 1) * rows].astype(BF) for i in range(parts)]
+    dense = ("out", "up", "down")
+    chunks = [[("qkv", 0)], [(name, 0) for name in dense], [(name, 1) for name in ("qkv", *dense)]]
     packs, places = [], {}
     for index, keys in enumerate(chunks):
         lanes = sum(block.shape[1] for key in keys for block in made[key])
         cut, at = cut_of(lanes), 0
         for key in keys:
             items = []
-            for wide, placer in tensor_items(key[0], rows, width, ff, parts):
+            for run, (wide, placer) in enumerate(tensor_items(key[0], rows, width, ff, parts)):
                 for half_at, low, high in ((0, 0, cut), (1, cut, lanes)):
                     start, stop = max(at, low), min(at + wide, high)
                     if start < stop:
-                        items.append((half_at, start - low, stop - start, placer(start - at)))
+                        items.append((half_at, start - low, stop - start, placer(start - at), run))
                 at += wide
             places[key] = (index, items)
         packs.append(jnp.concatenate([block for key in keys for block in made[key]], 1))
     return packs, places
-
-
-def gather_dense(w_out, w_up, w_down):
-    rows, ff = w_up.shape
-    width = w_out.shape[1]
-    parts = w_down.shape[0] // rows
-    up = w_up.astype(BF).reshape(rows, ff // (parts * rows), parts, rows).swapaxes(1, 2).reshape(rows, ff)
-    blocks = [w_down[i * rows : (i + 1) * rows].astype(BF) for i in range(parts)]
-    packed = jnp.concatenate([w_out.astype(BF), up, *blocks], 1)
-    whole = lax.all_gather(packed, ("dp", "head"), axis=0, tiled=True)
-    places = {
-        "out": [(0, width, 0)],
-        "up": [(width, ff, 0)],
-        "down": [(width + ff + i * width, width, i * width) for i in range(parts)],
-    }
-    return whole, places
 
 
 def body(
@@ -737,17 +839,20 @@
         weights = whole_weights(grid, tensors)
         weights.ff = w_up.shape[2]
     else:
-        whole, whole_places = gather_dense(w_out[1], w_up[1], w_down[1])
         packs, places = pack_chunks(tensors)
-        for name, lanes in whole_places.items():
-            places[name, 1] = ("dense", lanes)
         chunks = [Chunk(packed, grid) for packed in packs]
-        weights = Gathered(grid, {"dense": whole}, places)
+        weights = Gathered(grid, {}, places)
         weights.ff = w_up.shape[2]
 
-    def attention(at, stream):
-        q, k, v, o, lse, mid = attend_forward(stream, downs[at], ups[at], weights, at, seq_len)
-        saved.append({"q": q, "k": k, "v": v, "o": o, "lse": lse, "mid": mid, "x": stream})
+    def projection(at, stream):
+        got = project_forward(stream, downs[at], ups[at], weights, at)
+        saved.append(dict(zip(("q", "k", "v", "mid"), got)))
+        return got[0]
+
+    def attention(at, *gates):
+        q, k, v = (saved[at][name] for name in "qkv")
+        o, lse = attend_forward(after(q, *gates) if gates else q, k, v, seq_len)
+        saved[at].update(o=o, lse=lse)
         return o
 
     def dense(at, stream, attended):
@@ -758,17 +863,16 @@
 
     if not pieces:
         stream = tokens
-        for at in range(layers):
-            attended = attention(at, stream)
-            if at < layers - 1:
-                stream = dense(at, stream, attended)
+        for at in range(layers - 1):
+            projection(at, stream)
+            stream = dense(at, stream, attention(at))
     else:
-        gather_and_run(chunks, weights, tokens, attention, dense)
-    output, sums, ghid, gq, gk, gv, gm = backward(
-        saved, cotangent, rows8.reshape(8 * layers, width), downs, ups, weights, seq_len
+        stream = gather_and_run(chunks, weights, tokens, (downs, ups, rows8), projection, attention, dense)
+    output, ghid, gq, gk, gv, mine, send, gm = last_and_back(
+        stream, saved, cotangent, rows8.reshape(8 * layers, width), downs, ups, weights, seq_len
     )
     grad = input_grad(ghid, gq, gk, gv, gm, downs[0], weights)
-    total = sum_over_devices(sums, grid).reshape(layers, 4, rank, half)
+    total = sum_over_devices(mine, send, grid).reshape(layers, 4, rank, half)
     lower = total[:, :2].reshape(layers * 2 * rank, half)
     far = swap_cores(lower)
     lower = jnp.concatenate([jnp.where(core == 0, lower, far), jnp.where(core == 0, far, lower)], 1)

time: 286 us -> 269 us (0.941)
  between operations: 15.2 us -> 1.52 us
  other arithmetic: 4.92 us -> 12.5 us
  Pallas kernels: 108 us -> 102 us
    pallas_call x5, Pallas kernels: 108 us -> 102 us  [kernel_call(): pl.pallas_call(body, out_shape=tuple(outs), in_specs=specs, out_specs=tup...]
    another operation x6, other arithmetic: 0.44 us -> 4.06 us  [spread_second(): lines = [jnp.stack(flat[:split]), jnp.stack(flat[split:])]]
    unnamed x67 -> x58, local copies, waits for them, and re-layouts: 5.64 us -> 7.77 us
    ppermute x26 -> x27, starting transfers between devices: 37.4 us -> 35.9 us  [move(): return lax.ppermute(values, 'dp', pairs)]
    ppermute x26 -> x27, waiting for transfers between devices: 86.4 us -> 87.8 us  [move(): return lax.ppermute(values, 'dp', pairs)]
  transfers between devices with their start and end apart: 43 -> 43, of which waited for: 13 -> 19; matrix products, arithmetic and copies ran while one was open for 4% -> 6% of each run, Pallas kernels for 18% -> 14%
where the time goes in v3:
time: 269 us; the launch traced here: 265 us
  Pallas kernels  102 us (38%)
  waiting for transfers between devices  95.1 us (35%)
  starting transfers between devices  38.3 us (14%)
  local copies, waits for them, and re-layouts  15.4 us (6%)
  other arithmetic  12.5 us (5%)
    pallas_call x5, Pallas kernels, kernel_call(): pl.pallas_call(body, out_shape=tuple(outs), in_specs=specs, out_specs=tup...  102 us
    ppermute x27, waiting for transfers between devices, move(): return lax.ppermute(values, 'dp', pairs)  87.8 us
    ppermute x27, starting transfers between devices, move(): return lax.ppermute(values, 'dp', pairs)  35.9 us
    unnamed x58, local copies, waits for them, and re-layouts  7.77 us
    ppermute x16, waiting for transfers between devices, swap_cores(): lax.ppermute(values, 'head', [(i, (i + 1) % size) for i in range(size)])  7.3 us
  transfers between devices with their start and end apart: 43, of which 19 were waited for; matrix products, arithmetic and copies ran while one was open for 6% of the time, Pallas kernels for 14%

profile of v3, /device:TPU:0, one launch (start us, length us, event | category | flops | bytes accessed | tf_op | source)
XLA Modules:
  0.0 264.9 jit_solution(7767438226615699683)
XLA Ops:
  0.6 1.0 convert.45
  1.6 0.9 convert.46
  2.6 0.9 convert.47
  3.6 5.1 %collective-permute-start.7 = (bf16[48,1152]{1,0:T(8,128)(2,1)S(1)}, bf16[48,1152]{1,0:T(8,128)(2,1)S(1)}, u32[]{:S(2)}, u32[]{:S(2)}) collective-permute-start(bf16[48,1152]{1,0:T(8,128)(2,1)S(1)} %pad_maximum_fusion.16), channel_id=1, source_target_pairs={{0,24},{2,26},{4,28},{6,30},{8,0},{10,2},{12,4},{14,6},{16,8},{18,... | collective-permute-start | bytes 331784 | tf_op jit(solution)/shard_map/ppermute | solution.py:52
  8.7 1.0 collective-permute-start.5
  10.5 0.9 convert.38
  15.9 0.8 pad.17.rest_2_
  17.1 1.3 collective-permute-done.6
  18.4 1.9 collective-permute-start.3
  20.3 0.9 collective-permute-start.2
  21.2 1.7 collective-permute-start.1
  23.0 1.6 collective-permute-start.9
  24.6 1.6 collective-permute-start.8
  28.7 2.1 collective-permute-done.8
  30.9 1.6 collective-permute-start.14
  33.1 17.1 %collective-permute-done.2 = bf16[48,3456]{1,0:T(8,128)(2,1)S(1)} collective-permute-done((bf16[48,3456]{1,0:T(8,128)(2,1)S(1)}, bf16[48,3456]{1,0:T(8,128)(2,1)S(1)}, u32[]{:S(2)}, u32[]{:S(2)}) %collective-permute-start.2) | collective-permute-done | bytes 331808 | tf_op jit(solution)/shard_map/ppermute | solution.py:52
  50.7 1.6 collective-permute-start.18
  52.2 1.5 collective-permute-start.17
  54.3 0.9 slice_bitcast_fusion.up_in
  55.5 4.0 %collective-permute-start.26 = (bf16[48,4608]{1,0:T(8,128)(2,1)}, bf16[48,4608]{1,0:T(8,128)(2,1)S(1)}, u32[]{:S(2)}, u32[]{:S(2)}) collective-permute-start(bf16[48,4608]{1,0:T(8,128)(2,1)} %fusion.10), channel_id=1, source_target_pairs={{0,24},{2,26},{4,28},{6,30},{8,0},{10,2},{12,4},{14,6},{16,8},{18,... | collective-permute-start | bytes 1327112 | tf_op jit(solution)/shard_map/ppermute | solution.py:52
  60.2 6.8 %shard_map.190 = (bf16[512,768]{1,0:T(8,128)(2,1)}, bf16[512,768]{1,0:T(8,128)(2,1)}, bf16[512,768]{1,0:T(8,128)(2,1)}, bf16[512,128]{1,0:T(8,128)(2,1)}) custom-call(bf16[512,768]{1,0:T(8,128)(2,1)} %rest_14_.1, bf16[768,128]{1,0:T(8,128)(2,1)} %slice_bitcast_fusion.9.down_in.rest_4_, bf16[128,2304]{1,0:T(8,128)(2,1)} %slice_bitcast_fusion.up_in, ...), custom_call_target="tpu_custom_call" | custom-call | flops 1811939328 | bytes 7602176 | tf_op jit(solution)/shard_map/pallas_call | solution.py:167
  67.6 2.2 collective-permute-done.17
  69.8 2.3 pad_maximum_fusion.3.rest_4_.rest_27_
  72.1 1.5 collective-permute-start.23
  74.3 9.6 %shard_map.191 = (bf16[512,768]{1,0:T(8,128)(2,1)}, f32[12,8,512]{2,1,0:T(8,128)}) custom-call(s32[2]{0:T(128)} %len_ref.3, bf16[512,768]{1,0:T(8,128)(2,1)} %get-tuple-element.63.q_ref.rest_4_, bf16[512,768]{1,0:T(8,128)(2,1)} %get-tuple-element.64.k_ref.rest_5_, bf16[512,768]{1,0:T(8,128)(2,1)} %get-tuple-element.65.v_ref.rest_6_), custom_call_target="tpu_custom_call" | custom-call | flops 3221225472 | bytes 3342336 | tf_op jit(solution)/shard_map/pallas_call | solution.py:167
  84.4 8.9 %collective-permute-done.25 = bf16[48,4608]{1,0:T(8,128)(2,1)S(1)} collective-permute-done((bf16[48,4608]{1,0:T(8,128)(2,1)}, bf16[48,4608]{1,0:T(8,128)(2,1)S(1)}, u32[]{:S(2)}, u32[]{:S(2)}) %collective-permute-start.25) | collective-permute-done | bytes 442400 | tf_op jit(solution)/shard_map/ppermute | solution.py:52
  93.3 1.1 slice_bitcast_fusion.4
  94.4 1.1 slice_bitcast_fusion.3
  95.5 6.3 %collective-permute-done.23.rest_6_.rest_29_ = bf16[2,4,48,1664]{3,2,1,0:T(8,128)(2,1)} collective-permute-done((bf16[2,4,48,1664]{3,2,1,0:T(8,128)(2,1)}, bf16[2,4,48,1664]{3,2,1,0:T(8,128)(2,1)}, u32[]{:S(2)}, u32[]{:S(2)}) %collective-permute-start.23) | collective-permute-done | bytes 1277984 | tf_op jit(solution)/shard_map/ppermute | solution.py:52
  101.8 4.7 %collective-permute-done.20.rest_2_.rest_25_ = bf16[2,4,48,1792]{3,2,1,0:T(8,128)(2,1)} collective-permute-done((bf16[2,4,48,1792]{3,2,1,0:T(8,128)(2,1)S(1)}, bf16[2,4,48,1792]{3,2,1,0:T(8,128)(2,1)}, u32[]{:S(2)}, u32[]{:S(2)}) %collective-permute-start.20) | collective-permute-done | bytes 1376288 | tf_op jit(solution)/shard_map/ppermute | solution.py:52
  108.6 1.2 copy-done.25
  109.7 1.1 copy-done.26
  110.8 15.0 %shard_map.192 = (bf16[512,768]{1,0:T(8,128)(2,1)}, f32[512,128]{1,0:T(8,128)}, bf16[512,3072]{1,0:T(8,128)(2,1)}, f32[512,768]{1,0:T(8,128)}, bf16[512,768]{1,0:T(8,128)(2,1)}) custom-call(bf16[512,768]{1,0:T(8,128)(2,1)} %rest_14_.1, bf16[512,768]{1,0:T(8,128)(2,1)} %get-tuple-element.66.o_ref.rest_7_, f32[8,768]{1,0:T(8,128)} %slice_bitcast_fusion.40.rows_ref, ...), custom_call_target="tpu_custom_call" | custom-call | flops 5435817984 | bytes 18767872 | tf_op jit(solution)/shard_map/pallas_call | solution.py:167
  125.9 2.9 %collective-permute-done.27 = bf16[4,48,2304]{2,1,0:T(8,128)(2,1)S(1)} collective-permute-done((bf16[4,48,2304]{2,1,0:T(8,128)(2,1)S(1)}, bf16[4,48,2304]{2,1,0:T(8,128)(2,1)S(1)}, u32[]{:S(2)}, u32[]{:S(2)}) %collective-permute-start.27) | collective-permute-done | bytes 884768 | tf_op jit(solution)/shard_map/ppermute | solution.py:52
  129.7 1.4 pad_maximum_fusion.1.rest_19_
  131.1 1.2 collective-permute-start.33
  133.6 37.9 %collective-permute-done.33.rest_21_ = bf16[2,4,48,2304]{3,2,1,0:T(8,128)(2,1)S(1)} collective-permute-done((bf16[2,4,48,2304]{3,2,1,0:T(8,128)(2,1)S(1)}, bf16[2,4,48,2304]{3,2,1,0:T(8,128)(2,1)S(1)}, u32[]{:S(2)}, u32[]{:S(2)}) %collective-permute-start.33) | collective-permute-done | bytes 1769504 | tf_op jit(solution)/shard_map/ppermute | solution.py:52
  172.8 2.5 collective-permute-done.34.rest_22_
  175.2 2.5 collective-permute-done.31.rest_18_
  177.8 1.3 copy-done.24
  179.1 63.8 %shard_map.193 = (bf16[512,768]{1,0:T(8,128)(2,1)}, f32[512,768]{1,0:T(8,128)}, bf16[512,768]{1,0:T(8,128)(2,1)}, bf16[512,768]{1,0:T(8,128)(2,1)}, bf16[512,768...) custom-call(s32[2]{0:T(128)} %len_ref.3, ...), custom_call_target="tpu_custom_call" | custom-call | flops 37849399296 | bytes 42991616 | tf_op jit(solution)/shard_map/pallas_call | solution.py:167
  243.1 1.3 collective-permute-done.35
  244.4 0.9 add_convert_fusion.1
  246.1 1.3 collective-permute-start.37
  247.4 1.5 collective-permute-start.36
  248.9 1.9 collective-permute-done.38
  251.5 3.6 %collective-permute-start.41 = (bf16[64,384]{1,0:T(8,128)(2,1)S(1)}, bf16[64,384]{1,0:T(8,128)(2,1)S(1)}, u32[]{:S(2)}, u32[]{:S(2)}) collective-permute-start(bf16[64,384]{1,0:T(8,128)(2,1)S(1)} %add_convert_fusion), channel_id=1, source_target_pairs={{0,24},{2,26},{4,28},{6,30},{8,0},{10,2},{12,4},{14,6},{16,8},{18,... | collective-permute-start | bytes 147464 | tf_op jit(solution)/shard_map/ppermute | solution.py:52
  255.8 6.9 %shard_map.194 = f32[512,768]{1,0:T(8,128)} custom-call(bf16[512,768]{1,0:T(8,128)(2,1)} %get-tuple-element.91.rest_0_, bf16[512,768]{1,0:T(8,128)(2,1)} %get-tuple-element.92.rest_1_, bf16[512,768]{1,0:T(8,128)(2,1)} %get-tuple-element.93.rest_2_, bf16[512,128]{1,0:T(8,128)(2,1)} %get-tuple-element.94.rest_3_, ...), custom_call_target="tpu_custom_call" | custom-call | flops 1811939328 | bytes 9371648 | tf_op jit(solution)/shard_map/pallas_call | solution.py:167
  (174 shorter events, 22.4 us)
Async XLA Ops:
  0.6 10.8 %copy-start.8 = (f32[2,24,3072]{2,1,0:T(8,128)S(1)}, f32[2,24,3072]{2,1,0:T(8,128)}, u32[]{:S(2)}) copy-start(f32[2,24,3072]{2,1,0:T(8,128)} %param.21) | copy-start | bytes 1769476
  3.6 13.5 %collective-permute-start.7 = (bf16[48,1152]{1,0:T(8,128)(2,1)S(1)}, bf16[48,1152]{1,0:T(8,128)(2,1)S(1)}, u32[]{:S(2)}, u32[]{:S(2)}) collective-permute-start(bf16[48,1152]{1,0:T(8,128)(2,1)S(1)} %pad_maximum_fusion.16), channel_id=1, source_target_pairs={{0,24},{2,26},{4,28},{6,30},{8,0},{10,2},{12,4},{14,6},{16,8},{18,... | collective-permute-start | bytes 331784 | tf_op jit(solution)/shard_map/ppermute | solution.py:52
  8.7 9.7 %collective-permute-start.6 = (bf16[48,1152]{1,0:T(8,128)(2,1)S(1)}, bf16[48,1152]{1,0:T(8,128)(2,1)S(1)}, u32[]{:S(2)}, u32[]{:S(2)}) collective-permute-start(bf16[48,1152]{1,0:T(8,128)(2,1)S(1)} %pad_maximum_fusion.16), channel_id=1, source_target_pairs={{0,16},{2,18},{4,20},{6,22},{8,24},{10,26},{12,28},{14,30},{16,0},... | collective-permute-start | bytes 331784 | tf_op jit(solution)/shard_map/ppermute | solution.py:52
  8.7 9.7 %collective-permute-start.5 = (bf16[48,1152]{1,0:T(8,128)(2,1)S(1)}, bf16[48,1152]{1,0:T(8,128)(2,1)S(1)}, u32[]{:S(2)}, u32[]{:S(2)}) collective-permute-start(bf16[48,1152]{1,0:T(8,128)(2,1)S(1)} %pad_maximum_fusion.16), channel_id=1, source_target_pairs={{0,8},{2,10},{4,12},{6,14},{8,16},{10,18},{12,20},{14,22},{16,24},... | collective-permute-start | bytes 331784 | tf_op jit(solution)/shard_map/ppermute | solution.py:52
  10.5 6.3 %collective-permute-start.4 = (bf16[2,2,8,384]{3,2,0,1:T(8,128)(2,1)S(1)}, bf16[2,2,8,384]{3,2,0,1:T(8,128)(2,1)S(1)}, u32[]{:S(2)}, u32[]{:S(2)}) collective-permute-start(bf16[2,2,8,384]{3,2,0,1:T(8,128)(2,1)S(1)} %pad_maximum_fusion.20), channel_id=1, source_target_pairs={{0,1},{1,0},{2,3},{3,2},{4,5},{5,4},{6,7},{7,6},{8,9},{9,8},{10,11... | collective-permute-start | bytes 73736 | tf_op jit(solution)/shard_map/ppermute | solution.py:57
  11.8 5.2 %collective-permute-start = (bf16[2,24,1920]{2,1,0:T(8,128)(2,1)S(1)}, bf16[2,24,1920]{2,1,0:T(8,128)(2,1)S(1)}, u32[]{:S(2)}, u32[]{:S(2)}) collective-permute-start(bf16[2,24,1920]{2,1,0:T(8,128)(2,1)S(1)} %pad_maximum_fusion.14), channel_id=1, source_target_pairs={{0,1},{1,0},{2,3},{3,2},{4,5},{5,4},{6,7},{7,6},{8,9},{9,8},{10,11... | collective-permute-start | bytes 552968 | tf_op jit(solution)/shard_map/ppermute | solution.py:57
  16.9 37.4 %copy-start = (bf16[2,128,2304]{2,1,0:T(8,128)(2,1)}, bf16[2,128,2304]{2,1,0:T(8,128)(2,1)S(1)}, u32[]{:S(2)}) copy-start(bf16[2,128,2304]{2,1,0:T(8,128)(2,1)S(1)} %fusion.2.rest_3_) | copy-start | bytes 3538948
  18.4 14.1 %collective-permute-start.3 = (bf16[48,3456]{1,0:T(8,128)(2,1)S(1)}, bf16[48,3456]{1,0:T(8,128)(2,1)S(1)}, u32[]{:S(2)}, u32[]{:S(2)}) collective-permute-start(bf16[48,3456]{1,0:T(8,128)(2,1)S(1)} %pad_maximum_fusion.10), channel_id=1, source_target_pairs={{0,24},{2,26},{4,28},{6,30},{8,0},{10,2},{12,4},{14,6},{16,8},{18,... | collective-permute-start | bytes 995336 | tf_op jit(solution)/shard_map/ppermute | solution.py:52
  20.3 29.9 %collective-permute-start.2 = (bf16[48,3456]{1,0:T(8,128)(2,1)S(1)}, bf16[48,3456]{1,0:T(8,128)(2,1)S(1)}, u32[]{:S(2)}, u32[]{:S(2)}) collective-permute-start(bf16[48,3456]{1,0:T(8,128)(2,1)S(1)} %pad_maximum_fusion.10), channel_id=1, source_target_pairs={{0,16},{2,18},{4,20},{6,22},{8,24},{10,26},{12,28},{14,30},{16,0},... | collective-permute-start | bytes 995336 | tf_op jit(solution)/shard_map/ppermute | solution.py:52
  21.2 29.0 %collective-permute-start.1 = (bf16[48,3456]{1,0:T(8,128)(2,1)S(1)}, bf16[48,3456]{1,0:T(8,128)(2,1)S(1)}, u32[]{:S(2)}, u32[]{:S(2)}) collective-permute-start(bf16[48,3456]{1,0:T(8,128)(2,1)S(1)} %pad_maximum_fusion.10), channel_id=1, source_target_pairs={{0,8},{2,10},{4,12},{6,14},{8,16},{10,18},{12,20},{14,22},{16,24},... | collective-permute-start | bytes 995336 | tf_op jit(solution)/shard_map/ppermute | solution.py:52
  23.0 5.8 %collective-permute-start.9 = (bf16[4,48,512]{2,1,0:T(8,128)(2,1)S(1)}, bf16[4,48,512]{2,1,0:T(8,128)(2,1)S(1)}, u32[]{:S(2)}, u32[]{:S(2)}) collective-permute-start(bf16[4,48,512]{2,1,0:T(8,128)(2,1)S(1)} %pad_maximum_fusion.12), channel_id=1, source_target_pairs={{0,2},{2,0},{4,6},{6,4},{8,10},{10,8},{12,14},{14,12},{16,18},{18,... | collective-permute-start | bytes 589832 | tf_op jit(solution)/shard_map/ppermute | solution.py:52
  24.6 6.3 %collective-permute-start.8 = (bf16[4,48,640]{2,1,0:T(8,128)(2,1)S(1)}, bf16[4,48,640]{2,1,0:T(8,128)(2,1)S(1)}, u32[]{:S(2)}, u32[]{:S(2)}) collective-permute-start(bf16[4,48,640]{2,1,0:T(8,128)(2,1)S(1)} %pad_maximum_fusion.11), channel_id=1, source_target_pairs={{0,4},{2,6},{4,0},{6,2},{8,12},{10,14},{12,8},{14,10},{16,20},{18,... | collective-permute-start | bytes 737288 | tf_op jit(solution)/shard_map/ppermute | solution.py:52
  30.9 19.6 %copy-start.4 = (bf16[2,4,48,512]{3,2,1,0:T(8,128)(2,1)}, bf16[2,4,48,512]{3,2,1,0:T(8,128)(2,1)S(1)}, u32[]{:S(2)}) copy-start(bf16[2,4,48,512]{3,2,1,0:T(8,128)(2,1)S(1)} %pad_maximum_fusion.9.rest_4_.rest_10_) | copy-start | bytes 1179652
  30.9 19.8 %collective-permute-start.14 = (bf16[2,4,48,512]{3,2,1,0:T(8,128)(2,1)S(1)}, bf16[2,4,48,512]{3,2,1,0:T(8,128)(2,1)S(1)}, u32[]{:S(2)}, u32[]{:S(2)}) collective-permute-start(bf16[2,4,48,512]{3,2,1,0:T(8,128)(2,1)S(1)} %pad_maximum_fusion.9.rest_4_.rest_10_), channel_id=1, source_target_pairs={{0,4},{2,6},{4,0},{6,2},{8,12},{10,14},{12,8},{14,10},{16,20},{18,... | collective-permute-start | bytes 1179656 | tf_op jit(solution)/shard_map/ppermute | solution.py:52
  32.5 19.8 %collective-permute-start.13 = (bf16[2,4,48,512]{3,2,1,0:T(8,128)(2,1)S(1)}, bf16[2,4,48,512]{3,2,1,0:T(8,128)(2,1)}, u32[]{:S(2)}, u32[]{:S(2)}) collective-permute-start(bf16[2,4,48,512]{3,2,1,0:T(8,128)(2,1)S(1)} %pad_maximum_fusion.9.rest_4_.rest_10_), channel_id=1, source_target_pairs={{0,1},{1,0},{2,3},{3,2},{4,5},{5,4},{6,7},{7,6},{8,9},{9,8},{10,11... | collective-permute-start | bytes 1179656 | tf_op jit(solution)/shard_map/ppermute | solution.py:57
  32.5 18.0 %copy-start.1 = (bf16[2,4,48,640]{3,2,1,0:T(8,128)(2,1)}, bf16[2,4,48,640]{3,2,1,0:T(8,128)(2,1)S(1)}, u32[]{:S(2)}) copy-start(bf16[2,4,48,640]{3,2,1,0:T(8,128)(2,1)S(1)} %pad_maximum_fusion.8.rest_0_.rest_6_) | copy-start | bytes 1474564
  32.5 21.2 %collective-permute-start.11 = (bf16[2,4,48,640]{3,2,1,0:T(8,128)(2,1)S(1)}, bf16[2,4,48,640]{3,2,1,0:T(8,128)(2,1)S(1)}, u32[]{:S(2)}, u32[]{:S(2)}) collective-permute-start(bf16[2,4,48,640]{3,2,1,0:T(8,128)(2,1)S(1)} %pad_maximum_fusion.8.rest_0_.rest_6_), channel_id=1, source_target_pairs={{0,2},{2,0},{4,6},{6,4},{8,10},{10,8},{12,14},{14,12},{16,18},{18,... | collective-permute-start | bytes 1474568 | tf_op jit(solution)/shard_map/ppermute | solution.py:52
  50.2 3.5 %collective-permute-start.10 = (bf16[2,4,48,640]{3,2,1,0:T(8,128)(2,1)S(1)}, bf16[2,4,48,640]{3,2,1,0:T(8,128)(2,1)S(1)}, u32[]{:S(2)}, u32[]{:S(2)}) collective-permute-start(bf16[2,4,48,640]{3,2,1,0:T(8,128)(2,1)S(1)} %pad_maximum_fusion.8.rest_0_.rest_6_), channel_id=1, source_target_pairs={{0,1},{1,0},{2,3},{3,2},{4,5},{5,4},{6,7},{7,6},{8,9},{9,8},{10,11... | collective-permute-start | bytes 1474568 | tf_op jit(solution)/shard_map/ppermute | solution.py:57
  50.2 23.3 %collective-permute-start.16 = (bf16[48,4608]{1,0:T(8,128)(2,1)}, bf16[48,4608]{1,0:T(8,128)(2,1)}, u32[]{:S(2)}, u32[]{:S(2)}) collective-permute-start(bf16[48,4608]{1,0:T(8,128)(2,1)} %fusion.10), channel_id=1, source_target_pairs={{0,8},{2,10},{4,12},{6,14},{8,16},{10,18},{12,20},{14,22},{16,24},... | collective-permute-start | bytes 1327112 | tf_op jit(solution)/shard_map/ppermute | solution.py:52
  50.7 17.0 %collective-permute-start.18 = (bf16[4,48,1664]{2,1,0:T(8,128)(2,1)S(1)}, bf16[4,48,1664]{2,1,0:T(8,128)(2,1)}, u32[]{:S(2)}, u32[]{:S(2)}) collective-permute-start(bf16[4,48,1664]{2,1,0:T(8,128)(2,1)S(1)} %pad_maximum_fusion.7), channel_id=1, source_target_pairs={{0,2},{2,0},{4,6},{6,4},{8,10},{10,8},{12,14},{14,12},{16,18},{18,... | collective-permute-start | bytes 1916936 | tf_op jit(solution)/shard_map/ppermute | solution.py:52
  52.2 17.6 %collective-permute-start.17 = (bf16[4,48,1792]{2,1,0:T(8,128)(2,1)S(1)}, bf16[4,48,1792]{2,1,0:T(8,128)(2,1)S(1)}, u32[]{:S(2)}, u32[]{:S(2)}) collective-permute-start(bf16[4,48,1792]{2,1,0:T(8,128)(2,1)S(1)} %pad_maximum_fusion.6), channel_id=1, source_target_pairs={{0,4},{2,6},{4,0},{6,2},{8,12},{10,14},{12,8},{14,10},{16,20},{18,... | collective-permute-start | bytes 2064392 | tf_op jit(solution)/shard_map/ppermute | solution.py:52
  53.8 1.7 collective-permute-start.15
  53.8 5.7 %collective-permute-start.12 = (bf16[2,4,48,640]{3,2,1,0:T(8,128)(2,1)S(1)}, bf16[2,4,48,640]{3,2,1,0:T(8,128)(2,1)S(1)}, u32[]{:S(2)}, u32[]{:S(2)}) collective-permute-start(bf16[2,4,48,640]{3,2,1,0:T(8,128)(2,1)S(1)} %collective-permute-done.11.rest_2_.rest_8_), channel_id=1, source_target_pairs={{0,1},{1,0},{2,3},{3,2},{4,5},{5,4},{6,7},{7,6},{8,9},{9,8},{10,11... | collective-permute-start | bytes 1474568 | tf_op jit(solution)/shard_map/ppermute | solution.py:57
  55.5 28.4 %collective-permute-start.26 = (bf16[48,4608]{1,0:T(8,128)(2,1)}, bf16[48,4608]{1,0:T(8,128)(2,1)S(1)}, u32[]{:S(2)}, u32[]{:S(2)}) collective-permute-start(bf16[48,4608]{1,0:T(8,128)(2,1)} %fusion.10), channel_id=1, source_target_pairs={{0,24},{2,26},{4,28},{6,30},{8,0},{10,2},{12,4},{14,6},{16,8},{18,... | collective-permute-start | bytes 1327112 | tf_op jit(solution)/shard_map/ppermute | solution.py:52
  59.5 33.8 %collective-permute-start.25 = (bf16[48,4608]{1,0:T(8,128)(2,1)}, bf16[48,4608]{1,0:T(8,128)(2,1)S(1)}, u32[]{:S(2)}, u32[]{:S(2)}) collective-permute-start(bf16[48,4608]{1,0:T(8,128)(2,1)} %fusion.10), channel_id=1, source_target_pairs={{0,16},{2,18},{4,20},{6,22},{8,24},{10,26},{12,28},{14,30},{16,0},... | collective-permute-start | bytes 1327112 | tf_op jit(solution)/shard_map/ppermute | solution.py:52
  72.1 29.7 %collective-permute-start.23 = (bf16[2,4,48,1664]{3,2,1,0:T(8,128)(2,1)}, bf16[2,4,48,1664]{3,2,1,0:T(8,128)(2,1)}, u32[]{:S(2)}, u32[]{:S(2)}) collective-permute-start(bf16[2,4,48,1664]{3,2,1,0:T(8,128)(2,1)} %pad_maximum_fusion.3.rest_4_.rest_27_), channel_id=1, source_target_pairs={{0,4},{2,6},{4,0},{6,2},{8,12},{10,14},{12,8},{14,10},{16,20},{18,... | collective-permute-start | bytes 3833864 | tf_op jit(solution)/shard_map/ppermute | solution.py:52
  73.6 33.8 %collective-permute-start.22 = (bf16[2,4,48,1664]{3,2,1,0:T(8,128)(2,1)}, bf16[2,4,48,1664]{3,2,1,0:T(8,128)(2,1)}, u32[]{:S(2)}, u32[]{:S(2)}) collective-permute-start(bf16[2,4,48,1664]{3,2,1,0:T(8,128)(2,1)} %pad_maximum_fusion.3.rest_4_.rest_27_), channel_id=1, source_target_pairs={{0,1},{1,0},{2,3},{3,2},{4,5},{5,4},{6,7},{7,6},{8,9},{9,8},{10,11... | collective-permute-start | bytes 3833864 | tf_op jit(solution)/shard_map/ppermute | solution.py:57
  73.7 32.8 %collective-permute-start.20 = (bf16[2,4,48,1792]{3,2,1,0:T(8,128)(2,1)S(1)}, bf16[2,4,48,1792]{3,2,1,0:T(8,128)(2,1)}, u32[]{:S(2)}, u32[]{:S(2)}) collective-permute-start(bf16[2,4,48,1792]{3,2,1,0:T(8,128)(2,1)S(1)} %pad_maximum_fusion.2.rest_0_.rest_23_), channel_id=1, source_target_pairs={{0,2},{2,0},{4,6},{6,4},{8,10},{10,8},{12,14},{14,12},{16,18},{18,... | collective-permute-start | bytes 4128776 | tf_op jit(solution)/shard_map/ppermute | solution.py:52
  83.9 24.7 %collective-permute-start.19 = (bf16[2,4,48,1792]{3,2,1,0:T(8,128)(2,1)S(1)}, bf16[2,4,48,1792]{3,2,1,0:T(8,128)(2,1)S(1)}, u32[]{:S(2)}, u32[]{:S(2)}) collective-permute-start(bf16[2,4,48,1792]{3,2,1,0:T(8,128)(2,1)S(1)} %pad_maximum_fusion.2.rest_0_.rest_23_), channel_id=1, source_target_pairs={{0,1},{1,0},{2,3},{3,2},{4,5},{5,4},{6,7},{7,6},{8,9},{9,8},{10,11... | collective-permute-start | bytes 4128776 | tf_op jit(solution)/shard_map/ppermute | solution.py:57
  101.8 8.0 %collective-permute-start.24 = (bf16[2,4,48,1664]{3,2,1,0:T(8,128)(2,1)}, bf16[2,4,48,1664]{3,2,1,0:T(8,128)(2,1)S(1)}, u32[]{:S(2)}, u32[]{:S(2)}) collective-permute-start(bf16[2,4,48,1664]{3,2,1,0:T(8,128)(2,1)} %collective-permute-done.23.rest_6_.rest_29_), channel_id=1, source_target_pairs={{0,1},{1,0},{2,3},{3,2},{4,5},{5,4},{6,7},{7,6},{8,9},{9,8},{10,11... | collective-permute-start | bytes 3833864 | tf_op jit(solution)/shard_map/ppermute | solution.py:57
  106.5 4.3 %collective-permute-start.21 = (bf16[2,4,48,1792]{3,2,1,0:T(8,128)(2,1)}, bf16[2,4,48,1792]{3,2,1,0:T(8,128)(2,1)}, u32[]{:S(2)}, u32[]{:S(2)}) collective-permute-start(bf16[2,4,48,1792]{3,2,1,0:T(8,128)(2,1)} %collective-permute-done.20.rest_2_.rest_25_), channel_id=1, source_target_pairs={{0,1},{1,0},{2,3},{3,2},{4,5},{5,4},{6,7},{7,6},{8,9},{9,8},{10,11... | collective-permute-start | bytes 4128776 | tf_op jit(solution)/shard_map/ppermute | solution.py:57
  106.6 22.1 %collective-permute-start.27 = (bf16[4,48,2304]{2,1,0:T(8,128)(2,1)S(1)}, bf16[4,48,2304]{2,1,0:T(8,128)(2,1)S(1)}, u32[]{:S(2)}, u32[]{:S(2)}) collective-permute-start(bf16[4,48,2304]{2,1,0:T(8,128)(2,1)S(1)} %pad_maximum_fusion.4), channel_id=1, source_target_pairs={{0,4},{2,6},{4,0},{6,2},{8,12},{10,14},{12,8},{14,10},{16,20},{18,... | collective-permute-start | bytes 2654216 | tf_op jit(solution)/shard_map/ppermute | solution.py:52
  107.3 21.9 %collective-permute-start.28 = (bf16[4,48,2304]{2,1,0:T(8,128)(2,1)S(1)}, bf16[4,48,2304]{2,1,0:T(8,128)(2,1)}, u32[]{:S(2)}, u32[]{:S(2)}) collective-permute-start(bf16[4,48,2304]{2,1,0:T(8,128)(2,1)S(1)} %pad_maximum_fusion.5), channel_id=1, source_target_pairs={{0,2},{2,0},{4,6},{6,4},{8,10},{10,8},{12,14},{14,12},{16,18},{18,... | collective-permute-start | bytes 2654216 | tf_op jit(solution)/shard_map/ppermute | solution.py:52
  131.1 40.4 %collective-permute-start.33 = (bf16[2,4,48,2304]{3,2,1,0:T(8,128)(2,1)S(1)}, bf16[2,4,48,2304]{3,2,1,0:T(8,128)(2,1)S(1)}, u32[]{:S(2)}, u32[]{:S(2)}) collective-permute-start(bf16[2,4,48,2304]{3,2,1,0:T(8,128)(2,1)S(1)} %pad_maximum_fusion.1.rest_19_), channel_id=1, source_target_pairs={{0,4},{2,6},{4,0},{6,2},{8,12},{10,14},{12,8},{14,10},{16,20},{18,... | collective-permute-start | bytes 5308424 | tf_op jit(solution)/shard_map/ppermute | solution.py:52
  132.5 39.7 %copy-start.3 = (bf16[2,4,48,2304]{3,2,1,0:T(8,128)(2,1)}, bf16[2,4,48,2304]{3,2,1,0:T(8,128)(2,1)S(1)}, u32[]{:S(2)}) copy-start(bf16[2,4,48,2304]{3,2,1,0:T(8,128)(2,1)S(1)} %pad_maximum_fusion.rest_15_) | copy-start | bytes 5308420
  132.5 39.7 %collective-permute-start.30 = (bf16[2,4,48,2304]{3,2,1,0:T(8,128)(2,1)S(1)}, bf16[2,4,48,2304]{3,2,1,0:T(8,128)(2,1)S(1)}, u32[]{:S(2)}, u32[]{:S(2)}) collective-permute-start(bf16[2,4,48,2304]{3,2,1,0:T(8,128)(2,1)S(1)} %pad_maximum_fusion.rest_15_), channel_id=1, source_target_pairs={{0,2},{2,0},{4,6},{6,4},{8,10},{10,8},{12,14},{14,12},{16,18},{18,... | collective-permute-start | bytes 5308424 | tf_op jit(solution)/shard_map/ppermute | solution.py:52
  133.1 39.1 %collective-permute-start.32 = (bf16[2,4,48,2304]{3,2,1,0:T(8,128)(2,1)S(1)}, bf16[2,4,48,2304]{3,2,1,0:T(8,128)(2,1)S(1)}, u32[]{:S(2)}, u32[]{:S(2)}) collective-permute-start(bf16[2,4,48,2304]{3,2,1,0:T(8,128)(2,1)S(1)} %pad_maximum_fusion.1.rest_19_), channel_id=1, source_target_pairs={{0,1},{1,0},{2,3},{3,2},{4,5},{5,4},{6,7},{7,6},{8,9},{9,8},{10,11... | collective-permute-start | bytes 5308424 | tf_op jit(solution)/shard_map/ppermute | solution.py:57
  133.1 39.1 %collective-permute-start.29 = (bf16[2,4,48,2304]{3,2,1,0:T(8,128)(2,1)S(1)}, bf16[2,4,48,2304]{3,2,1,0:T(8,128)(2,1)S(1)}, u32[]{:S(2)}, u32[]{:S(2)}) collective-permute-start(bf16[2,4,48,2304]{3,2,1,0:T(8,128)(2,1)S(1)} %pad_maximum_fusion.rest_15_), channel_id=1, source_target_pairs={{0,1},{1,0},{2,3},{3,2},{4,5},{5,4},{6,7},{7,6},{8,9},{9,8},{10,11... | collective-permute-start | bytes 5308424 | tf_op jit(solution)/shard_map/ppermute | solution.py:57
  171.6 3.7 %collective-permute-start.34 = (bf16[2,4,48,2304]{3,2,1,0:T(8,128)(2,1)S(1)}, bf16[2,4,48,2304]{3,2,1,0:T(8,128)(2,1)S(1)}, u32[]{:S(2)}, u32[]{:S(2)}) collective-permute-start(bf16[2,4,48,2304]{3,2,1,0:T(8,128)(2,1)S(1)} %collective-permute-done.33.rest_21_), channel_id=1, source_target_pairs={{0,1},{1,0},{2,3},{3,2},{4,5},{5,4},{6,7},{7,6},{8,9},{9,8},{10,11... | collective-permute-start | bytes 5308424 | tf_op jit(solution)/shard_map/ppermute | solution.py:57
  172.2 5.6 %collective-permute-start.31 = (bf16[2,4,48,2304]{3,2,1,0:T(8,128)(2,1)S(1)}, bf16[2,4,48,2304]{3,2,1,0:T(8,128)(2,1)S(1)}, u32[]{:S(2)}, u32[]{:S(2)}) collective-permute-start(bf16[2,4,48,2304]{3,2,1,0:T(8,128)(2,1)S(1)} %collective-permute-done.30.rest_17_), channel_id=1, source_target_pairs={{0,1},{1,0},{2,3},{3,2},{4,5},{5,4},{6,7},{7,6},{8,9},{9,8},{10,11... | collective-permute-start | bytes 5308424 | tf_op jit(solution)/shard_map/ppermute | solution.py:57
  242.9 1.5 collective-permute-start.35
  245.3 5.4 %collective-permute-start.38 = (bf16[64,384]{1,0:T(8,128)(2,1)S(1)}, bf16[64,384]{1,0:T(8,128)(2,1)S(1)}, u32[]{:S(2)}, u32[]{:S(2)}) collective-permute-start(bf16[64,384]{1,0:T(8,128)(2,1)S(1)} %add_convert_fusion.1), channel_id=1, source_target_pairs={{0,6},{2,4},{4,2},{6,0},{8,14},{10,12},{12,10},{14,8},{16,22},{18,... | collective-permute-start | bytes 147464 | tf_op jit(solution)/shard_map/ppermute | solution.py:52
  246.1 4.7 %collective-permute-start.37 = (bf16[64,384]{1,0:T(8,128)(2,1)S(1)}, bf16[64,384]{1,0:T(8,128)(2,1)S(1)}, u32[]{:S(2)}, u32[]{:S(2)}) collective-permute-start(bf16[64,384]{1,0:T(8,128)(2,1)S(1)} %add_convert_fusion.1), channel_id=1, source_target_pairs={{0,4},{2,6},{4,0},{6,2},{8,12},{10,14},{12,8},{14,10},{16,20},{18,... | collective-permute-start | bytes 147464 | tf_op jit(solution)/shard_map/ppermute | solution.py:52
  247.4 4.1 %collective-permute-start.36 = (bf16[64,384]{1,0:T(8,128)(2,1)S(1)}, bf16[64,384]{1,0:T(8,128)(2,1)S(1)}, u32[]{:S(2)}, u32[]{:S(2)}) collective-permute-start(bf16[64,384]{1,0:T(8,128)(2,1)S(1)} %add_convert_fusion.1), channel_id=1, source_target_pairs={{0,2},{2,0},{4,6},{6,4},{8,10},{10,8},{12,14},{14,12},{16,18},{18,... | collective-permute-start | bytes 147464 | tf_op jit(solution)/shard_map/ppermute | solution.py:52
  251.5 11.1 %collective-permute-start.41 = (bf16[64,384]{1,0:T(8,128)(2,1)S(1)}, bf16[64,384]{1,0:T(8,128)(2,1)S(1)}, u32[]{:S(2)}, u32[]{:S(2)}) collective-permute-start(bf16[64,384]{1,0:T(8,128)(2,1)S(1)} %add_convert_fusion), channel_id=1, source_target_pairs={{0,24},{2,26},{4,28},{6,30},{8,0},{10,2},{12,4},{14,6},{16,8},{18,... | collective-permute-start | bytes 147464 | tf_op jit(solution)/shard_map/ppermute | solution.py:52
  255.1 7.6 %collective-permute-start.40 = (bf16[64,384]{1,0:T(8,128)(2,1)S(1)}, bf16[64,384]{1,0:T(8,128)(2,1)S(1)}, u32[]{:S(2)}, u32[]{:S(2)}) collective-permute-start(bf16[64,384]{1,0:T(8,128)(2,1)S(1)} %add_convert_fusion), channel_id=1, source_target_pairs={{0,16},{2,18},{4,20},{6,22},{8,24},{10,26},{12,28},{14,30},{16,0},... | collective-permute-start | bytes 147464 | tf_op jit(solution)/shard_map/ppermute | solution.py:52
  255.1 7.6 %collective-permute-start.39 = (bf16[64,384]{1,0:T(8,128)(2,1)S(1)}, bf16[64,384]{1,0:T(8,128)(2,1)S(1)}, u32[]{:S(2)}, u32[]{:S(2)}) collective-permute-start(bf16[64,384]{1,0:T(8,128)(2,1)S(1)} %add_convert_fusion), channel_id=1, source_target_pairs={{0,8},{2,10},{4,12},{6,14},{8,16},{10,18},{12,20},{14,22},{16,24},... | collective-permute-start | bytes 147464 | tf_op jit(solution)/shard_map/ppermute | solution.py:52
  262.7 1.3 collective-permute-start.42
  (22 other events, 97.8 us)
